TPU v7x, 512 devices: a whole 4x8x8 slice. The times are simulated.
512 devices in a mesh: seq: 128 (over z, y, core), tp: 4 (over x).
Axes of the slice: x: 4, y: 8, z: 8, core: 2. Of those that a mesh axis runs over, the one named last changes fastest.
Arguments:
- queries: bfloat16 [32768, 4096], P('seq', 'tp'), may hold values from -6 to 6, as said below
- keys: bfloat16 [32768, 512], P('seq', 'tp'), may hold values from -6 to 6, as said below
- values: bfloat16 [32768, 512], P('seq', 'tp'), may hold values from -6 to 6
- segment: int32 [32768], P('seq'), may hold values from 0 to 255, never falling along the last dimension, each value on 1 to 512 neighbouring positions
- repack: int32 [32768], P('seq'), may hold values from 0 to 32767, as said below
- proj: bfloat16 [1536, 4096], P('seq', 'tp'), may hold values from -0.5 to 0.5
- student_states: bfloat16 [32768, 1536], P('seq'), may hold values from -6 to 6
- target_row: int32 [32768], P('seq'), may hold values from 0 to 255
Outputs:
- student_rows: bfloat16 [32768, 1536], P('seq', 'tp')
- grad: float32 [1536, 4096], P('seq', 'tp')
Inputs may be any that keep to these rules, and one draw needn't show every extreme that they name: `queries`: scaled normal entries. `keys`: scaled normal entries. `repack`: A permutation of the student rows. Each device's teacher rows go in consecutive groups of 4 rows, in order, each group to one student owner (the device holding student rows owner * 256 to owner * 256 + 255); every device sends exactly 4 rows to each of 64 other devices and none to itself, so at most 4 rows from one device to one owner, reached by every sending pair.
All inputs are finite; a program needn't handle non-finite values.
Results may differ from a plain program's by a relative error of at most 0.0056.
Values may be sent and summed in bfloat16 or wider, within the bound.
No kernel may reach another device: no remote copies, remote signals or barrier semaphores. Data moves between devices by JAX's collectives and lax.ppermute only.
A program may use at most 64 MiB of HBM per device.

v0:
```python
import math

import jax
import jax.numpy as jnp
from jax import lax
from jax.sharding import PartitionSpec as P

HEADS = 32
KV_HEADS = 4
HEAD_DIM = 128
SW = 1536
REACH = 2


neg_large = -1e30


def prefix(value, axis, combine, identity):
    size, here = (lax.axis_size(axis), lax.axis_index(axis))
    everything = jax.tree.map(lambda part: lax.all_gather(part, axis), value)
    start = jax.tree.map(
        lambda part, zero: jnp.broadcast_to(jnp.asarray(zero, part.dtype), part.shape),
        value,
        identity,
    )

    def hop(k, before):
        reached = k < here
        new = combine(before, jax.tree.map(lambda part: part[k], everything))
        return jax.tree.map(lambda a, b: jnp.where(reached, a, b), new, before)

    return lax.fori_loop(0, size, hop, start)


def passed_along(block, axis, distance):
    devices = range(lax.axis_size(axis))
    route = [(i - distance, i) for i in devices if i - distance in devices]
    return lax.ppermute(block, axis, route)


def anchor_combine(earlier, later):
    first_id = jnp.where(earlier[0] < 0, later[0], earlier[0])
    last_id = jnp.where(later[1] < 0, earlier[1], later[1])
    whole_later = (later[0] == later[1]) & (later[0] == earlier[1]) & (later[0] >= 0)
    start_pos = jnp.where(later[1] < 0, earlier[2], jnp.where(whole_later, earlier[2], later[2]))
    return (first_id, last_id, start_pos)


def document_starts(segment):
    row_count = segment.shape[0]
    row_pos = lax.axis_index("seq") * row_count + jnp.arange(row_count, dtype=jnp.int32)
    first_id = segment[0]
    last_id = segment[-1]
    last_start = jnp.min(jnp.where(segment == last_id, row_pos, jnp.int32(2**30)))
    sentinel = jnp.int32(-1)
    carried = prefix(
        (first_id, last_id, last_start), "seq", anchor_combine, (sentinel, sentinel, sentinel)
    )
    is_new = jnp.concatenate([jnp.ones((1,), bool), segment[1:] != segment[:-1]])
    local_start = lax.cummax(jnp.where(is_new, row_pos, jnp.int32(-1)), axis=0)
    inherit = (segment == carried[1]) & (segment == first_id)
    return (jnp.where(inherit, carried[2], local_start), row_pos)


def attend(queries, keys, values, row_start, row_pos):
    row_count = queries.shape[0]
    key_list = [keys]
    value_list = [values]
    pos_list = [row_pos]
    for step in range(1, REACH + 1):
        earlier = passed_along((keys, values), "seq", step)
        key_list.insert(0, earlier[0])
        value_list.insert(0, earlier[1])
        pos_list.insert(0, row_pos - step * row_count)
    all_keys = jnp.concatenate(key_list, axis=0)
    all_values = jnp.concatenate(value_list, axis=0)
    key_pos = jnp.concatenate(pos_list, axis=0)
    allowed = (key_pos[None, :] >= row_start[:, None]) & (key_pos[None, :] <= row_pos[:, None])
    kv_local = keys.shape[1] // HEAD_DIM
    group = HEADS // KV_HEADS
    part_size = 1
    q_heads = queries.reshape(row_count, kv_local, group, HEAD_DIM)
    scale = 1.0 / math.sqrt(HEAD_DIM)
    outputs = []
    for first in range(0, group, part_size):
        q_part = q_heads[:, 0, first : first + part_size, :]
        scores = (
            jnp.einsum("tjd,sd->jts", q_part, all_keys, preferred_element_type=jnp.float32) * scale
        )
        scores = jnp.where(allowed[None], scores, neg_large)
        top = jnp.max(scores, axis=-1, keepdims=True)
        expo = jnp.exp(scores - top)
        weights = (expo / jnp.sum(expo, axis=-1, keepdims=True)).astype(jnp.bfloat16)
        mixed = jnp.einsum("jts,sd->tjd", weights, all_values, preferred_element_type=jnp.float32)
        outputs.append(mixed.astype(jnp.bfloat16))
    return jnp.concatenate(outputs, axis=1).reshape(row_count, -1)


def project_rows(row_data, proj):
    return jnp.einsum(
        "tf,nf->tn",
        row_data,
        lax.all_gather(proj, "seq", axis=0, tiled=True),
        preferred_element_type=jnp.float32,
    )


def fill_buckets(data, target_dev, slot_rank, devices, capacity):
    empty = jnp.zeros((devices, capacity, data.shape[1]), data.dtype)
    return empty.at[target_dev, slot_rank].set(data)


def place_rows(received, slots, row_count):
    width = received.shape[-1]
    holder = jnp.zeros((row_count + 1, width), received.dtype)
    holder = holder.at[slots.reshape(-1)].set(received.reshape(-1, width))
    return holder[:row_count]


def on_device(queries, keys, values, segment, repack, proj, student_states, target_row):
    row_count = queries.shape[0]
    devices = lax.axis_size("seq")
    row_start, row_pos = document_starts(segment)
    attended = attend(queries, keys, values, row_start, row_pos)
    capacity = max(2 * row_count // devices, 2)
    target_dev = repack // row_count
    local_slot = repack - target_dev * row_count
    same_dev = target_dev[:, None] == target_dev[None, :]
    row_ids = jnp.arange(row_count, dtype=jnp.int32)
    before = row_ids[None, :] < row_ids[:, None]
    slot_rank = jnp.sum((same_dev & before).astype(jnp.int32), axis=1)
    slot_table = (
        jnp.full((devices, capacity), row_count, jnp.int32)
        .at[target_dev, slot_rank]
        .set(local_slot)
    )
    width_share = SW // lax.axis_size("tp")
    tp_index = lax.axis_index("tp")
    targets = student_states[target_row]
    buckets = fill_buckets(attended, target_dev, slot_rank, devices, capacity)
    arrived = (
        lax.all_to_all(buckets, "seq", split_axis=0, concat_axis=0, tiled=True),
        lax.all_to_all(slot_table, "seq", split_axis=0, concat_axis=0, tiled=True),
    )
    student_x = place_rows(arrived[0], arrived[1], row_count)
    y_part = project_rows(student_x, proj)
    y_total = lax.psum(y_part, "tp")
    y_rounded = y_total.astype(jnp.bfloat16)
    delta = (y_rounded.astype(jnp.float32) - targets.astype(jnp.float32)).astype(jnp.bfloat16)
    out_rows = lax.dynamic_slice_in_dim(y_rounded, tp_index * width_share, width_share, 1)
    norm_factor = 1.0 / math.sqrt(row_count * devices)
    grad_rows = delta.shape[1] // devices
    term = jnp.einsum("ts,tf->sf", delta, student_x, preferred_element_type=jnp.float32)
    pieces = term.reshape(devices, grad_rows, term.shape[1])
    summed = lax.all_to_all(
        pieces.astype(jnp.bfloat16), "seq", split_axis=0, concat_axis=0, tiled=True
    ).astype(pieces.dtype)
    grad = jnp.sum(summed, axis=0) * norm_factor
    return (out_rows, grad)


def solution(mesh):
    placed = (
        P("seq", "tp"),
        P("seq", "tp"),
        P("seq", "tp"),
        P("seq"),
        P("seq"),
        P("seq", "tp"),
        P("seq", None),
        P("seq"),
    )
    return jax.shard_map(
        on_device,
        mesh=mesh,
        in_specs=placed,
        out_specs=(P("seq", "tp"), P("seq", "tp")),
        check_vma=False,
    )
```

profile of v0, /device:TPU:41, one launch (start us, length us, event | category | flops | bytes accessed | tf_op | source)
XLA Modules:
  0.0 1132.1 jit_solution(2342865572813222749)
XLA Ops:
  7.2 2.4 collective-permute-start
  9.7 3.1 collective-permute-start.1
  12.8 3.2 collective-permute-start.2
  16.1 2.2 collective-permute-start.3
  18.3 0.7 multiply_subtract_fusion
  19.2 11.1 scatter_fusion
  30.3 0.7 copy.34
  31.0 15.8 %all-to-all-start = ((s32[128,1,4]{2,1,0:T(1,128)}), s32[128,1,4]{2,1,0:T(1,128)S(1)}, u32[]{:S(2)}, u32[]{:S(2)}) async-start(s32[128,1,4]{2,1,0:T(1,128)} %copy.34), calls=%async_computation | async-start | bytes 131072 | tf_op jit(solution)/shard_map/all_to_all | solution.py:143
  46.9 1.2 copy.35
  48.9 1.3 dynamic-slice
  50.1 1.2 fusion.59
  52.0 1.3 fusion.56
  53.3 1.3 dynamic-update-slice.2
  54.6 18.9 %all-reduce.3 = (s32[128]{0:T(128)S(1)}, s32[128]{0:T(128)S(1)}, s32[128]{0:T(128)S(1)}) all-reduce(s32[128]{0:T(128)S(1)} %get-tuple-element.149, s32[128]{0:T(128)S(1)} %slice_dynamic-update-slice_fusion, s32[128]{0:T(128)S(1)} %dynamic-update-slice.2), channel_id=1, replica_groups=mesh['seq'=128,'tp'=4] {'seq'}, use_global_device_ids=true, to_apply=%add | all-reduce | flops 384 | bytes 3072
  73.5 786.0 %while.15 = (s32[]{:T(128)}, s32[]{:T(128)}, s32[]{:T(128)}, s32[]{:T(128)}, s32[128]{0:T(128)S(1)}, /*index=5*/s32[128]{0:T(128)S(1)}, s32[128]{0:T(128)S(1)}, s32[]{:T(128)}, s32[]{:T(128)}) while((s32[]{:T(128)}, s32[]{:T(128)}, s32[]{:T(128)}, s32[]{:T(128)}, s32[128]{0:T(128)S(1)}, /*index=5*/s32[128]{0:T(128)S(1)}, s32[128]{0:T(128)S(1)}, ...), condition=%wide.region_4.5_spmd, body=%wide.region_3.4_spmd.sunk | while | flops 14 | bytes 261 | solution.py:32
  859.6 0.7 and_select_fusion
  866.9 1.2 broadcast_in_dim.35
  868.1 37.0 %scatter_fusion.1 = bf16[128,4,1024]{2,1,0:T(4,128)(2,1)} fusion(bf16[128,4,1024]{2,1,0:T(4,128)(2,1)} %broadcast_in_dim.35, s32[256]{0:T(256)S(1)} %bitcast.214, bf16[256,1024]{1,0:T(8,128)(2,1)S(1)} %copy.44), kind=kCustom, calls=%fused_computation.2 | custom fusion | bytes 1574912 | tf_op jit(solution)/shard_map/scatter | solution.py:110
  905.2 15.0 %all-to-all-start.1 = ((bf16[128,4,1024]{2,1,0:T(4,128)(2,1)}), bf16[128,4,1024]{2,1,0:T(4,128)(2,1)S(1)}, u32[]{:S(2)}, u32[]{:S(2)}) async-start(bf16[128,4,1024]{2,1,0:T(4,128)(2,1)} %scatter_fusion.1), calls=%async_computation.1 | async-start | bytes 2097152 | tf_op jit(solution)/shard_map/all_to_all | solution.py:142
  920.2 2.1 gather_fusion
  922.9 0.8 reduce.21
  923.8 25.2 %all-to-all-done.1 = bf16[128,4,1024]{2,1,0:T(4,128)(2,1)S(1)} async-done(((bf16[128,4,1024]{2,1,0:T(4,128)(2,1)}), bf16[128,4,1024]{2,1,0:T(4,128)(2,1)S(1)}, u32[]{:S(2)}, u32[]{:S(2)}) %all-to-all-start.1) | async-done | bytes 1048608 | tf_op jit(solution)/shard_map/all_to_all | solution.py:142
  949.3 2.8 scatter_custom_fusion.2
  952.1 6.2 reshape.408
  958.3 2.9 fusion.41
  961.2 34.8 %all-reduce.5 = bf16[256,1536]{1,0:T(8,128)(2,1)} all-reduce(f32[256,1536]{1,0:T(8,128)S(1)} %fusion.41), channel_id=1, replica_groups=mesh['seq'=128,'tp'=4] {'tp'}, use_global_device_ids=true, to_apply=%region_25.26 | all-reduce | flops 393216 | bytes 2359296 | tf_op jit(solution)/shard_map/psum | solution.py:147
  996.0 4.1 convolution_convert_fusion
  1000.1 6.1 convert_element_type.158
  1006.1 11.3 all-to-all-start.2
  1017.4 1.6 constant_dynamic-slice_fusion
  1019.1 102.5 %all-to-all-done.2 = bf16[128,12,1024]{2,1,0:T(8,128)(2,1)} async-done(((bf16[128,12,1024]{2,1,0:T(8,128)(2,1)}), bf16[128,12,1024]{2,1,0:T(8,128)(2,1)}, u32[]{:S(2)}, u32[]{:S(2)}) %all-to-all-start.2) | async-done | bytes 3145760 | tf_op jit(solution)/shard_map/all_to_all | solution.py:155
  1121.6 3.0 convert_reduce_fusion
  (457 shorter events, 242.0 us)
Async XLA Ops:
  7.2 913.1 %copy-start = (bf16[256,1536]{1,0:T(8,128)(2,1)S(1)}, bf16[256,1536]{1,0:T(8,128)(2,1)}, u32[]{:S(2)}) copy-start(bf16[256,1536]{1,0:T(8,128)(2,1)} %param.16) | copy-start | bytes 2359300
  7.2 853.1 %copy-start.1 = (bf16[256,128]{1,0:T(8,128)(2,1)S(1)}, bf16[256,128]{1,0:T(8,128)(2,1)}, u32[]{:S(2)}) copy-start(bf16[256,128]{1,0:T(8,128)(2,1)} %param.11) | copy-start | bytes 196612
  7.2 41.0 %copy-start.3 = (s32[256]{0:T(256)S(1)}, s32[256]{0:T(256)}, u32[]{:S(2)}) copy-start(s32[256]{0:T(256)} %param.13) | copy-start | bytes 3076
  7.2 944.9 %all-gather.3.cloned.1.call-start = ((), (), s32[]{:S(2)}) async-start(), calls=%async_computation.3 | async-start | bytes 4227072 | tf_op jit(solution)/shard_map/all_gather | solution.py:103
  7.2 854.4 %collective-permute-start = (bf16[256,128]{1,0:T(8,128)(2,1)}, bf16[256,128]{1,0:T(8,128)(2,1)S(1)}, u32[]{:S(2)}, u32[]{:S(2)}) collective-permute-start(bf16[256,128]{1,0:T(8,128)(2,1)} %param.12), channel_id=1, source_target_pairs={{0,8},{4,12},{8,16},{12,20},{16,24},{20,28},{24,32},{28,36},{32,40... | collective-permute-start | bytes 196616 | tf_op jit(solution)/shard_map/ppermute | solution.py:38
  9.7 852.0 %collective-permute-start.1 = (bf16[256,128]{1,0:T(8,128)(2,1)}, bf16[256,128]{1,0:T(8,128)(2,1)S(1)}, u32[]{:S(2)}, u32[]{:S(2)}) collective-permute-start(bf16[256,128]{1,0:T(8,128)(2,1)} %param.12), channel_id=1, source_target_pairs={{0,4},{4,8},{8,12},{12,16},{16,20},{20,24},{24,28},{28,32},{32,36}... | collective-permute-start | bytes 196616 | tf_op jit(solution)/shard_map/ppermute | solution.py:38
  12.8 847.4 %collective-permute-start.2 = (bf16[256,128]{1,0:T(8,128)(2,1)}, bf16[256,128]{1,0:T(8,128)(2,1)S(1)}, u32[]{:S(2)}, u32[]{:S(2)}) collective-permute-start(bf16[256,128]{1,0:T(8,128)(2,1)} %param.11), channel_id=1, source_target_pairs={{0,8},{4,12},{8,16},{12,20},{16,24},{20,28},{24,32},{28,36},{32,40... | collective-permute-start | bytes 196616 | tf_op jit(solution)/shard_map/ppermute | solution.py:38
  16.1 844.2 %collective-permute-start.3 = (bf16[256,128]{1,0:T(8,128)(2,1)}, bf16[256,128]{1,0:T(8,128)(2,1)S(1)}, u32[]{:S(2)}, u32[]{:S(2)}) collective-permute-start(bf16[256,128]{1,0:T(8,128)(2,1)} %param.11), channel_id=1, source_target_pairs={{0,4},{4,8},{8,12},{12,16},{16,20},{20,24},{24,28},{28,32},{32,36}... | collective-permute-start | bytes 196616 | tf_op jit(solution)/shard_map/ppermute | solution.py:38
  31.0 874.2 %all-to-all-start = ((s32[128,1,4]{2,1,0:T(1,128)}), s32[128,1,4]{2,1,0:T(1,128)S(1)}, u32[]{:S(2)}, u32[]{:S(2)}) async-start(s32[128,1,4]{2,1,0:T(1,128)} %copy.34), calls=%async_computation | async-start | bytes 131072 | tf_op jit(solution)/shard_map/all_to_all | solution.py:143
  860.3 1.4 copy-start.2
  868.1 52.0 %copy-start.4 = (s32[256]{0:T(256)S(1)}, s32[256]{0:T(256)}, u32[]{:S(2)}) copy-start(s32[256]{0:T(256)} %param.17) | copy-start | bytes 3076
  905.2 43.8 %all-to-all-start.1 = ((bf16[128,4,1024]{2,1,0:T(4,128)(2,1)}), bf16[128,4,1024]{2,1,0:T(4,128)(2,1)S(1)}, u32[]{:S(2)}, u32[]{:S(2)}) async-start(bf16[128,4,1024]{2,1,0:T(4,128)(2,1)} %scatter_fusion.1), calls=%async_computation.1 | async-start | bytes 2097152 | tf_op jit(solution)/shard_map/all_to_all | solution.py:142
  1006.1 115.5 %all-to-all-start.2 = ((bf16[128,12,1024]{2,1,0:T(8,128)(2,1)}), bf16[128,12,1024]{2,1,0:T(8,128)(2,1)}, u32[]{:S(2)}, u32[]{:S(2)}) async-start(bf16[128,12,1024]{2,1,0:T(8,128)(2,1)} %convert_element_type.158), calls=%async_computation.2 | async-start | bytes 8388608 | tf_op jit(solution)/shard_map/all_to_all | solution.py:155
Sparse Core Ops, SparseCore 0:
  18.4 86.5 all-gather.2
where the time goes:
time: 1140 us; the launch traced here: 1130 us
  loops' own time  554 us (49%)
  local copies, waits for them, and re-layouts  308 us (27%)
  waiting for transfers between devices  128 us (11%)
  blocking collectives  53.7 us (5%)
  starting transfers between devices  53.2 us (5%)
  between operations  14.4 us (1%)
  matrix products  11.8 us (1%)
    another operation x1, loops' own time, prefix(): return lax.fori_loop(0, size, hop, start)  554 us
    dynamic_slice x384, local copies, waits for them, and re-layouts, hop(): new = combine(before, jax.tree.map(lambda part: part[k], everything))  232 us
    all_to_all x1, waiting for transfers between devices, on_device(): lax.all_to_all(pieces.astype(jnp.bfloat16), 'seq', split_axis=0, concat_a...  103 us
    scatter x1, local copies, waits for them, and re-layouts, fill_buckets(): return empty.at[target_dev, slot_rank].set(data)  37 us
    psum x1, blocking collectives, on_device(): y_total = lax.psum(y_part, 'tp')  34.8 us
    all_to_all x1, waiting for transfers between devices, on_device(): lax.all_to_all(buckets, 'seq', split_axis=0, concat_axis=0, tiled=True)  25.2 us
  transfers between devices with their start and end apart: 8, of which 2 were waited for; matrix products, arithmetic and copies ran while one was open for 27% of the time, Pallas kernels for 0%

commit v1 on v0

v1 whole, which is shorter than its diff:
```python
import math

import jax
import jax.numpy as jnp
from jax import lax
from jax.sharding import PartitionSpec as P

HEADS = 32
KV_HEADS = 4
HEAD_DIM = 128
SW = 1536
REACH = 2
GROUP_ROWS = 4


neg_large = -1e30


def passed_along(block, axis, distance):
    devices = range(lax.axis_size(axis))
    route = [(i - distance, i) for i in devices if i - distance in devices]
    return lax.ppermute(block, axis, route)


def attend(queries, keys, values, segment):
    row_count = queries.shape[0]
    lanes = keys.shape[1]
    seg_rows = (segment + 1).astype(jnp.bfloat16).reshape(-1, lanes)
    seg_rows = jnp.concatenate([seg_rows, jnp.zeros((14, lanes), jnp.bfloat16)], 0)
    packed = jnp.concatenate([keys, values, seg_rows], 0)
    blocks = [packed]
    for step in range(1, REACH + 1):
        blocks.insert(0, passed_along(packed, "seq", step))
    all_keys = jnp.concatenate([b[:row_count] for b in blocks], 0)
    all_values = jnp.concatenate([b[row_count : 2 * row_count] for b in blocks], 0)
    key_seg = jnp.concatenate(
        [b[2 * row_count : 2 * row_count + 2].reshape(-1) for b in blocks], 0
    ).astype(jnp.int32)
    key_pos = jnp.arange(3 * row_count, dtype=jnp.int32) - REACH * row_count
    row_pos = jnp.arange(row_count, dtype=jnp.int32)
    allowed = (key_seg[None, :] == (segment + 1)[:, None]) & (key_pos[None, :] <= row_pos[:, None])
    group = HEADS // KV_HEADS
    q_heads = queries.reshape(row_count, group, HEAD_DIM)
    scale = 1.0 / math.sqrt(HEAD_DIM)
    outputs = []
    for head in range(group):
        scores = (
            jnp.einsum("td,sd->ts", q_heads[:, head], all_keys, preferred_element_type=jnp.float32)
            * scale
        )
        scores = jnp.where(allowed, scores, neg_large)
        top = jnp.max(scores, axis=-1, keepdims=True)
        expo = jnp.exp(scores - top)
        weights = (expo / jnp.sum(expo, axis=-1, keepdims=True)).astype(jnp.bfloat16)
        mixed = jnp.einsum("ts,sd->td", weights, all_values, preferred_element_type=jnp.float32)
        outputs.append(mixed.astype(jnp.bfloat16))
    return jnp.concatenate(outputs, axis=1)


def on_device(queries, keys, values, segment, repack, proj, student_states, target_row):
    row_count = queries.shape[0]
    devices = lax.axis_size("seq")
    groups = row_count // GROUP_ROWS
    attended = attend(queries, keys, values, segment)
    target_dev = repack // row_count
    local_slot = repack - target_dev * row_count
    owners = target_dev.reshape(groups, GROUP_ROWS)[:, 0]
    owner_hot = owners[None, :] == jnp.arange(devices, dtype=jnp.int32)[:, None]
    slots_by_group = local_slot.reshape(groups, GROUP_ROWS)
    slot_table = jnp.sum(
        jnp.where(owner_hot[:, :, None], slots_by_group[None], 0), axis=1
    )
    slot_table = jnp.where(jnp.any(owner_hot, axis=1)[:, None], slot_table, row_count)
    slots = lax.all_to_all(slot_table, "seq", split_axis=0, concat_axis=0, tiled=True)
    width_share = SW // lax.axis_size("tp")
    tp_index = lax.axis_index("tp")
    targets = student_states[target_row]
    bucket_dev = jnp.arange(devices * GROUP_ROWS, dtype=jnp.int32) // GROUP_ROWS
    bucket_pos = jnp.arange(devices * GROUP_ROWS, dtype=jnp.int32) % GROUP_ROWS
    row_ids = jnp.arange(row_count, dtype=jnp.int32)
    pick = (
        (bucket_dev[:, None] == target_dev[None, :])
        & (bucket_pos[:, None] == (row_ids % GROUP_ROWS)[None, :])
    ).astype(jnp.bfloat16)
    buckets = jnp.dot(pick, attended, preferred_element_type=jnp.float32).astype(jnp.bfloat16)
    arrived = lax.all_to_all(buckets, "seq", split_axis=0, concat_axis=0, tiled=True)
    place = (row_ids[:, None] == slots.reshape(-1)[None, :]).astype(jnp.bfloat16)
    student_x = jnp.dot(place, arrived, preferred_element_type=jnp.float32).astype(jnp.bfloat16)
    all_proj = lax.all_gather(proj, "seq", axis=0, tiled=True)
    y_part = jnp.einsum("tf,nf->tn", student_x, all_proj, preferred_element_type=jnp.float32)
    y_total = lax.psum(y_part, "tp")
    y_rounded = y_total.astype(jnp.bfloat16)
    delta = (y_rounded.astype(jnp.float32) - targets.astype(jnp.float32)).astype(jnp.bfloat16)
    out_rows = lax.dynamic_slice_in_dim(y_rounded, tp_index * width_share, width_share, 1)
    norm_factor = 1.0 / math.sqrt(row_count * devices)
    grad_rows = delta.shape[1] // devices
    term = jnp.einsum("ts,tf->sf", delta, student_x, preferred_element_type=jnp.float32)
    pieces = term.reshape(devices, grad_rows, term.shape[1])
    summed = lax.all_to_all(
        pieces.astype(jnp.bfloat16), "seq", split_axis=0, concat_axis=0, tiled=True
    ).astype(pieces.dtype)
    grad = jnp.sum(summed, axis=0) * norm_factor
    return (out_rows, grad)


def solution(mesh):
    placed = (
        P("seq", "tp"),
        P("seq", "tp"),
        P("seq", "tp"),
        P("seq"),
        P("seq"),
        P("seq", "tp"),
        P("seq", None),
        P("seq"),
    )
    return jax.shard_map(
        on_device,
        mesh=mesh,
        in_specs=placed,
        out_specs=(P("seq", "tp"), P("seq", "tp")),
        check_vma=False,
    )
```

time: 1140 us -> 318 us (0.28)
  loops' own time: 554 us -> 0 us
  local copies, waits for them, and re-layouts: 308 us -> 19.7 us
  waiting for transfers between devices: 128 us -> 176 us
  blocking collectives: 53.7 us -> 33.8 us
    another operation x1 -> x0, loops' own time: 554 us -> none  [prefix(): return lax.fori_loop(0, size, hop, start)]
    dynamic_slice x384 -> x0, local copies, waits for them, and re-layouts: 232 us -> none  [hop(): new = combine(before, jax.tree.map(lambda part: part[k], everything))]
    scatter x3 -> x0, local copies, waits for them, and re-layouts: 50.9 us -> none  [the longest x1 37 us: fill_buckets(): return empty.at[target_dev, slot_rank].set(data)]
    all_gather x1, waiting for transfers between devices: 0.02 us -> 46 us  [on_device(): all_proj = lax.all_gather(proj, 'seq', axis=0, tiled=True)]
    unnamed x1 -> x0, blocking collectives: 18.9 us -> none
  transfers between devices with their start and end apart: 8 -> 6, of which waited for: 2 -> 3; matrix products, arithmetic and copies ran while one was open for 27% -> 5% of each run, Pallas kernels for 0% -> 0%
where the time goes in v1:
time: 318 us; the launch traced here: 317 us
  waiting for transfers between devices  176 us (55%)
  starting transfers between devices  49.4 us (16%)
  blocking collectives  33.8 us (11%)
  local copies, waits for them, and re-layouts  19.7 us (6%)
  matrix products  14.9 us (5%)
  between operations  14.4 us (5%)
  other arithmetic  8.56 us (3%)
    all_to_all x1, waiting for transfers between devices, on_device(): lax.all_to_all(pieces.astype(jnp.bfloat16), 'seq', split_axis=0, concat_a...  103 us
    all_gather x1, waiting for transfers between devices, on_device(): all_proj = lax.all_gather(proj, 'seq', axis=0, tiled=True)  46 us
    psum x1, blocking collectives, on_device(): y_total = lax.psum(y_part, 'tp')  33.8 us
    all_to_all x1, waiting for transfers between devices, on_device(): lax.all_to_all(buckets, 'seq', split_axis=0, concat_axis=0, tiled=True)  26.4 us
    all_to_all x1, starting transfers between devices, on_device(): lax.all_to_all(slot_table, 'seq', split_axis=0, concat_axis=0, tiled=True)  16.6 us
    all_to_all x1, starting transfers between devices, on_device(): lax.all_to_all(pieces.astype(jnp.bfloat16), 'seq', split_axis=0, concat_a...  13.8 us
    all_to_all x1, starting transfers between devices, on_device(): lax.all_to_all(buckets, 'seq', split_axis=0, concat_axis=0, tiled=True)  13.7 us
    unnamed x10, local copies, waits for them, and re-layouts  7.43 us
  transfers between devices with their start and end apart: 6, of which 3 were waited for; matrix products, arithmetic and copies ran while one was open for 5% of the time, Pallas kernels for 0%

profile of v1, /device:TPU:41, one launch (start us, length us, event | category | flops | bytes accessed | tf_op | source)
XLA Modules:
  0.0 316.8 jit_solution(7449039841433495899)
XLA Ops:
  7.2 0.8 broadcast_add_fusion
  8.0 1.0 maximum_maximum_fusion
  9.1 2.9 collective-permute-start.1
  11.9 2.3 collective-permute-start
  14.2 0.7 multiply_subtract_fusion
  15.6 0.7 copy.29
  16.3 16.6 %all-to-all-start = ((s32[128,1,4]{2,1,0:T(1,128)}), s32[128,1,4]{2,1,0:T(1,128)S(1)}, u32[]{:S(2)}, u32[]{:S(2)}) async-start(s32[128,1,4]{2,1,0:T(1,128)} %copy.29), calls=%async_computation | async-start | bytes 131072 | tf_op jit(solution)/shard_map/all_to_all | solution.py:74
  33.0 0.7 all-gather.3.cloned.1.call-update
  33.7 1.2 copy.30
  35.1 1.2 fusion.52
  37.0 0.4 fusion.55
  38.5 0.4 fusion.57
  42.6 0.5 convolution_convert_fusion.1
  43.0 1.2 all_to_all.16
  44.3 13.7 %all-to-all-start.1 = ((bf16[128,4,1024]{2,1,0:T(4,128)(2,1)}), bf16[128,4,1024]{2,1,0:T(4,128)(2,1)S(1)}, u32[]{:S(2)}, u32[]{:S(2)}) async-start(bf16[128,4,1024]{2,1,0:T(4,128)(2,1)} %all_to_all.16), calls=%async_computation.1 | async-start | bytes 2097152 | tf_op jit(solution)/shard_map/all_to_all | solution.py:86
  58.1 1.3 gather_fusion
  59.4 0.5 broadcast.182
  59.9 0.8 reduce.5
  60.8 26.4 %all-to-all-done.1 = bf16[128,4,1024]{2,1,0:T(4,128)(2,1)S(1)} async-done(((bf16[128,4,1024]{2,1,0:T(4,128)(2,1)}), bf16[128,4,1024]{2,1,0:T(4,128)(2,1)S(1)}, u32[]{:S(2)}, u32[]{:S(2)}) %all-to-all-start.1) | async-done | bytes 1048608 | tf_op jit(solution)/shard_map/all_to_all | solution.py:86
  87.2 1.1 all_to_all.18
  88.3 1.7 convolution_convert_fusion.2
  90.0 46.0 %all-gather.3.cloned.1.call-done = bf16[128,12,1024]{2,1,0:T(8,128)(2,1)} async-done(((bf16[1,12,1024]{2,1,0:T(8,128)(2,1)}), bf16[128,12,1024]{2,1,0:T(8,128)(2,1)}) %all-gather.3.cloned.1.call-update) | async-done | bytes 3145744 | tf_op jit(solution)/shard_map/all_gather | solution.py:89
  136.0 6.2 %reshape.159 = bf16[1536,1024]{1,0:T(8,128)(2,1)} reshape(bf16[128,12,1024]{2,1,0:T(8,128)(2,1)} %all-gather.3.cloned.1.call-done) | data formatting | bytes 6291456
  142.2 4.1 %fusion.60 = f32[256,1536]{1,0:T(8,128)} fusion(bf16[256,1024]{1,0:T(8,128)(2,1)S(1)} %convolution_convert_fusion.2, bf16[1536,1024]{1,0:T(8,128)(2,1)} %reshape.159), kind=kOutput, calls=%fused_computation.134 | convolution fusion | flops 805306368 | bytes 5242880 | tf_op jit(solution)/shard_map/tf,nf->tn/dot_general | solution.py:90
  146.2 33.8 %all-reduce.1 = bf16[256,1536]{1,0:T(8,128)(2,1)S(1)} all-reduce(f32[256,1536]{1,0:T(8,128)} %fusion.60), channel_id=1, replica_groups=mesh['seq'=128,'tp'=4] {'tp'}, use_global_device_ids=true, to_apply=%region_18.19 | all-reduce | flops 393216 | bytes 2359296 | tf_op jit(solution)/shard_map/psum | solution.py:91
  180.0 2.7 convolution_convert_fusion
  182.7 6.1 %convert_element_type.112 = bf16[128,12,1024]{2,1,0:T(8,128)(2,1)} reshape(bf16[1536,1024]{1,0:T(8,128)(2,1)} %convolution_convert_fusion) | data formatting | bytes 6291456 | tf_op jit(solution)/shard_map/convert_element_type | solution.py:100
  188.8 13.8 %all-to-all-start.2 = ((bf16[128,12,1024]{2,1,0:T(8,128)(2,1)}), bf16[128,12,1024]{2,1,0:T(8,128)(2,1)}, u32[]{:S(2)}, u32[]{:S(2)}) async-start(bf16[128,12,1024]{2,1,0:T(8,128)(2,1)} %convert_element_type.112), calls=%async_computation.2 | async-start | bytes 8388608 | tf_op jit(solution)/shard_map/all_to_all | solution.py:99
  202.6 0.7 constant_dynamic-slice_fusion
  203.3 103.0 %all-to-all-done.2 = bf16[128,12,1024]{2,1,0:T(8,128)(2,1)} async-done(((bf16[128,12,1024]{2,1,0:T(8,128)(2,1)}), bf16[128,12,1024]{2,1,0:T(8,128)(2,1)}, u32[]{:S(2)}, u32[]{:S(2)}) %all-to-all-start.2) | async-done | bytes 3145760 | tf_op jit(solution)/shard_map/all_to_all | solution.py:99
  306.3 3.0 convert_reduce_fusion
  309.3 0.6 broadcast_multiply_fusion
  (53 shorter events, 6.4 us)
Async XLA Ops:
  7.2 50.9 %copy-start = (bf16[256,1536]{1,0:T(8,128)(2,1)S(1)}, bf16[256,1536]{1,0:T(8,128)(2,1)}, u32[]{:S(2)}) copy-start(bf16[256,1536]{1,0:T(8,128)(2,1)} %param.14) | copy-start | bytes 2359300
  7.2 29.1 %copy-start.1 = (bf16[256,128]{1,0:T(8,128)(2,1)S(1)}, bf16[256,128]{1,0:T(8,128)(2,1)}, u32[]{:S(2)}) copy-start(bf16[256,128]{1,0:T(8,128)(2,1)} %param.9) | copy-start | bytes 196612
  9.1 25.9 %collective-permute-start.1 = (bf16[528,128]{1,0:T(8,128)(2,1)S(1)}, bf16[528,128]{1,0:T(8,128)(2,1)S(1)}, u32[]{:S(2)}, u32[]{:S(2)}) collective-permute-start(bf16[528,128]{1,0:T(8,128)(2,1)S(1)} %maximum_maximum_fusion), channel_id=1, source_target_pairs={{0,4},{4,8},{8,12},{12,16},{16,20},{20,24},{24,28},{28,32},{32,36}... | collective-permute-start | bytes 405512 | tf_op jit(solution)/shard_map/ppermute | solution.py:22
  11.9 23.1 %collective-permute-start = (bf16[528,128]{1,0:T(8,128)(2,1)S(1)}, bf16[528,128]{1,0:T(8,128)(2,1)S(1)}, u32[]{:S(2)}, u32[]{:S(2)}) collective-permute-start(bf16[528,128]{1,0:T(8,128)(2,1)S(1)} %maximum_maximum_fusion), channel_id=1, source_target_pairs={{0,8},{4,12},{8,16},{12,20},{16,24},{20,28},{24,32},{28,36},{32,40... | collective-permute-start | bytes 405512 | tf_op jit(solution)/shard_map/ppermute | solution.py:22
  16.3 28.0 %all-to-all-start = ((s32[128,1,4]{2,1,0:T(1,128)}), s32[128,1,4]{2,1,0:T(1,128)S(1)}, u32[]{:S(2)}, u32[]{:S(2)}) async-start(s32[128,1,4]{2,1,0:T(1,128)} %copy.29), calls=%async_computation | async-start | bytes 131072 | tf_op jit(solution)/shard_map/all_to_all | solution.py:74
  33.0 103.0 %all-gather.3.cloned.1.call-start = ((), (), s32[]{:S(2)}) async-start(), calls=%async_computation.3 | async-start | bytes 4227072 | tf_op jit(solution)/shard_map/all_gather | solution.py:89
  38.9 1.2 copy-start.2
  42.5 15.5 %copy-start.3 = (s32[256]{0:T(256)S(1)}, s32[256]{0:T(256)}, u32[]{:S(2)}) copy-start(s32[256]{0:T(256)} %param.15) | copy-start | bytes 3076
  44.3 42.9 %all-to-all-start.1 = ((bf16[128,4,1024]{2,1,0:T(4,128)(2,1)}), bf16[128,4,1024]{2,1,0:T(4,128)(2,1)S(1)}, u32[]{:S(2)}, u32[]{:S(2)}) async-start(bf16[128,4,1024]{2,1,0:T(4,128)(2,1)} %all_to_all.16), calls=%async_computation.1 | async-start | bytes 2097152 | tf_op jit(solution)/shard_map/all_to_all | solution.py:86
  188.8 117.5 %all-to-all-start.2 = ((bf16[128,12,1024]{2,1,0:T(8,128)(2,1)}), bf16[128,12,1024]{2,1,0:T(8,128)(2,1)}, u32[]{:S(2)}, u32[]{:S(2)}) async-start(bf16[128,12,1024]{2,1,0:T(8,128)(2,1)} %convert_element_type.112), calls=%async_computation.2 | async-start | bytes 8388608 | tf_op jit(solution)/shard_map/all_to_all | solution.py:99
Sparse Core Ops, SparseCore 0:
  36.9 99.0 all-gather.2

commit v2 on v1

v2 whole, which is shorter than its diff:
```python
import math

import jax
import jax.numpy as jnp
from jax import lax
from jax.sharding import PartitionSpec as P

HEADS = 32
KV_HEADS = 4
HEAD_DIM = 128
SW = 1536
REACH = 2
GROUP_ROWS = 4
SIDE = 8

neg_large = -1e30
bf16, f32, i32 = jnp.bfloat16, jnp.float32, jnp.int32


def seq_index(z, y, core):
    return (z * SIDE + y) * 2 + core


NEAR = [[seq_index(z, y, 0) for y in range(SIDE)] for z in range(SIDE)] + [
    [seq_index(z, y, 1) for z in range(SIDE)] for y in range(SIDE)
]
FAR = [[seq_index(z, y, 0) for z in range(SIDE)] for y in range(SIDE)] + [
    [seq_index(z, y, 1) for y in range(SIDE)] for z in range(SIDE)
]


def exchange(block, groups=None, axis="seq"):
    return lax.all_to_all(
        block, axis, split_axis=0, concat_axis=0, tiled=True, axis_index_groups=groups
    )


def passed_along(block, axis, distance):
    devices = range(lax.axis_size(axis))
    route = [(i - distance, i) for i in devices if i - distance in devices]
    return lax.ppermute(block, axis, route)


def other_core(block):
    return lax.ppermute(block, "seq", [(i, i ^ 1) for i in range(lax.axis_size("seq"))])


def to_all(block, count):
    return jnp.broadcast_to(block[None], (count,) + block.shape)


def attend(queries, keys, values, segment):
    row_count = queries.shape[0]
    lanes = keys.shape[1]
    seg_rows = (segment + 1).astype(bf16).reshape(-1, lanes)
    seg_rows = jnp.concatenate([seg_rows, jnp.zeros((14, lanes), bf16)], 0)
    packed = jnp.concatenate([keys, values, seg_rows], 0)
    blocks = [packed]
    for step in range(1, REACH + 1):
        blocks.insert(0, passed_along(packed, "seq", step))
    all_keys = jnp.concatenate([b[:row_count] for b in blocks], 0)
    all_values = jnp.concatenate([b[row_count : 2 * row_count] for b in blocks], 0)
    key_seg = jnp.concatenate(
        [b[2 * row_count : 2 * row_count + 2].reshape(-1) for b in blocks], 0
    ).astype(i32)
    key_pos = jnp.arange(3 * row_count, dtype=i32) - REACH * row_count
    row_pos = jnp.arange(row_count, dtype=i32)
    allowed = (key_seg[None, :] == (segment + 1)[:, None]) & (key_pos[None, :] <= row_pos[:, None])
    group = HEADS // KV_HEADS
    q_heads = queries.reshape(row_count, group, HEAD_DIM)
    scale = 1.0 / math.sqrt(HEAD_DIM)
    outputs = []
    for head in range(group):
        scores = (
            jnp.einsum("td,sd->ts", q_heads[:, head], all_keys, preferred_element_type=f32)
            * scale
        )
        scores = jnp.where(allowed, scores, neg_large)
        top = jnp.max(scores, axis=-1, keepdims=True)
        expo = jnp.exp(scores - top)
        weights = (expo / jnp.sum(expo, axis=-1, keepdims=True)).astype(bf16)
        mixed = jnp.einsum("ts,sd->td", weights, all_values, preferred_element_type=f32)
        outputs.append(mixed.astype(bf16))
    return jnp.concatenate(outputs, axis=1)


def dot(a, b, dims):
    return lax.dot_general(a, b, (dims, ((), ())), preferred_element_type=f32)


def hot(a, b):
    return (a == b).astype(bf16)


def spread_of(core):
    block = jnp.arange(192, dtype=i32) // 12
    inner = jnp.arange(192, dtype=i32) % 12
    if core == 0:
        pair = block
    else:
        pair = (block % 2) * SIDE + block // 2
    source = 24 * pair + 12 * core + inner
    return hot(jnp.arange(384, dtype=i32)[:, None], source[None, :])


def on_device(queries, keys, values, segment, repack, proj, student_states, target_row):
    rows = queries.shape[0]
    devices = lax.axis_size("seq")
    shares = lax.axis_size("tp")
    groups = rows // GROUP_ROWS
    share = SW // shares
    core = lax.axis_index("seq") % 2
    tp_index = lax.axis_index("tp")
    feats = proj.shape[0]
    near = exchange(to_all(proj, SIDE), NEAR)
    near = near.reshape(SIDE * feats, -1)
    half_proj = exchange(to_all(near, SIDE), FAR).reshape(SIDE * SIDE * feats, -1)
    target_dev = repack // rows
    local_slot = repack - target_dev * rows
    owners = target_dev.reshape(groups, GROUP_ROWS)[:, 0]
    owner_hot = owners[None, :] == jnp.arange(devices, dtype=i32)[:, None]
    slots_by_group = local_slot.reshape(groups, GROUP_ROWS)
    slot_table = jnp.sum(jnp.where(owner_hot[:, :, None], slots_by_group[None], 0), axis=1)
    slot_table = jnp.where(jnp.any(owner_hot, axis=1)[:, None], slot_table, rows)
    slots = exchange(slot_table).reshape(-1)
    slot_hot = hot(slots[:, None], jnp.arange(rows, dtype=i32)[None, :])
    student_part = lax.dynamic_slice_in_dim(student_states, tp_index * share, share, 1)
    chosen = dot(hot(target_row[:, None], jnp.arange(rows, dtype=i32)[None, :]), student_part, ((1,), (0,)))
    chosen = dot(slot_hot, chosen.astype(bf16), ((1,), (0,))).astype(bf16)
    spreads = [spread_of(0), spread_of(1)]
    chips = devices // 2
    outgoing = [
        dot(chosen, s, ((1,), (0,))).astype(bf16).reshape(chips, 1, 2 * GROUP_ROWS, -1)
        for s in spreads
    ]
    outgoing = jnp.concatenate(outgoing, 1).reshape(devices, 2 * GROUP_ROWS, -1)
    target_in = exchange(outgoing).reshape(devices * 2 * GROUP_ROWS, -1)
    dev_both = jnp.concatenate([target_dev, other_core(target_dev)], 0)
    row_ids = jnp.arange(2 * rows, dtype=i32)
    row_core = jnp.where(row_ids < rows, core, 1 - core)
    row_place = dev_both * (2 * GROUP_ROWS) + row_core * GROUP_ROWS + row_ids % GROUP_ROWS
    place_hot = hot(jnp.arange(devices * 2 * GROUP_ROWS, dtype=i32)[:, None], row_place[None, :])
    target = dot(target_in, place_hot, ((0,), (0,)))
    attended = attend(queries, keys, values, segment)
    both = jnp.concatenate([attended, other_core(attended)], 0)
    y_part = dot(half_proj, both, ((1,), (1,))).astype(bf16)
    per_share = y_part.shape[0] // shares
    along = y_part.reshape(shares, per_share, 2 * rows)
    across = y_part.reshape(SIDE, shares, 2 * feats, 2 * rows).swapaxes(0, 1)
    y_split = jnp.where(core == 0, along, across.reshape(along.shape))
    y_terms = exchange(y_split, axis="tp")
    y_rounded = jnp.sum(y_terms.astype(f32), axis=0).astype(bf16)
    delta = (y_rounded.astype(f32) - target).astype(bf16)
    deltas = exchange(to_all(delta, shares), axis="tp")
    y_out = dot(place_hot, y_rounded, ((1,), (1,))).astype(bf16)
    y_in = exchange(y_out.reshape(devices, 2 * GROUP_ROWS, -1))
    y_in = y_in.reshape(chips, 2, 2 * GROUP_ROWS, -1)
    out_rows = 0.0
    for k in range(2):
        part = y_in[:, k].reshape(chips * 2 * GROUP_ROWS, -1)
        part = dot(slot_hot, part, ((0,), (0,))).astype(bf16)
        out_rows = out_rows + dot(part, spreads[k], ((1,), (1,)))
    out_rows = out_rows.astype(bf16)
    across = deltas.reshape(shares, SIDE, 2 * feats, 2 * rows).swapaxes(0, 1)
    deltas = jnp.where(
        core == 0, deltas.reshape(-1, 2 * rows), across.reshape(-1, 2 * rows)
    )
    term = dot(deltas, both, ((1,), (0,))).astype(bf16)
    far = exchange(term.reshape(SIDE, SIDE * feats, -1), FAR)
    far = jnp.sum(far.astype(f32), axis=0).astype(bf16)
    last = exchange(far.reshape(SIDE, feats, -1), NEAR)
    norm_factor = 1.0 / math.sqrt(rows * devices)
    grad = jnp.sum(last.astype(f32), axis=0) * norm_factor
    return (out_rows, grad)


def solution(mesh):
    placed = (
        P("seq", "tp"),
        P("seq", "tp"),
        P("seq", "tp"),
        P("seq"),
        P("seq"),
        P("seq", "tp"),
        P("seq", None),
        P("seq"),
    )
    return jax.shard_map(
        on_device,
        mesh=mesh,
        in_specs=placed,
        out_specs=(P("seq", "tp"), P("seq", "tp")),
        check_vma=False,
    )
```

time: 318 us -> 216 us (0.68)
  the two profiles are of different devices: /device:TPU:41 before, /device:TPU:1 now
where the time goes in v2:
time: 216 us; the launch traced here: 215 us
  waiting for transfers between devices  97.6 us (45%)
  starting transfers between devices  62.3 us (29%)
  matrix products  20.8 us (10%)
  blocking collectives  15 us (7%)
  local copies, waits for them, and re-layouts  9.61 us (4%)
  other arithmetic  8.57 us (4%)
    all_to_all x8, waiting for transfers between devices, exchange(): lax.all_to_all(block, axis, split_axis=0, concat_axis=0, tiled=True, axis...  96.8 us
    all_to_all x8, starting transfers between devices, exchange(): lax.all_to_all(block, axis, split_axis=0, concat_axis=0, tiled=True, axis...  49.1 us
    all_to_all x1, blocking collectives, exchange(): lax.all_to_all(block, axis, split_axis=0, concat_axis=0, tiled=True, axis...  15 us
    dot_general x9, matrix products, dot(): return lax.dot_general(a, b, (dims, ((), ())), preferred_element_type=f32)  9.83 us
    ppermute x2, starting transfers between devices, passed_along(): return lax.ppermute(block, axis, route)  7.79 us
    dot_general x8, matrix products, attend(): jnp.einsum('ts,sd->td', weights, all_values, preferred_element_type=f32)  7.31 us
    ppermute x2, starting transfers between devices, other_core(): lax.ppermute(block, 'seq', [(i, i ^ 1) for i in range(lax.axis_size('seq'...  5.38 us
  transfers between devices with their start and end apart: 12, of which 9 were waited for; matrix products, arithmetic and copies ran while one was open for 12% of the time, Pallas kernels for 0%

profile of v2, /device:TPU:1, one launch (start us, length us, event | category | flops | bytes accessed | tf_op | source)
XLA Modules:
  0.0 215.0 jit_solution(11970693822579305341)
XLA Ops:
  1.5 1.0 maximum_maximum_fusion
  2.5 4.6 %collective-permute-start.2 = (bf16[528,128]{1,0:T(8,128)(2,1)S(1)}, bf16[528,128]{1,0:T(8,128)(2,1)S(1)}, u32[]{:S(2)}, u32[]{:S(2)}) collective-permute-start(bf16[528,128]{1,0:T(8,128)(2,1)S(1)} %maximum_maximum_fusion), channel_id=1, source_target_pairs={{0,4},{4,8},{8,12},{12,16},{16,20},{20,24},{24,28},{28,32},{32,36}... | collective-permute-start | bytes 405512 | tf_op jit(solution)/shard_map/ppermute | solution.py:41
  7.1 3.2 %collective-permute-start.1 = (bf16[528,128]{1,0:T(8,128)(2,1)S(1)}, bf16[528,128]{1,0:T(8,128)(2,1)S(1)}, u32[]{:S(2)}, u32[]{:S(2)}) collective-permute-start(bf16[528,128]{1,0:T(8,128)(2,1)S(1)} %maximum_maximum_fusion), channel_id=1, source_target_pairs={{0,8},{4,12},{8,16},{12,20},{16,24},{20,28},{24,32},{28,36},{32,40... | collective-permute-start | bytes 405512 | tf_op jit(solution)/shard_map/ppermute | solution.py:41
  10.4 1.5 broadcast_in_dim.117
  11.8 10.0 %all-to-all-start.1 = ((bf16[8,12,1024]{2,1,0:T(8,128)(2,1)}), bf16[8,12,1024]{2,1,0:T(8,128)(2,1)S(1)}, u32[]{:S(2)}, u32[]{:S(2)}) async-start(bf16[8,12,1024]{2,1,0:T(8,128)(2,1)} %broadcast_in_dim.117), calls=%async_computation.1 | async-start | bytes 524288 | tf_op jit(solution)/shard_map/all_to_all | solution.py:33
  27.6 1.2 fusion.81
  28.8 2.4 %all-to-all-done.1 = bf16[8,12,1024]{2,1,0:T(8,128)(2,1)S(1)} async-done(((bf16[8,12,1024]{2,1,0:T(8,128)(2,1)}), bf16[8,12,1024]{2,1,0:T(8,128)(2,1)S(1)}, u32[]{:S(2)}, u32[]{:S(2)}) %all-to-all-start.1) | async-done | bytes 196640 | tf_op jit(solution)/shard_map/all_to_all | solution.py:33
  31.2 9.9 %all-to-all-start = ((s32[128,1,4]{2,1,0:T(1,128)}), s32[128,1,4]{2,1,0:T(1,128)S(1)}, u32[]{:S(2)}, u32[]{:S(2)}) async-start(s32[128,1,4]{2,1,0:T(1,128)} %copy.58), calls=%async_computation | async-start | bytes 131072 | tf_op jit(solution)/shard_map/all_to_all | solution.py:33
  41.4 11.2 %all-to-all-done = s32[128,1,4]{2,1,0:T(1,128)S(1)} async-done(((s32[128,1,4]{2,1,0:T(1,128)}), s32[128,1,4]{2,1,0:T(1,128)S(1)}, u32[]{:S(2)}, u32[]{:S(2)}) %all-to-all-start) | async-done | bytes 2080 | tf_op jit(solution)/shard_map/all_to_all | solution.py:33
  52.6 1.3 broadcast_in_dim.119
  53.9 3.6 %all-to-all-start.2 = ((bf16[8,96,1024]{2,1,0:T(8,128)(2,1)}), bf16[8,96,1024]{2,1,0:T(8,128)(2,1)S(1)}, u32[]{:S(2)}, u32[]{:S(2)}) async-start(bf16[8,96,1024]{2,1,0:T(8,128)(2,1)} %broadcast_in_dim.119), calls=%async_computation.2 | async-start | bytes 3145728 | tf_op jit(solution)/shard_map/all_to_all | solution.py:33
  57.7 1.4 fusion.42
  59.1 0.9 fusion.24
  67.7 2.5 %collective-permute-start.3 = (bf16[256,1024]{0,1:T(8,128)(2,1)}, bf16[256,1024]{0,1:T(8,128)(2,1)}, u32[]{:S(2)}, u32[]{:S(2)}) collective-permute-start(bf16[256,1024]{0,1:T(8,128)(2,1)} %fusion.31), channel_id=1, source_target_pairs={{0,4},{4,0},{8,12},{12,8},{16,20},{20,16},{24,28},{28,24},{32,36},... | collective-permute-start | bytes 1572872 | tf_op jit(solution)/shard_map/ppermute | solution.py:45
  72.2 8.9 %all-to-all-done.2 = bf16[8,96,1024]{2,1,0:T(8,128)(2,1)S(1)} async-done(((bf16[8,96,1024]{2,1,0:T(8,128)(2,1)}), bf16[8,96,1024]{2,1,0:T(8,128)(2,1)S(1)}, u32[]{:S(2)}, u32[]{:S(2)}) %all-to-all-start.2) | async-done | bytes 1572896 | tf_op jit(solution)/shard_map/all_to_all | solution.py:33
  81.1 2.2 %fusion.2 = bf16[768,512]{0,1:T(8,128)(2,1)S(1)} fusion(bf16[768,1024]{1,0:T(8,128)(2,1)S(1)} %bitcast.133, bf16[256,1024]{0,1:T(8,128)(2,1)} %collective-permute-done.3, bf16[256,1024]{0,1:T(8,128)(2,1)} %fusion.31), kind=kOutput, calls=%fused_computation.5 | convolution fusion | flops 807796736 | bytes 3407872 | tf_op jit(solution)/shard_map/dot_general | solution.py:88
  83.7 1.0 bitcast_select_fusion.1
  84.7 4.0 %all-to-all-start.3 = ((bf16[4,192,512]{2,1,0:T(8,128)(2,1)}), bf16[4,192,512]{2,1,0:T(8,128)(2,1)S(1)}, u32[]{:S(2)}, u32[]{:S(2)}) async-start(bf16[4,192,512]{2,1,0:T(8,128)(2,1)} %bitcast_select_fusion.1), calls=%async_computation.3 | async-start | bytes 1572864 | tf_op jit(solution)/shard_map/all_to_all | solution.py:33
  90.6 8.5 %all-to-all-done.3 = bf16[4,192,512]{2,1,0:T(8,128)(2,1)S(1)} async-done(((bf16[4,192,512]{2,1,0:T(8,128)(2,1)}), bf16[4,192,512]{2,1,0:T(8,128)(2,1)S(1)}, u32[]{:S(2)}, u32[]{:S(2)}) %all-to-all-start.3) | async-done | bytes 786464 | tf_op jit(solution)/shard_map/all_to_all | solution.py:33
  99.2 8.0 %all-to-all-start.5 = ((bf16[128,8,192]{2,1,0:T(8,128)(2,1)}), bf16[128,8,192]{2,1,0:T(8,128)(2,1)S(1)}, u32[]{:S(2)}, u32[]{:S(2)}) async-start(bf16[128,8,192]{2,1,0:T(8,128)(2,1)} %bitcast.33), calls=%async_computation.5 | async-start | bytes 1048576 | tf_op jit(solution)/shard_map/all_to_all | solution.py:33
  107.1 2.9 %collective-permute-start = (s32[256]{0:T(256)S(1)}, s32[256]{0:T(256)S(1)}, u32[]{:S(2)}, u32[]{:S(2)}) collective-permute-start(s32[256]{0:T(256)S(1)} %get-tuple-element.3), channel_id=1, source_target_pairs={{0,4},{4,0},{8,12},{12,8},{16,20},{20,16},{24,28},{28,24},{32,36},... | collective-permute-start | bytes 3080 | tf_op jit(solution)/shard_map/ppermute | solution.py:45
  111.0 16.8 %all-to-all-done.5 = bf16[128,8,192]{2,1,0:T(8,128)(2,1)S(1)} async-done(((bf16[128,8,192]{2,1,0:T(8,128)(2,1)}), bf16[128,8,192]{2,1,0:T(8,128)(2,1)S(1)}, u32[]{:S(2)}, u32[]{:S(2)}) %all-to-all-start.5) | async-done | bytes 393248 | tf_op jit(solution)/shard_map/all_to_all | solution.py:33
  128.5 15.0 %all_to_all.46 = bf16[4,192,512]{2,1,0:T(8,128)(2,1)S(1)} all-to-all(bf16[4,192,512]{2,1,0:T(8,128)(2,1)S(1)} %broadcast_in_dim.120), channel_id=1, replica_groups=mesh['seq'=128,'tp'=4] {'tp'}, dimensions={0} | all-to-all | bytes 1572864 | tf_op jit(solution)/shard_map/all_to_all | solution.py:33
  143.8 3.4 %convolution_convert_fusion = bf16[768,1024]{1,0:T(8,128)(2,1)} fusion(bf16[768,512]{1,0:T(8,128)(2,1)S(1)} %bitcast_select_fusion, bf16[256,1024]{0,1:T(8,128)(2,1)} %collective-permute-done.3, bf16[256,1024]{0,1:T(8,128)(2,1)} %fusion.31), kind=kOutput, calls=%fused_computation.3 | convolution fusion | flops 808189952 | bytes 3407872 | tf_op jit(solution)/shard_map/dot_general | solution.py:88
  147.1 3.6 %all-to-all-start.7 = ((bf16[8,96,1024]{2,1,0:T(8,128)(2,1)}), bf16[8,96,1024]{2,1,0:T(8,128)(2,1)S(1)}, u32[]{:S(2)}, u32[]{:S(2)}) async-start(bf16[8,96,1024]{2,1,0:T(8,128)(2,1)} %bitcast.134), calls=%async_computation.7 | async-start | bytes 3145728 | tf_op jit(solution)/shard_map/all_to_all | solution.py:33
  151.3 1.0 copy.71
  152.3 22.0 %all-to-all-done.7 = bf16[8,96,1024]{2,1,0:T(8,128)(2,1)S(1)} async-done(((bf16[8,96,1024]{2,1,0:T(8,128)(2,1)}), bf16[8,96,1024]{2,1,0:T(8,128)(2,1)S(1)}, u32[]{:S(2)}, u32[]{:S(2)}) %all-to-all-start.7) | async-done | bytes 1572896 | tf_op jit(solution)/shard_map/all_to_all | solution.py:33
  174.4 6.6 %all-to-all-start.4 = ((bf16[128,8,192]{2,1,0:T(8,128)(2,1)}), bf16[128,8,192]{2,1,0:T(8,128)(2,1)S(1)}, u32[]{:S(2)}, u32[]{:S(2)}) async-start(bf16[128,8,192]{2,1,0:T(8,128)(2,1)} %bitcast.27), calls=%async_computation.4 | async-start | bytes 1048576 | tf_op jit(solution)/shard_map/all_to_all | solution.py:33
  182.0 19.6 %all-to-all-done.4 = bf16[128,8,192]{2,1,0:T(8,128)(2,1)S(1)} async-done(((bf16[128,8,192]{2,1,0:T(8,128)(2,1)}), bf16[128,8,192]{2,1,0:T(8,128)(2,1)S(1)}, u32[]{:S(2)}, u32[]{:S(2)}) %all-to-all-start.4) | async-done | bytes 393248 | tf_op jit(solution)/shard_map/all_to_all | solution.py:33
  201.6 3.4 %all-to-all-start.8 = ((bf16[8,12,1024]{2,1,0:T(8,128)(2,1)}), bf16[8,12,1024]{2,1,0:T(8,128)(2,1)S(1)}, u32[]{:S(2)}, u32[]{:S(2)}) async-start(bf16[8,12,1024]{2,1,0:T(8,128)(2,1)} %reshape.260), calls=%async_computation.8 | async-start | bytes 524288 | tf_op jit(solution)/shard_map/all_to_all | solution.py:33
  205.6 1.3 fusion.21
  206.9 7.4 %all-to-all-done.8 = bf16[8,12,1024]{2,1,0:T(8,128)(2,1)S(1)} async-done(((bf16[8,12,1024]{2,1,0:T(8,128)(2,1)}), bf16[8,12,1024]{2,1,0:T(8,128)(2,1)S(1)}, u32[]{:S(2)}, u32[]{:S(2)}) %all-to-all-start.8) | async-done | bytes 196640 | tf_op jit(solution)/shard_map/all_to_all | solution.py:33
  (107 shorter events, 23.5 us)
Async XLA Ops:
  0.6 71.0 %copy-start = (bf16[256,1536]{1,0:T(8,128)(2,1)S(1)}, bf16[256,1536]{1,0:T(8,128)(2,1)}, u32[]{:S(2)}) copy-start(bf16[256,1536]{1,0:T(8,128)(2,1)} %param.14) | copy-start | bytes 2359300
  0.6 23.6 %copy-start.15 = (bf16[256,128]{1,0:T(8,128)(2,1)S(1)}, bf16[256,128]{1,0:T(8,128)(2,1)}, u32[]{:S(2)}) copy-start(bf16[256,128]{1,0:T(8,128)(2,1)} %param.9) | copy-start | bytes 196612
  0.7 22.5 %copy-start.14 = (bf16[256,1024]{1,0:T(8,128)(2,1)S(1)}, bf16[256,1024]{1,0:T(8,128)(2,1)}, u32[]{:S(2)}) copy-start(bf16[256,1024]{1,0:T(8,128)(2,1)} %param.8) | copy-start | bytes 1572868
  2.5 21.6 %collective-permute-start.2 = (bf16[528,128]{1,0:T(8,128)(2,1)S(1)}, bf16[528,128]{1,0:T(8,128)(2,1)S(1)}, u32[]{:S(2)}, u32[]{:S(2)}) collective-permute-start(bf16[528,128]{1,0:T(8,128)(2,1)S(1)} %maximum_maximum_fusion), channel_id=1, source_target_pairs={{0,4},{4,8},{8,12},{12,16},{16,20},{20,24},{24,28},{28,32},{32,36}... | collective-permute-start | bytes 405512 | tf_op jit(solution)/shard_map/ppermute | solution.py:41
  7.1 17.0 %collective-permute-start.1 = (bf16[528,128]{1,0:T(8,128)(2,1)S(1)}, bf16[528,128]{1,0:T(8,128)(2,1)S(1)}, u32[]{:S(2)}, u32[]{:S(2)}) collective-permute-start(bf16[528,128]{1,0:T(8,128)(2,1)S(1)} %maximum_maximum_fusion), channel_id=1, source_target_pairs={{0,8},{4,12},{8,16},{12,20},{16,24},{20,28},{24,32},{28,36},{32,40... | collective-permute-start | bytes 405512 | tf_op jit(solution)/shard_map/ppermute | solution.py:41
  11.8 19.4 %all-to-all-start.1 = ((bf16[8,12,1024]{2,1,0:T(8,128)(2,1)}), bf16[8,12,1024]{2,1,0:T(8,128)(2,1)S(1)}, u32[]{:S(2)}, u32[]{:S(2)}) async-start(bf16[8,12,1024]{2,1,0:T(8,128)(2,1)} %broadcast_in_dim.117), calls=%async_computation.1 | async-start | bytes 524288 | tf_op jit(solution)/shard_map/all_to_all | solution.py:33
  24.6 2.1 copy-start.12
  24.9 2.0 copy-start.10
  25.3 1.8 copy-start.8
  25.7 1.6 copy-start.5
  26.0 1.4 copy-start.3
  26.4 14.8 %copy-start.1 = (f32[256,768]{0,1:T(8,128)}, f32[256,768]{0,1:T(8,128)S(1)}, u32[]{:S(2)}) copy-start(f32[256,768]{0,1:T(8,128)S(1)} %get-tuple-element.23) | copy-start | bytes 2359300
  31.2 21.4 %all-to-all-start = ((s32[128,1,4]{2,1,0:T(1,128)}), s32[128,1,4]{2,1,0:T(1,128)S(1)}, u32[]{:S(2)}, u32[]{:S(2)}) async-start(s32[128,1,4]{2,1,0:T(1,128)} %copy.58), calls=%async_computation | async-start | bytes 131072 | tf_op jit(solution)/shard_map/all_to_all | solution.py:33
  53.9 27.2 %all-to-all-start.2 = ((bf16[8,96,1024]{2,1,0:T(8,128)(2,1)}), bf16[8,96,1024]{2,1,0:T(8,128)(2,1)S(1)}, u32[]{:S(2)}, u32[]{:S(2)}) async-start(bf16[8,96,1024]{2,1,0:T(8,128)(2,1)} %broadcast_in_dim.119), calls=%async_computation.2 | async-start | bytes 3145728 | tf_op jit(solution)/shard_map/all_to_all | solution.py:33
  57.5 1.6 copy-start.13
  57.5 1.6 copy-start.16
  59.1 1.1 copy-start.11
  60.2 1.1 copy-start.9
  61.3 1.1 copy-start.6
  62.5 1.1 copy-start.4
  63.6 1.1 copy-start.2
  65.6 1.1 copy-start.7
  66.8 4.9 %copy-start.17 = (s32[256]{0:T(256)S(1)}, s32[256]{0:T(256)}, u32[]{:S(2)}) copy-start(s32[256]{0:T(256)} %param.15) | copy-start | bytes 3076
  67.7 4.5 %collective-permute-start.3 = (bf16[256,1024]{0,1:T(8,128)(2,1)}, bf16[256,1024]{0,1:T(8,128)(2,1)}, u32[]{:S(2)}, u32[]{:S(2)}) collective-permute-start(bf16[256,1024]{0,1:T(8,128)(2,1)} %fusion.31), channel_id=1, source_target_pairs={{0,4},{4,0},{8,12},{12,8},{16,20},{20,16},{24,28},{28,24},{32,36},... | collective-permute-start | bytes 1572872 | tf_op jit(solution)/shard_map/ppermute | solution.py:45
  84.7 14.4 %all-to-all-start.3 = ((bf16[4,192,512]{2,1,0:T(8,128)(2,1)}), bf16[4,192,512]{2,1,0:T(8,128)(2,1)S(1)}, u32[]{:S(2)}, u32[]{:S(2)}) async-start(bf16[4,192,512]{2,1,0:T(8,128)(2,1)} %bitcast_select_fusion.1), calls=%async_computation.3 | async-start | bytes 1572864 | tf_op jit(solution)/shard_map/all_to_all | solution.py:33
  99.2 28.6 %all-to-all-start.5 = ((bf16[128,8,192]{2,1,0:T(8,128)(2,1)}), bf16[128,8,192]{2,1,0:T(8,128)(2,1)S(1)}, u32[]{:S(2)}, u32[]{:S(2)}) async-start(bf16[128,8,192]{2,1,0:T(8,128)(2,1)} %bitcast.33), calls=%async_computation.5 | async-start | bytes 1048576 | tf_op jit(solution)/shard_map/all_to_all | solution.py:33
  107.1 3.7 %collective-permute-start = (s32[256]{0:T(256)S(1)}, s32[256]{0:T(256)S(1)}, u32[]{:S(2)}, u32[]{:S(2)}) collective-permute-start(s32[256]{0:T(256)S(1)} %get-tuple-element.3), channel_id=1, source_target_pairs={{0,4},{4,0},{8,12},{12,8},{16,20},{20,16},{24,28},{28,24},{32,36},... | collective-permute-start | bytes 3080 | tf_op jit(solution)/shard_map/ppermute | solution.py:45
  147.1 27.2 %all-to-all-start.7 = ((bf16[8,96,1024]{2,1,0:T(8,128)(2,1)}), bf16[8,96,1024]{2,1,0:T(8,128)(2,1)S(1)}, u32[]{:S(2)}, u32[]{:S(2)}) async-start(bf16[8,96,1024]{2,1,0:T(8,128)(2,1)} %bitcast.134), calls=%async_computation.7 | async-start | bytes 3145728 | tf_op jit(solution)/shard_map/all_to_all | solution.py:33
  174.4 27.3 %all-to-all-start.4 = ((bf16[128,8,192]{2,1,0:T(8,128)(2,1)}), bf16[128,8,192]{2,1,0:T(8,128)(2,1)S(1)}, u32[]{:S(2)}, u32[]{:S(2)}) async-start(bf16[128,8,192]{2,1,0:T(8,128)(2,1)} %bitcast.27), calls=%async_computation.4 | async-start | bytes 1048576 | tf_op jit(solution)/shard_map/all_to_all | solution.py:33
  201.6 12.7 %all-to-all-start.8 = ((bf16[8,12,1024]{2,1,0:T(8,128)(2,1)}), bf16[8,12,1024]{2,1,0:T(8,128)(2,1)S(1)}, u32[]{:S(2)}, u32[]{:S(2)}) async-start(bf16[8,12,1024]{2,1,0:T(8,128)(2,1)} %reshape.260), calls=%async_computation.8 | async-start | bytes 524288 | tf_op jit(solution)/shard_map/all_to_all | solution.py:33

commit v3 on v2

v3 whole, which is shorter than its diff:
```python
import math

import jax
import jax.numpy as jnp
from jax import lax
from jax.experimental import pallas as pl
from jax.experimental.pallas import tpu as pltpu
from jax.sharding import PartitionSpec as P


HEADS = 32
KV_HEADS = 4
HEAD_DIM = 128
SW = 1536
REACH = 2
GROUP_ROWS = 4
SIDE = 8

neg_large = -1e30
bf16, f32, i32 = jnp.bfloat16, jnp.float32, jnp.int32


def seq_index(z, y, core):
    return (z * SIDE + y) * 2 + core


NEAR = [[seq_index(z, y, 0) for y in range(SIDE)] for z in range(SIDE)] + [
    [seq_index(z, y, 1) for z in range(SIDE)] for y in range(SIDE)
]
FAR = [[seq_index(z, y, 0) for z in range(SIDE)] for y in range(SIDE)] + [
    [seq_index(z, y, 1) for y in range(SIDE)] for z in range(SIDE)
]


def exchange(block, groups=None, axis="seq"):
    return lax.all_to_all(
        block, axis, split_axis=0, concat_axis=0, tiled=True, axis_index_groups=groups
    )


def passed_along(block, axis, distance):
    devices = range(lax.axis_size(axis))
    route = [(i - distance, i) for i in devices if i - distance in devices]
    return lax.ppermute(block, axis, route)


def along_ring(block, distance):
    route = []
    for z in range(SIDE):
        for y in range(SIDE):
            route.append((seq_index(z, y, 0), seq_index((z + distance) % SIDE, y, 0)))
            route.append((seq_index(z, y, 1), seq_index(z, (y + distance) % SIDE, 1)))
    return lax.ppermute(block, "seq", route)


def other_core(block):
    return lax.ppermute(block, "seq", [(i, i ^ 1) for i in range(lax.axis_size("seq"))])


def to_all(block, count):
    return jnp.broadcast_to(block[None], (count,) + block.shape)


def attend_kernel(q_ref, b2_ref, b1_ref, b0_ref, o_ref, bias_ref):
    rows = q_ref.shape[0]
    blocks = (b2_ref, b1_ref, b0_ref)
    seg_lanes = [
        b[2 * rows + i : 2 * rows + i + 1, :].astype(f32) for b in blocks for i in range(2)
    ]
    seg_keys = jnp.concatenate(seg_lanes, axis=1)
    for i in range(2):
        column = jnp.transpose(jnp.broadcast_to(seg_lanes[4 + i], (HEAD_DIM, HEAD_DIM)))
        column = jnp.concatenate([column] * 6, axis=1)
        row_pos = lax.broadcasted_iota(i32, column.shape, 0) + i * HEAD_DIM
        key_pos = lax.broadcasted_iota(i32, column.shape, 1) - REACH * rows
        allowed = (column == seg_keys) & (key_pos <= row_pos)
        bias_ref[pl.ds(i * HEAD_DIM, HEAD_DIM), :] = jnp.where(allowed, 0.0, neg_large)
    keys = jnp.concatenate([b[0:rows, :] for b in blocks], axis=0)
    values = jnp.concatenate([b[rows : 2 * rows, :] for b in blocks], axis=0)
    scale = 1.0 / math.sqrt(HEAD_DIM)
    for head in range(HEADS // KV_HEADS):
        lanes = slice(head * HEAD_DIM, (head + 1) * HEAD_DIM)
        scores = dot(q_ref[:, lanes], keys, ((1,), (1,))) * scale + bias_ref[...]
        top = jnp.max(scores, axis=-1, keepdims=True)
        expo = jnp.exp(scores - top)
        weights = (expo * (1.0 / jnp.sum(expo, axis=-1, keepdims=True))).astype(bf16)
        o_ref[:, lanes] = dot(weights, values, ((1,), (0,))).astype(bf16)


def attend(queries, keys, values, segment):
    rows, lanes = keys.shape
    seg_rows = (segment + 1).astype(bf16).reshape(-1, lanes)
    seg_rows = jnp.concatenate([seg_rows, jnp.zeros((14, lanes), bf16)], 0)
    packed = jnp.concatenate([keys, values, seg_rows], 0)
    earlier = [passed_along(packed, "seq", step) for step in (1, 2)]
    vmem = pl.BlockSpec(memory_space=pltpu.VMEM)
    return pl.pallas_call(
        attend_kernel,
        out_shape=jax.ShapeDtypeStruct(queries.shape, bf16),
        in_specs=[vmem] * 4,
        out_specs=vmem,
        scratch_shapes=[pltpu.VMEM((rows, (REACH + 1) * rows), f32)],
        compiler_params=pltpu.CompilerParams(vmem_limit_bytes=24 << 20),
        cost_estimate=pl.CostEstimate(
            flops=4 * rows * 3 * rows * 1024, bytes_accessed=2 << 20, transcendentals=rows * 3 * rows * 8
        ),
        name="attend",
    )(queries, earlier[1], earlier[0], packed)


def dot(a, b, dims):
    return lax.dot_general(a, b, (dims, ((), ())), preferred_element_type=f32)


def hot(a, b):
    return (a == b).astype(bf16)


VMEM = pl.BlockSpec(memory_space=pltpu.VMEM)
SMEM = pl.BlockSpec(memory_space=pltpu.SMEM)


def chunk_of(core, ring, quarter):
    return jnp.where(core == 0, ring * 4 + quarter, quarter * SIDE + ring)


def project_kernel(place_ref, own_ref, other_ref, *refs):
    blocks, out_ref = refs[:SIDE], refs[SIDE]
    core, here = place_ref[0], place_ref[1]
    both = jnp.concatenate([own_ref[...], other_ref[...]], axis=0)
    for distance, block in enumerate(blocks):
        ring = lax.rem(here - distance + SIDE, SIDE)
        y = dot(block[...], both, ((1,), (1,))).astype(bf16)
        for quarter in range(4):
            out_ref[chunk_of(core, ring, quarter)] = y[quarter * 24 : quarter * 24 + 24]


def project(place, own, other, blocks):
    rows, feats = own.shape[0] * 2, own.shape[1]
    return pl.pallas_call(
        project_kernel,
        out_shape=jax.ShapeDtypeStruct((32, 24, rows), bf16),
        in_specs=[SMEM] + [VMEM] * (2 + SIDE),
        out_specs=VMEM,
        compiler_params=pltpu.CompilerParams(vmem_limit_bytes=24 << 20),
        cost_estimate=pl.CostEstimate(
            flops=2 * 768 * rows * feats, bytes_accessed=4 << 20, transcendentals=0
        ),
        name="project",
    )(place, own, other, *blocks)


def term_kernel(place_ref, delta_ref, own_ref, other_ref, out_ref):
    core = place_ref[0]
    both = jnp.concatenate([own_ref[...], other_ref[...]], axis=0)
    for ring in range(SIDE):
        left = jnp.concatenate(
            [delta_ref[chunk_of(core, ring, quarter)] for quarter in range(4)], axis=0
        )
        out_ref[ring] = dot(left, both, ((1,), (0,))).astype(bf16)


def term_of(place, deltas, own, other):
    rows, feats = own.shape[0] * 2, own.shape[1]
    return pl.pallas_call(
        term_kernel,
        out_shape=jax.ShapeDtypeStruct((SIDE, 96, feats), bf16),
        in_specs=[SMEM] + [VMEM] * 3,
        out_specs=VMEM,
        compiler_params=pltpu.CompilerParams(vmem_limit_bytes=24 << 20),
        cost_estimate=pl.CostEstimate(
            flops=2 * 768 * rows * feats, bytes_accessed=4 << 20, transcendentals=0
        ),
        name="term",
    )(place, deltas, own, other)


def spread_of(core):
    block = jnp.arange(192, dtype=i32) // 12
    inner = jnp.arange(192, dtype=i32) % 12
    pair = jnp.where(core == 0, block, (block % 2) * SIDE + block // 2)
    source = 24 * pair + 12 * core + inner
    return hot(jnp.arange(384, dtype=i32)[:, None], source[None, :])


def on_device(queries, keys, values, segment, repack, proj, student_states, target_row):
    rows = queries.shape[0]
    devices = lax.axis_size("seq")
    shares = lax.axis_size("tp")
    share = SW // shares
    index = lax.axis_index("seq")
    core = index % 2
    here = jnp.where(core == 0, index // (2 * SIDE), (index // 2) % SIDE)
    place = jnp.stack([core, here]).astype(i32)
    tp_index = lax.axis_index("tp")
    feats = proj.shape[0]
    near = exchange(to_all(proj, SIDE), NEAR).reshape(SIDE * feats, -1)
    attended = attend(queries, keys, values, segment)
    target_dev = repack // rows
    local_slot = repack - target_dev * rows
    row_ids = jnp.arange(rows, dtype=i32)
    bucket_row = target_dev * GROUP_ROWS + row_ids % GROUP_ROWS
    pick = hot(jnp.arange(devices * GROUP_ROWS, dtype=i32)[:, None], bucket_row[None, :])
    slot_lanes = jnp.broadcast_to(local_slot.astype(bf16)[:, None], (rows, 128))
    attended, near = lax.optimization_barrier((attended, near))
    wide = jnp.concatenate([attended, slot_lanes], 1)
    buckets = dot(pick, wide, ((1,), (0,))).astype(bf16)
    buckets = buckets.reshape(devices, GROUP_ROWS, -1)
    arrived = exchange(buckets).reshape(devices * GROUP_ROWS, -1)
    blocks = [near]
    for distance in range(1, SIDE):
        blocks.append(along_ring(near, distance))
    mine, theirs = spread_of(core), spread_of(1 - core)
    student_part = lax.dynamic_slice_in_dim(student_states, tp_index * share, share, 1)
    chosen = dot(hot(target_row[:, None], row_ids[None, :]), student_part, ((1,), (0,)))
    chosen = chosen.astype(bf16)
    target_own = dot(mine, chosen, ((0,), (1,))).astype(bf16)
    target_other = other_core(dot(theirs, chosen, ((0,), (1,))).astype(bf16))
    target = jnp.concatenate([target_own, target_other], 1)
    arrived, target, blocks = lax.optimization_barrier((arrived, target, blocks))
    slot_hot = hot(arrived[:, 1024:1025].astype(i32), row_ids[None, :])
    own = dot(slot_hot, arrived[:, :1024], ((0,), (0,))).astype(bf16)
    other = other_core(own)
    y_split = project(place, own, other, blocks)
    y_split = y_split.reshape(shares, -1, 2 * rows)
    y_terms = exchange(y_split, axis="tp")
    y_rounded = jnp.sum(y_terms.astype(f32), axis=0).astype(bf16)
    delta = (y_rounded.astype(f32) - target.astype(f32)).astype(bf16)
    deltas = exchange(to_all(delta, shares), axis="tp")
    term = term_of(place, deltas.reshape(32, 24, 2 * rows), own, other)
    far = exchange(term, FAR)
    far = jnp.sum(far.astype(f32), axis=0).astype(bf16)
    last = exchange(far.reshape(SIDE, feats, -1), NEAR)
    norm_factor = 1.0 / math.sqrt(rows * devices)
    grad = jnp.sum(last.astype(f32), axis=0) * norm_factor
    rest = other_core(y_rounded[:, rows:])
    out_rows = dot(y_rounded[:, :rows], mine, ((0,), (1,)))
    out_rows = (out_rows + dot(rest, theirs, ((0,), (1,)))).astype(bf16)
    return (out_rows, grad)


def solution(mesh):
    placed = (
        P("seq", "tp"),
        P("seq", "tp"),
        P("seq", "tp"),
        P("seq"),
        P("seq"),
        P("seq", "tp"),
        P("seq", None),
        P("seq"),
    )
    return jax.shard_map(
        on_device,
        mesh=mesh,
        in_specs=placed,
        out_specs=(P("seq", "tp"), P("seq", "tp")),
        check_vma=False,
    )
```

time: 216 us -> 180 us (0.83)
  the two profiles are of different devices: /device:TPU:1 before, /device:TPU:2 now
where the time goes in v3:
time: 180 us; the launch traced here: 179 us
  starting transfers between devices  77 us (43%)
  waiting for transfers between devices  43.9 us (24%)
  blocking collectives  29.7 us (16%)
  Pallas kernels  10.8 us (6%)
  local copies, waits for them, and re-layouts  7.14 us (4%)
  other arithmetic  5.26 us (3%)
  matrix products  4.34 us (2%)
    all_to_all x4, waiting for transfers between devices, exchange(): lax.all_to_all(block, axis, split_axis=0, concat_axis=0, tiled=True, axis...  35.4 us
    ppermute x7, starting transfers between devices, along_ring(): return lax.ppermute(block, 'seq', route)  34.6 us
    all_to_all x4, starting transfers between devices, exchange(): lax.all_to_all(block, axis, split_axis=0, concat_axis=0, tiled=True, axis...  31.6 us
    all_to_all x2, blocking collectives, exchange(): lax.all_to_all(block, axis, split_axis=0, concat_axis=0, tiled=True, axis...  29.7 us
    ppermute x7, waiting for transfers between devices, along_ring(): return lax.ppermute(block, 'seq', route)  6.79 us
    ppermute x3, starting transfers between devices, other_core(): lax.ppermute(block, 'seq', [(i, i ^ 1) for i in range(lax.axis_size('seq'...  5.76 us
    ppermute x2, starting transfers between devices, passed_along(): return lax.ppermute(block, axis, route)  4.96 us
    pallas_call x1, Pallas kernels, attend(): pl.pallas_call(attend_kernel, out_shape=jax.ShapeDtypeStruct(queries.shap...  4.49 us
  transfers between devices with their start and end apart: 16, of which 8 were waited for; matrix products, arithmetic and copies ran while one was open for 5% of the time, Pallas kernels for 3%

profile of v3, /device:TPU:2, one launch (start us, length us, event | category | flops | bytes accessed | tf_op | source)
XLA Modules:
  0.0 179.2 jit_solution(8412390681389467346)
XLA Ops:
  2.5 3.5 %collective-permute-start = (bf16[528,128]{1,0:T(8,128)(2,1)S(1)}, bf16[528,128]{1,0:T(8,128)(2,1)S(1)}, u32[]{:S(2)}, u32[]{:S(2)}) collective-permute-start(bf16[528,128]{1,0:T(8,128)(2,1)S(1)} %maximum_maximum_fusion.b0_ref), channel_id=1, source_target_pairs={{0,8},{4,12},{8,16},{12,20},{16,24},{20,28},{24,32},{28,36},{32,40... | collective-permute-start | bytes 405512 | tf_op jit(solution)/shard_map/ppermute | solution.py:44
  6.0 1.5 collective-permute-start.1
  7.5 1.5 broadcast_in_dim.9
  9.0 6.7 %all-to-all-start = ((bf16[8,12,1024]{2,1,0:T(8,128)(2,1)}), bf16[8,12,1024]{2,1,0:T(8,128)(2,1)S(1)}, u32[]{:S(2)}, u32[]{:S(2)}) async-start(bf16[8,12,1024]{2,1,0:T(8,128)(2,1)} %broadcast_in_dim.9), calls=%async_computation | async-start | bytes 524288 | tf_op jit(solution)/shard_map/all_to_all | solution.py:36
  17.0 1.0 copy-done.1
  18.0 4.5 %attend.1 = bf16[256,1024]{1,0:T(8,128)(2,1)S(1)} custom-call(bf16[256,1024]{1,0:T(8,128)(2,1)S(1)} %copy-done.1, bf16[528,128]{1,0:T(8,128)(2,1)S(1)} %collective-permute-done.b2_ref, bf16[528,128]{1,0:T(8,128)(2,1)S(1)} %collective-permute-done.1.b1_ref, bf16[528,128]{1,0:T(8,128)(2,1)S(1)} %maximum_maximum_fusion.b0_ref), custom_call_target="tpu_custom_call" | custom-call | flops 805306368 | bytes 2097152 | tf_op jit(solution)/shard_map/attend/pallas_call | solution.py:97
  22.5 3.6 %all-to-all-done = bf16[8,12,1024]{2,1,0:T(8,128)(2,1)S(1)} async-done(((bf16[8,12,1024]{2,1,0:T(8,128)(2,1)}), bf16[8,12,1024]{2,1,0:T(8,128)(2,1)S(1)}, u32[]{:S(2)}, u32[]{:S(2)}) %all-to-all-start) | async-done | bytes 196640 | tf_op jit(solution)/shard_map/all_to_all | solution.py:36
  26.8 1.2 reshape.89
  28.0 15.0 %all-to-all-start.1 = ((bf16[128,4,1152]{2,1,0:T(4,128)(2,1)}), bf16[128,4,1152]{2,1,0:T(4,128)(2,1)}, u32[]{:S(2)}, u32[]{:S(2)}) async-start(bf16[128,4,1152]{2,1,0:T(4,128)(2,1)} %reshape.89), calls=%async_computation.1 | async-start | bytes 2359296 | tf_op jit(solution)/shard_map/all_to_all | solution.py:36
  43.3 3.0 %collective-permute-start.3 = (bf16[96,1024]{1,0:T(8,128)(2,1)S(1)}, bf16[96,1024]{1,0:T(8,128)(2,1)S(1)}, u32[]{:S(2)}, u32[]{:S(2)}) collective-permute-start(bf16[96,1024]{1,0:T(8,128)(2,1)S(1)} %reshape.88.refs_0_), channel_id=1, source_target_pairs={{0,64},{4,12},{8,72},{12,20},{16,80},{20,28},{24,88},{28,36},{32,9... | collective-permute-start | bytes 589832 | tf_op jit(solution)/shard_map/ppermute | solution.py:53
  46.3 4.5 %collective-permute-start.4 = (bf16[96,1024]{1,0:T(8,128)(2,1)S(1)}, bf16[96,1024]{1,0:T(8,128)(2,1)S(1)}, u32[]{:S(2)}, u32[]{:S(2)}) collective-permute-start(bf16[96,1024]{1,0:T(8,128)(2,1)S(1)} %reshape.88.refs_0_), channel_id=1, source_target_pairs={{0,128},{4,20},{8,136},{12,28},{16,144},{20,36},{24,152},{28,44},{... | collective-permute-start | bytes 589832 | tf_op jit(solution)/shard_map/ppermute | solution.py:53
  51.0 1.9 %collective-permute-start.2 = (bf16[192,256]{1,0:T(8,128)(2,1)S(1)}, bf16[192,256]{1,0:T(8,128)(2,1)S(1)}, u32[]{:S(2)}, u32[]{:S(2)}) collective-permute-start(bf16[192,256]{1,0:T(8,128)(2,1)S(1)} %convolution_convert_fusion.3), channel_id=1, source_target_pairs={{0,4},{4,0},{8,12},{12,8},{16,20},{20,16},{24,28},{28,24},{32,36},... | collective-permute-start | bytes 294920 | tf_op jit(solution)/shard_map/ppermute | solution.py:57
  52.9 4.9 %collective-permute-start.5 = (bf16[96,1024]{1,0:T(8,128)(2,1)S(1)}, bf16[96,1024]{1,0:T(8,128)(2,1)S(1)}, u32[]{:S(2)}, u32[]{:S(2)}) collective-permute-start(bf16[96,1024]{1,0:T(8,128)(2,1)S(1)} %reshape.88.refs_0_), channel_id=1, source_target_pairs={{0,192},{4,28},{8,200},{12,36},{16,208},{20,44},{24,216},{28,52},{... | collective-permute-start | bytes 589832 | tf_op jit(solution)/shard_map/ppermute | solution.py:53
  57.9 4.9 %collective-permute-start.6 = (bf16[96,1024]{1,0:T(8,128)(2,1)S(1)}, bf16[96,1024]{1,0:T(8,128)(2,1)S(1)}, u32[]{:S(2)}, u32[]{:S(2)}) collective-permute-start(bf16[96,1024]{1,0:T(8,128)(2,1)S(1)} %reshape.88.refs_0_), channel_id=1, source_target_pairs={{0,256},{4,36},{8,264},{12,44},{16,272},{20,52},{24,280},{28,60},{... | collective-permute-start | bytes 589832 | tf_op jit(solution)/shard_map/ppermute | solution.py:53
  62.8 6.1 %collective-permute-start.7 = (bf16[96,1024]{1,0:T(8,128)(2,1)S(1)}, bf16[96,1024]{1,0:T(8,128)(2,1)S(1)}, u32[]{:S(2)}, u32[]{:S(2)}) collective-permute-start(bf16[96,1024]{1,0:T(8,128)(2,1)S(1)} %reshape.88.refs_0_), channel_id=1, source_target_pairs={{0,320},{4,44},{8,328},{12,52},{16,336},{20,60},{24,344},{28,4},{3... | collective-permute-start | bytes 589832 | tf_op jit(solution)/shard_map/ppermute | solution.py:53
  69.2 6.7 %collective-permute-start.8 = (bf16[96,1024]{1,0:T(8,128)(2,1)S(1)}, bf16[96,1024]{1,0:T(8,128)(2,1)S(1)}, u32[]{:S(2)}, u32[]{:S(2)}) collective-permute-start(bf16[96,1024]{1,0:T(8,128)(2,1)S(1)} %reshape.88.refs_0_), channel_id=1, source_target_pairs={{0,384},{4,52},{8,392},{12,60},{16,400},{20,4},{24,408},{28,12},{3... | collective-permute-start | bytes 589832 | tf_op jit(solution)/shard_map/ppermute | solution.py:53
  75.9 1.2 collective-permute-done.4.refs_2_
  77.1 4.6 %collective-permute-start.9 = (bf16[96,1024]{1,0:T(8,128)(2,1)S(1)}, bf16[96,1024]{1,0:T(8,128)(2,1)S(1)}, u32[]{:S(2)}, u32[]{:S(2)}) collective-permute-start(bf16[96,1024]{1,0:T(8,128)(2,1)S(1)} %reshape.88.refs_0_), channel_id=1, source_target_pairs={{0,448},{4,60},{8,456},{12,4},{16,464},{20,12},{24,472},{28,20},{3... | collective-permute-start | bytes 589832 | tf_op jit(solution)/shard_map/ppermute | solution.py:53
  82.7 2.4 %reshape.90 = bf16[512,1152]{1,0:T(8,128)(2,1)S(1)} reshape(bf16[128,4,1152]{2,1,0:T(4,128)(2,1)} %all-to-all-done.1) | data formatting | bytes 2359296 | tf_op jit(solution)/shard_map/reshape | solution.py:209
  86.0 4.3 %collective-permute-done.6.refs_4_ = bf16[96,1024]{1,0:T(8,128)(2,1)S(1)} collective-permute-done((bf16[96,1024]{1,0:T(8,128)(2,1)S(1)}, bf16[96,1024]{1,0:T(8,128)(2,1)S(1)}, u32[]{:S(2)}, u32[]{:S(2)}) %collective-permute-start.6) | collective-permute-done | bytes 196640 | tf_op jit(solution)/shard_map/ppermute | solution.py:53
  90.4 1.8 %convolution_convert_fusion.1.own_ref = bf16[256,1024]{1,0:T(8,128)(2,1)S(1)} fusion(bf16[512,1152]{1,0:T(8,128)(2,1)} %copy-done.2, s32[512]{0:T(512)S(1)} %convert_reduce_fusion.1), kind=kOutput, calls=%fused_computation.1 | convolution fusion | flops 268828672 | bytes 1574912 | tf_op jit(solution)/shard_map/dot_general | solution.py:112
  92.3 1.9 %collective-permute-start.10 = (bf16[256,1024]{1,0:T(8,128)(2,1)S(1)}, bf16[256,1024]{1,0:T(8,128)(2,1)S(1)}, u32[]{:S(2)}, u32[]{:S(2)}) collective-permute-start(bf16[256,1024]{1,0:T(8,128)(2,1)S(1)} %convolution_convert_fusion.1.own_ref), channel_id=1, source_target_pairs={{0,4},{4,0},{8,12},{12,8},{16,20},{20,16},{24,28},{28,24},{32,36},... | collective-permute-start | bytes 1572872 | tf_op jit(solution)/shard_map/ppermute | solution.py:57
  94.3 1.8 collective-permute-done.10.other_ref
  96.1 3.2 %project.1 = bf16[32,24,512]{2,1,0:T(8,128)(2,1)S(1)} custom-call(s32[2]{0:T(128)S(1)} %pad_add_fusion.place_ref, bf16[256,1024]{1,0:T(8,128)(2,1)S(1)} %convolution_convert_fusion.1.own_ref, bf16[256,1024]{1,0:T(8,128)(2,1)S(1)} %collective-permute-done.10.other_ref, bf16[96,1024]{1,0:T(8,128)(2,1)S(1)} %reshape.88.refs_0_, ...), custom_call_target="tpu_custom_call" | custom-call | flops 805306368 | bytes 4194304 | tf_op jit(solution)/shard_map/project/pallas_call | solution.py:140
  99.3 15.9 %all_to_all.30 = bf16[4,192,512]{2,1,0:T(8,128)(2,1)S(1)} all-to-all(bf16[4,192,512]{2,1,0:T(8,128)(2,1)S(1)} %bitcast.9), channel_id=1, replica_groups=mesh['seq'=128,'tp'=4] {'tp'}, dimensions={0} | all-to-all | bytes 1572864 | tf_op jit(solution)/shard_map/all_to_all | solution.py:36
  115.4 13.8 %all_to_all.31 = bf16[4,192,512]{2,1,0:T(8,128)(2,1)S(1)} all-to-all(bf16[4,192,512]{2,1,0:T(8,128)(2,1)S(1)} %broadcast_in_dim.11), channel_id=1, replica_groups=mesh['seq'=128,'tp'=4] {'tp'}, dimensions={0} | all-to-all | bytes 1572864 | tf_op jit(solution)/shard_map/all_to_all | solution.py:36
  129.3 3.2 %term.1 = bf16[8,96,1024]{2,1,0:T(8,128)(2,1)} custom-call(s32[2]{0:T(128)S(1)} %pad_add_fusion.place_ref, bf16[32,24,512]{2,1,0:T(8,128)(2,1)S(1)} %bitcast.10, bf16[256,1024]{1,0:T(8,128)(2,1)S(1)} %convolution_convert_fusion.1.own_ref, bf16[256,1024]{1,0:T(8,128)(2,1)S(1)} %collective-permute-done.10.other_ref), custom_call_target="tpu_custom_call" | custom-call | flops 805306368 | bytes 4194304 | tf_op jit(solution)/shard_map/term/pallas_call | solution.py:165
  132.5 6.0 %all-to-all-start.4 = ((bf16[8,96,1024]{2,1,0:T(8,128)(2,1)}), bf16[8,96,1024]{2,1,0:T(8,128)(2,1)S(1)}, u32[]{:S(2)}, u32[]{:S(2)}) async-start(bf16[8,96,1024]{2,1,0:T(8,128)(2,1)} %term.1), calls=%async_computation.4 | async-start | bytes 3145728 | tf_op jit(solution)/shard_map/all_to_all | solution.py:36
  138.4 1.9 %collective-permute-start.11 = (bf16[192,256]{1,0:T(8,128)(2,1)S(1)}, bf16[192,256]{1,0:T(8,128)(2,1)S(1)}, u32[]{:S(2)}, u32[]{:S(2)}) collective-permute-start(bf16[192,256]{1,0:T(8,128)(2,1)S(1)} %slice.17), channel_id=1, source_target_pairs={{0,4},{4,0},{8,12},{12,8},{16,20},{20,16},{24,28},{28,24},{32,36},... | collective-permute-start | bytes 294920 | tf_op jit(solution)/shard_map/ppermute | solution.py:57
  140.4 22.6 %all-to-all-done.4 = bf16[8,96,1024]{2,1,0:T(8,128)(2,1)S(1)} async-done(((bf16[8,96,1024]{2,1,0:T(8,128)(2,1)}), bf16[8,96,1024]{2,1,0:T(8,128)(2,1)S(1)}, u32[]{:S(2)}, u32[]{:S(2)}) %all-to-all-start.4) | async-done | bytes 1572896 | tf_op jit(solution)/shard_map/all_to_all | solution.py:36
  164.0 4.1 %all-to-all-start.5 = ((bf16[8,12,1024]{2,1,0:T(8,128)(2,1)}), bf16[8,12,1024]{2,1,0:T(8,128)(2,1)S(1)}, u32[]{:S(2)}, u32[]{:S(2)}) async-start(bf16[8,12,1024]{2,1,0:T(8,128)(2,1)} %reshape.93), calls=%async_computation.5 | async-start | bytes 524288 | tf_op jit(solution)/shard_map/all_to_all | solution.py:36
  169.3 9.2 %all-to-all-done.5 = bf16[8,12,1024]{2,1,0:T(8,128)(2,1)S(1)} async-done(((bf16[8,12,1024]{2,1,0:T(8,128)(2,1)}), bf16[8,12,1024]{2,1,0:T(8,128)(2,1)S(1)}, u32[]{:S(2)}, u32[]{:S(2)}) %all-to-all-start.5) | async-done | bytes 196640 | tf_op jit(solution)/shard_map/all_to_all | solution.py:36
  (46 shorter events, 10.1 us)
Async XLA Ops:
  0.6 42.3 %copy-start = (bf16[256,1536]{1,0:T(8,128)(2,1)S(1)}, bf16[256,1536]{1,0:T(8,128)(2,1)}, u32[]{:S(2)}) copy-start(bf16[256,1536]{1,0:T(8,128)(2,1)} %param.14) | copy-start | bytes 2359300
  2.5 14.5 %collective-permute-start = (bf16[528,128]{1,0:T(8,128)(2,1)S(1)}, bf16[528,128]{1,0:T(8,128)(2,1)S(1)}, u32[]{:S(2)}, u32[]{:S(2)}) collective-permute-start(bf16[528,128]{1,0:T(8,128)(2,1)S(1)} %maximum_maximum_fusion.b0_ref), channel_id=1, source_target_pairs={{0,8},{4,12},{8,16},{12,20},{16,24},{20,28},{24,32},{28,36},{32,40... | collective-permute-start | bytes 405512 | tf_op jit(solution)/shard_map/ppermute | solution.py:44
  6.0 11.0 %collective-permute-start.1 = (bf16[528,128]{1,0:T(8,128)(2,1)S(1)}, bf16[528,128]{1,0:T(8,128)(2,1)S(1)}, u32[]{:S(2)}, u32[]{:S(2)}) collective-permute-start(bf16[528,128]{1,0:T(8,128)(2,1)S(1)} %maximum_maximum_fusion.b0_ref), channel_id=1, source_target_pairs={{0,4},{4,8},{8,12},{12,16},{16,20},{20,24},{24,28},{28,32},{32,36}... | collective-permute-start | bytes 405512 | tf_op jit(solution)/shard_map/ppermute | solution.py:44
  9.0 17.1 %all-to-all-start = ((bf16[8,12,1024]{2,1,0:T(8,128)(2,1)}), bf16[8,12,1024]{2,1,0:T(8,128)(2,1)S(1)}, u32[]{:S(2)}, u32[]{:S(2)}) async-start(bf16[8,12,1024]{2,1,0:T(8,128)(2,1)} %broadcast_in_dim.9), calls=%async_computation | async-start | bytes 524288 | tf_op jit(solution)/shard_map/all_to_all | solution.py:36
  17.0 1.0 copy-start.1
  28.0 15.0 %copy-start.4 = (s32[256]{0:T(256)S(1)}, s32[256]{0:T(256)}, u32[]{:S(2)}) copy-start(s32[256]{0:T(256)} %param.15) | copy-start | bytes 3076
  28.0 54.7 %all-to-all-start.1 = ((bf16[128,4,1152]{2,1,0:T(4,128)(2,1)}), bf16[128,4,1152]{2,1,0:T(4,128)(2,1)}, u32[]{:S(2)}, u32[]{:S(2)}) async-start(bf16[128,4,1152]{2,1,0:T(4,128)(2,1)} %reshape.89), calls=%async_computation.1 | async-start | bytes 2359296 | tf_op jit(solution)/shard_map/all_to_all | solution.py:36
  43.3 25.9 %collective-permute-start.3 = (bf16[96,1024]{1,0:T(8,128)(2,1)S(1)}, bf16[96,1024]{1,0:T(8,128)(2,1)S(1)}, u32[]{:S(2)}, u32[]{:S(2)}) collective-permute-start(bf16[96,1024]{1,0:T(8,128)(2,1)S(1)} %reshape.88.refs_0_), channel_id=1, source_target_pairs={{0,64},{4,12},{8,72},{12,20},{16,80},{20,28},{24,88},{28,36},{32,9... | collective-permute-start | bytes 589832 | tf_op jit(solution)/shard_map/ppermute | solution.py:53
  46.3 30.9 %collective-permute-start.4 = (bf16[96,1024]{1,0:T(8,128)(2,1)S(1)}, bf16[96,1024]{1,0:T(8,128)(2,1)S(1)}, u32[]{:S(2)}, u32[]{:S(2)}) collective-permute-start(bf16[96,1024]{1,0:T(8,128)(2,1)S(1)} %reshape.88.refs_0_), channel_id=1, source_target_pairs={{0,128},{4,20},{8,136},{12,28},{16,144},{20,36},{24,152},{28,44},{... | collective-permute-start | bytes 589832 | tf_op jit(solution)/shard_map/ppermute | solution.py:53
  51.0 11.8 %collective-permute-start.2 = (bf16[192,256]{1,0:T(8,128)(2,1)S(1)}, bf16[192,256]{1,0:T(8,128)(2,1)S(1)}, u32[]{:S(2)}, u32[]{:S(2)}) collective-permute-start(bf16[192,256]{1,0:T(8,128)(2,1)S(1)} %convolution_convert_fusion.3), channel_id=1, source_target_pairs={{0,4},{4,0},{8,12},{12,8},{16,20},{20,16},{24,28},{28,24},{32,36},... | collective-permute-start | bytes 294920 | tf_op jit(solution)/shard_map/ppermute | solution.py:57
  52.9 33.1 %collective-permute-start.5 = (bf16[96,1024]{1,0:T(8,128)(2,1)S(1)}, bf16[96,1024]{1,0:T(8,128)(2,1)S(1)}, u32[]{:S(2)}, u32[]{:S(2)}) collective-permute-start(bf16[96,1024]{1,0:T(8,128)(2,1)S(1)} %reshape.88.refs_0_), channel_id=1, source_target_pairs={{0,192},{4,28},{8,200},{12,36},{16,208},{20,44},{24,216},{28,52},{... | collective-permute-start | bytes 589832 | tf_op jit(solution)/shard_map/ppermute | solution.py:53
  57.9 32.4 %collective-permute-start.6 = (bf16[96,1024]{1,0:T(8,128)(2,1)S(1)}, bf16[96,1024]{1,0:T(8,128)(2,1)S(1)}, u32[]{:S(2)}, u32[]{:S(2)}) collective-permute-start(bf16[96,1024]{1,0:T(8,128)(2,1)S(1)} %reshape.88.refs_0_), channel_id=1, source_target_pairs={{0,256},{4,36},{8,264},{12,44},{16,272},{20,52},{24,280},{28,60},{... | collective-permute-start | bytes 589832 | tf_op jit(solution)/shard_map/ppermute | solution.py:53
  62.8 27.5 %collective-permute-start.7 = (bf16[96,1024]{1,0:T(8,128)(2,1)S(1)}, bf16[96,1024]{1,0:T(8,128)(2,1)S(1)}, u32[]{:S(2)}, u32[]{:S(2)}) collective-permute-start(bf16[96,1024]{1,0:T(8,128)(2,1)S(1)} %reshape.88.refs_0_), channel_id=1, source_target_pairs={{0,320},{4,44},{8,328},{12,52},{16,336},{20,60},{24,344},{28,4},{3... | collective-permute-start | bytes 589832 | tf_op jit(solution)/shard_map/ppermute | solution.py:53
  69.2 21.1 %collective-permute-start.8 = (bf16[96,1024]{1,0:T(8,128)(2,1)S(1)}, bf16[96,1024]{1,0:T(8,128)(2,1)S(1)}, u32[]{:S(2)}, u32[]{:S(2)}) collective-permute-start(bf16[96,1024]{1,0:T(8,128)(2,1)S(1)} %reshape.88.refs_0_), channel_id=1, source_target_pairs={{0,384},{4,52},{8,392},{12,60},{16,400},{20,4},{24,408},{28,12},{3... | collective-permute-start | bytes 589832 | tf_op jit(solution)/shard_map/ppermute | solution.py:53
  77.1 13.1 %collective-permute-start.9 = (bf16[96,1024]{1,0:T(8,128)(2,1)S(1)}, bf16[96,1024]{1,0:T(8,128)(2,1)S(1)}, u32[]{:S(2)}, u32[]{:S(2)}) collective-permute-start(bf16[96,1024]{1,0:T(8,128)(2,1)S(1)} %reshape.88.refs_0_), channel_id=1, source_target_pairs={{0,448},{4,60},{8,456},{12,4},{16,464},{20,12},{24,472},{28,20},{3... | collective-permute-start | bytes 589832 | tf_op jit(solution)/shard_map/ppermute | solution.py:53
  85.1 5.2 %copy-start.2 = (bf16[512,1152]{1,0:T(8,128)(2,1)}, bf16[512,1152]{1,0:T(8,128)(2,1)S(1)}, u32[]{:S(2)}) copy-start(bf16[512,1152]{1,0:T(8,128)(2,1)S(1)} %reshape.90) | copy-start | bytes 3538948
  92.3 3.8 %collective-permute-start.10 = (bf16[256,1024]{1,0:T(8,128)(2,1)S(1)}, bf16[256,1024]{1,0:T(8,128)(2,1)S(1)}, u32[]{:S(2)}, u32[]{:S(2)}) collective-permute-start(bf16[256,1024]{1,0:T(8,128)(2,1)S(1)} %convolution_convert_fusion.1.own_ref), channel_id=1, source_target_pairs={{0,4},{4,0},{8,12},{12,8},{16,20},{20,16},{24,28},{28,24},{32,36},... | collective-permute-start | bytes 1572872 | tf_op jit(solution)/shard_map/ppermute | solution.py:57
  99.3 16.0 %copy-start.3 = (bf16[192,512]{1,0:T(8,128)(2,1)S(1)}, bf16[192,512]{1,0:T(8,128)(2,1)}, u32[]{:S(2)}) copy-start(bf16[192,512]{1,0:T(8,128)(2,1)} %pad_maximum_fusion) | copy-start | bytes 589828
  132.5 30.5 %all-to-all-start.4 = ((bf16[8,96,1024]{2,1,0:T(8,128)(2,1)}), bf16[8,96,1024]{2,1,0:T(8,128)(2,1)S(1)}, u32[]{:S(2)}, u32[]{:S(2)}) async-start(bf16[8,96,1024]{2,1,0:T(8,128)(2,1)} %term.1), calls=%async_computation.4 | async-start | bytes 3145728 | tf_op jit(solution)/shard_map/all_to_all | solution.py:36
  138.4 29.9 %collective-permute-start.11 = (bf16[192,256]{1,0:T(8,128)(2,1)S(1)}, bf16[192,256]{1,0:T(8,128)(2,1)S(1)}, u32[]{:S(2)}, u32[]{:S(2)}) collective-permute-start(bf16[192,256]{1,0:T(8,128)(2,1)S(1)} %slice.17), channel_id=1, source_target_pairs={{0,4},{4,0},{8,12},{12,8},{16,20},{20,16},{24,28},{28,24},{32,36},... | collective-permute-start | bytes 294920 | tf_op jit(solution)/shard_map/ppermute | solution.py:57
  164.0 14.6 %all-to-all-start.5 = ((bf16[8,12,1024]{2,1,0:T(8,128)(2,1)}), bf16[8,12,1024]{2,1,0:T(8,128)(2,1)S(1)}, u32[]{:S(2)}, u32[]{:S(2)}) async-start(bf16[8,12,1024]{2,1,0:T(8,128)(2,1)} %reshape.93), calls=%async_computation.5 | async-start | bytes 524288 | tf_op jit(solution)/shard_map/all_to_all | solution.py:36

commit v4 on v3

--- a/solution.py
+++ b/solution.py
@@ -29,6 +29,11 @@
 ]
 FAR = [[seq_index(z, y, 0) for z in range(SIDE)] for y in range(SIDE)] + [
     [seq_index(z, y, 1) for y in range(SIDE)] for z in range(SIDE)
+]
+
+
+SAME_CORE = [
+    [seq_index(z, y, core) for z in range(SIDE) for y in range(SIDE)] for core in range(2)
 ]
 
 
@@ -124,10 +129,37 @@
     return jnp.where(core == 0, ring * 4 + quarter, quarter * SIDE + ring)
 
 
+def place_kernel(in_ref, out_ref):
+    count = out_ref.shape[0]
+    arrived = in_ref[...].reshape(count, -1)
+    slot = arrived[:, 1024:].astype(f32)
+    row = lax.broadcasted_iota(i32, slot.shape, 0)
+    owner = lax.rem(row, 2 * GROUP_ROWS) // GROUP_ROWS
+    slot = slot + (owner * (count // 2)).astype(f32)
+    slot = jnp.concatenate([slot] * (count // 128), axis=1)
+    slot_hot = (slot == lax.broadcasted_iota(i32, slot.shape, 1).astype(f32)).astype(bf16)
+    out_ref[...] = dot(slot_hot, arrived[:, :1024], ((0,), (0,))).astype(bf16)
+
+
+def placed_rows(arrived):
+    count = arrived.shape[0] * arrived.shape[1]
+    return pl.pallas_call(
+        place_kernel,
+        out_shape=jax.ShapeDtypeStruct((count, 1024), bf16),
+        in_specs=[VMEM],
+        out_specs=VMEM,
+        compiler_params=pltpu.CompilerParams(vmem_limit_bytes=16 << 20),
+        cost_estimate=pl.CostEstimate(
+            flops=2 * count * count * 1024, bytes_accessed=3 << 20, transcendentals=0
+        ),
+        name="place",
+    )(arrived)
+
+
 def project_kernel(place_ref, own_ref, other_ref, *refs):
     blocks, out_ref = refs[:SIDE], refs[SIDE]
     core, here = place_ref[0], place_ref[1]
-    both = jnp.concatenate([own_ref[...], other_ref[...]], axis=0)
+    both = own_ref[...] + other_ref[...]
     for distance, block in enumerate(blocks):
         ring = lax.rem(here - distance + SIDE, SIDE)
         y = dot(block[...], both, ((1,), (1,))).astype(bf16)
@@ -136,13 +168,13 @@
 
 
 def project(place, own, other, blocks):
-    rows, feats = own.shape[0] * 2, own.shape[1]
+    rows, feats = own.shape
     return pl.pallas_call(
         project_kernel,
         out_shape=jax.ShapeDtypeStruct((32, 24, rows), bf16),
         in_specs=[SMEM] + [VMEM] * (2 + SIDE),
         out_specs=VMEM,
-        compiler_params=pltpu.CompilerParams(vmem_limit_bytes=24 << 20),
+        compiler_params=pltpu.CompilerParams(vmem_limit_bytes=16 << 20),
         cost_estimate=pl.CostEstimate(
             flops=2 * 768 * rows * feats, bytes_accessed=4 << 20, transcendentals=0
         ),
@@ -152,7 +184,7 @@
 
 def term_kernel(place_ref, delta_ref, own_ref, other_ref, out_ref):
     core = place_ref[0]
-    both = jnp.concatenate([own_ref[...], other_ref[...]], axis=0)
+    both = own_ref[...] + other_ref[...]
     for ring in range(SIDE):
         left = jnp.concatenate(
             [delta_ref[chunk_of(core, ring, quarter)] for quarter in range(4)], axis=0
@@ -161,7 +193,7 @@
 
 
 def term_of(place, deltas, own, other):
-    rows, feats = own.shape[0] * 2, own.shape[1]
+    rows, feats = own.shape
     return pl.pallas_call(
         term_kernel,
         out_shape=jax.ShapeDtypeStruct((SIDE, 96, feats), bf16),
@@ -202,26 +234,34 @@
     bucket_row = target_dev * GROUP_ROWS + row_ids % GROUP_ROWS
     pick = hot(jnp.arange(devices * GROUP_ROWS, dtype=i32)[:, None], bucket_row[None, :])
     slot_lanes = jnp.broadcast_to(local_slot.astype(bf16)[:, None], (rows, 128))
-    attended, near = lax.optimization_barrier((attended, near))
+    attended, near, place = lax.optimization_barrier((attended, near, place))
     wide = jnp.concatenate([attended, slot_lanes], 1)
     buckets = dot(pick, wide, ((1,), (0,))).astype(bf16)
-    buckets = buckets.reshape(devices, GROUP_ROWS, -1)
-    arrived = exchange(buckets).reshape(devices * GROUP_ROWS, -1)
-    blocks = [near]
-    for distance in range(1, SIDE):
-        blocks.append(along_ring(near, distance))
+    buckets = buckets.reshape(devices // 2, 2 * GROUP_ROWS, -1)
+    arrived = exchange(buckets, SAME_CORE)
+    blocks = [near] * SIDE
+    for step in range(1, SIDE // 2 + 1):
+        blocks[step] = along_ring(blocks[step - 1], 1)
+        if step < SIDE // 2:
+            blocks[SIDE - step] = along_ring(blocks[(SIDE - step + 1) % SIDE], -1)
+    arrived, blocks = lax.optimization_barrier((arrived, blocks))
+    own = placed_rows(arrived)
+    other = other_core(own)
+    y_split = project(place, own, other, blocks)
+    y_split, target_row = lax.optimization_barrier((y_split, target_row))
     mine, theirs = spread_of(core), spread_of(1 - core)
     student_part = lax.dynamic_slice_in_dim(student_states, tp_index * share, share, 1)
     chosen = dot(hot(target_row[:, None], row_ids[None, :]), student_part, ((1,), (0,)))
     chosen = chosen.astype(bf16)
     target_own = dot(mine, chosen, ((0,), (1,))).astype(bf16)
     target_other = other_core(dot(theirs, chosen, ((0,), (1,))).astype(bf16))
-    target = jnp.concatenate([target_own, target_other], 1)
-    arrived, target, blocks = lax.optimization_barrier((arrived, target, blocks))
-    slot_hot = hot(arrived[:, 1024:1025].astype(i32), row_ids[None, :])
-    own = dot(slot_hot, arrived[:, :1024], ((0,), (0,))).astype(bf16)
-    other = other_core(own)
-    y_split = project(place, own, other, blocks)
+    target = jnp.concatenate(
+        [
+            jnp.where(core == 0, target_own, target_other),
+            jnp.where(core == 0, target_other, target_own),
+        ],
+        1,
+    )
     y_split = y_split.reshape(shares, -1, 2 * rows)
     y_terms = exchange(y_split, axis="tp")
     y_rounded = jnp.sum(y_terms.astype(f32), axis=0).astype(bf16)
@@ -233,8 +273,9 @@
     last = exchange(far.reshape(SIDE, feats, -1), NEAR)
     norm_factor = 1.0 / math.sqrt(rows * devices)
     grad = jnp.sum(last.astype(f32), axis=0) * norm_factor
-    rest = other_core(y_rounded[:, rows:])
-    out_rows = dot(y_rounded[:, :rows], mine, ((0,), (1,)))
+    first, second = y_rounded[:, :rows], y_rounded[:, rows:]
+    rest = other_core(jnp.where(core == 0, second, first))
+    out_rows = dot(jnp.where(core == 0, first, second), mine, ((0,), (1,)))
     out_rows = (out_rows + dot(rest, theirs, ((0,), (1,)))).astype(bf16)
     return (out_rows, grad)
 

time: 180 us -> 197 us (1.094)
  waiting for transfers between devices: 43.9 us -> 70.7 us
  blocking collectives: 29.7 us -> 14.5 us
  local copies, waits for them, and re-layouts: 7.14 us -> 13.1 us
    ppermute x7, waiting for transfers between devices: 6.79 us -> 24.1 us  [along_ring(): return lax.ppermute(block, 'seq', route)]
    all_to_all x2 -> x1, blocking collectives: 29.7 us -> 14.5 us  [exchange(): lax.all_to_all(block, axis, split_axis=0, concat_axis=0, tiled=True, axis...]
    ppermute x7, starting transfers between devices: 34.6 us -> 24.1 us  [along_ring(): return lax.ppermute(block, 'seq', route)]
    unnamed x10 -> x32, local copies, waits for them, and re-layouts: 1.06 us -> 10.6 us
    all_to_all x4 -> x5, waiting for transfers between devices: 35.4 us -> 43.1 us  [exchange(): lax.all_to_all(block, axis, split_axis=0, concat_axis=0, tiled=True, axis...]
    all_to_all x4 -> x5, starting transfers between devices: 31.6 us -> 37.5 us  [exchange(): lax.all_to_all(block, axis, split_axis=0, concat_axis=0, tiled=True, axis...]
    reshape x2 -> x0, local copies, waits for them, and re-layouts: 3.55 us -> none  [the longest x1 2.37 us: on_device(): arrived = exchange(buckets).reshape(devices * GROUP_ROWS, -1)]
    ppermute x3, starting transfers between devices: 5.76 us -> 8.37 us  [other_core(): lax.ppermute(block, 'seq', [(i, i ^ 1) for i in range(lax.axis_size('seq'...]
  transfers between devices with their start and end apart: 16 -> 17, of which waited for: 8 -> 11; matrix products, arithmetic and copies ran while one was open for 5% -> 3% of each run, Pallas kernels for 3% -> 2%
where the time goes in v4:
time: 197 us; the launch traced here: 195 us
  starting transfers between devices  75.4 us (38%)
  waiting for transfers between devices  70.7 us (36%)
  blocking collectives  14.5 us (7%)
  local copies, waits for them, and re-layouts  13.1 us (7%)
  Pallas kernels  11.7 us (6%)
  other arithmetic  5.6 us (3%)
  matrix products  3.55 us (2%)
    all_to_all x5, waiting for transfers between devices, exchange(): lax.all_to_all(block, axis, split_axis=0, concat_axis=0, tiled=True, axis...  43.1 us
    all_to_all x5, starting transfers between devices, exchange(): lax.all_to_all(block, axis, split_axis=0, concat_axis=0, tiled=True, axis...  37.5 us
    ppermute x7, starting transfers between devices, along_ring(): return lax.ppermute(block, 'seq', route)  24.1 us
    ppermute x7, waiting for transfers between devices, along_ring(): return lax.ppermute(block, 'seq', route)  24.1 us
    all_to_all x1, blocking collectives, exchange(): lax.all_to_all(block, axis, split_axis=0, concat_axis=0, tiled=True, axis...  14.5 us
    unnamed x32, local copies, waits for them, and re-layouts  10.6 us
    ppermute x3, starting transfers between devices, other_core(): lax.ppermute(block, 'seq', [(i, i ^ 1) for i in range(lax.axis_size('seq'...  8.37 us
    ppermute x2, starting transfers between devices, passed_along(): return lax.ppermute(block, axis, route)  5.41 us
  transfers between devices with their start and end apart: 17, of which 11 were waited for; matrix products, arithmetic and copies ran while one was open for 3% of the time, Pallas kernels for 2%

profile of v4, /device:TPU:2, one launch (start us, length us, event | category | flops | bytes accessed | tf_op | source)
XLA Modules:
  0.0 195.5 jit_solution(13903555975376590646)
XLA Ops:
  2.5 1.7 collective-permute-start.1
  4.3 3.7 %collective-permute-start = (bf16[528,128]{1,0:T(8,128)(2,1)S(1)}, bf16[528,128]{1,0:T(8,128)(2,1)S(1)}, u32[]{:S(2)}, u32[]{:S(2)}) collective-permute-start(bf16[528,128]{1,0:T(8,128)(2,1)S(1)} %maximum_maximum_fusion.b0_ref), channel_id=1, source_target_pairs={{0,8},{4,12},{8,16},{12,20},{16,24},{20,28},{24,32},{28,36},{32,40... | collective-permute-start | bytes 405512 | tf_op jit(solution)/shard_map/ppermute | solution.py:49
  8.0 1.5 broadcast_in_dim.9
  9.4 6.2 %all-to-all-start = ((bf16[8,12,1024]{2,1,0:T(8,128)(2,1)}), bf16[8,12,1024]{2,1,0:T(8,128)(2,1)S(1)}, u32[]{:S(2)}, u32[]{:S(2)}) async-start(bf16[8,12,1024]{2,1,0:T(8,128)(2,1)} %broadcast_in_dim.9), calls=%async_computation | async-start | bytes 524288 | tf_op jit(solution)/shard_map/all_to_all | solution.py:41
  17.1 4.5 %attend.1 = bf16[256,1024]{1,0:T(8,128)(2,1)S(1)} custom-call(bf16[256,1024]{1,0:T(8,128)(2,1)S(1)} %copy-done.14, bf16[528,128]{1,0:T(8,128)(2,1)S(1)} %collective-permute-done.b2_ref, bf16[528,128]{1,0:T(8,128)(2,1)S(1)} %collective-permute-done.1.b1_ref, bf16[528,128]{1,0:T(8,128)(2,1)S(1)} %maximum_maximum_fusion.b0_ref), custom_call_target="tpu_custom_call" | custom-call | flops 805306368 | bytes 2097152 | tf_op jit(solution)/shard_map/attend/pallas_call | solution.py:102
  21.6 4.5 %all-to-all-done = bf16[8,12,1024]{2,1,0:T(8,128)(2,1)S(1)} async-done(((bf16[8,12,1024]{2,1,0:T(8,128)(2,1)}), bf16[8,12,1024]{2,1,0:T(8,128)(2,1)S(1)}, u32[]{:S(2)}, u32[]{:S(2)}) %all-to-all-start) | async-done | bytes 196640 | tf_op jit(solution)/shard_map/all_to_all | solution.py:41
  26.3 1.5 fusion
  27.8 12.2 %all-to-all-start.1 = ((bf16[64,8,1152]{2,1,0:T(8,128)(2,1)}), bf16[64,8,1152]{2,1,0:T(8,128)(2,1)S(1)}, u32[]{:S(2)}, u32[]{:S(2)}) async-start(bf16[64,8,1152]{2,1,0:T(8,128)(2,1)} %fusion), calls=%async_computation.1 | async-start | bytes 2359296 | tf_op jit(solution)/shard_map/all_to_all | solution.py:41
  40.0 3.5 %collective-permute-start.2 = (bf16[96,1024]{1,0:T(8,128)(2,1)S(1)}, bf16[96,1024]{1,0:T(8,128)(2,1)S(1)}, u32[]{:S(2)}, u32[]{:S(2)}) collective-permute-start(bf16[96,1024]{1,0:T(8,128)(2,1)S(1)} %reshape.104.refs_0_), channel_id=1, source_target_pairs={{0,64},{4,12},{8,72},{12,20},{16,80},{20,28},{24,88},{28,36},{32,9... | collective-permute-start | bytes 589832 | tf_op jit(solution)/shard_map/ppermute | solution.py:58
  43.5 3.6 %collective-permute-start.6 = (bf16[96,1024]{1,0:T(8,128)(2,1)S(1)}, bf16[96,1024]{1,0:T(8,128)(2,1)S(1)}, u32[]{:S(2)}, u32[]{:S(2)}) collective-permute-start(bf16[96,1024]{1,0:T(8,128)(2,1)S(1)} %reshape.104.refs_0_), channel_id=1, source_target_pairs={{0,448},{4,60},{8,456},{12,4},{16,464},{20,12},{24,472},{28,20},{3... | collective-permute-start | bytes 589832 | tf_op jit(solution)/shard_map/ppermute | solution.py:58
  47.1 11.6 %collective-permute-done.2.refs_1_ = bf16[96,1024]{1,0:T(8,128)(2,1)S(1)} collective-permute-done((bf16[96,1024]{1,0:T(8,128)(2,1)S(1)}, bf16[96,1024]{1,0:T(8,128)(2,1)S(1)}, u32[]{:S(2)}, u32[]{:S(2)}) %collective-permute-start.2) | collective-permute-done | bytes 196640 | tf_op jit(solution)/shard_map/ppermute | solution.py:58
  58.7 5.1 %collective-permute-start.3 = (bf16[96,1024]{1,0:T(8,128)(2,1)S(1)}, bf16[96,1024]{1,0:T(8,128)(2,1)S(1)}, u32[]{:S(2)}, u32[]{:S(2)}) collective-permute-start(bf16[96,1024]{1,0:T(8,128)(2,1)S(1)} %collective-permute-done.2.refs_1_), channel_id=1, source_target_pairs={{0,64},{4,12},{8,72},{12,20},{16,80},{20,28},{24,88},{28,36},{32,9... | collective-permute-start | bytes 589832 | tf_op jit(solution)/shard_map/ppermute | solution.py:58
  63.8 3.6 %collective-permute-done.6.refs_7_ = bf16[96,1024]{1,0:T(8,128)(2,1)S(1)} collective-permute-done((bf16[96,1024]{1,0:T(8,128)(2,1)S(1)}, bf16[96,1024]{1,0:T(8,128)(2,1)S(1)}, u32[]{:S(2)}, u32[]{:S(2)}) %collective-permute-start.6) | collective-permute-done | bytes 196640 | tf_op jit(solution)/shard_map/ppermute | solution.py:58
  67.4 3.0 %collective-permute-start.7 = (bf16[96,1024]{1,0:T(8,128)(2,1)S(1)}, bf16[96,1024]{1,0:T(8,128)(2,1)S(1)}, u32[]{:S(2)}, u32[]{:S(2)}) collective-permute-start(bf16[96,1024]{1,0:T(8,128)(2,1)S(1)} %collective-permute-done.6.refs_7_), channel_id=1, source_target_pairs={{0,448},{4,60},{8,456},{12,4},{16,464},{20,12},{24,472},{28,20},{3... | collective-permute-start | bytes 589832 | tf_op jit(solution)/shard_map/ppermute | solution.py:58
  71.1 3.1 %collective-permute-done.3.refs_2_ = bf16[96,1024]{1,0:T(8,128)(2,1)S(1)} collective-permute-done((bf16[96,1024]{1,0:T(8,128)(2,1)S(1)}, bf16[96,1024]{1,0:T(8,128)(2,1)S(1)}, u32[]{:S(2)}, u32[]{:S(2)}) %collective-permute-start.3) | collective-permute-done | bytes 196640 | tf_op jit(solution)/shard_map/ppermute | solution.py:58
  74.1 1.9 collective-permute-start.4
  76.7 5.1 %collective-permute-start.8 = (bf16[96,1024]{1,0:T(8,128)(2,1)S(1)}, bf16[96,1024]{1,0:T(8,128)(2,1)S(1)}, u32[]{:S(2)}, u32[]{:S(2)}) collective-permute-start(bf16[96,1024]{1,0:T(8,128)(2,1)S(1)} %collective-permute-done.7.refs_6_), channel_id=1, source_target_pairs={{0,448},{4,60},{8,456},{12,4},{16,464},{20,12},{24,472},{28,20},{3... | collective-permute-start | bytes 589832 | tf_op jit(solution)/shard_map/ppermute | solution.py:58
  82.9 1.9 collective-permute-start.5
  86.2 5.5 %collective-permute-done.5.refs_4_ = bf16[96,1024]{1,0:T(8,128)(2,1)S(1)} collective-permute-done((bf16[96,1024]{1,0:T(8,128)(2,1)S(1)}, bf16[96,1024]{1,0:T(8,128)(2,1)S(1)}, u32[]{:S(2)}, u32[]{:S(2)}) %collective-permute-start.5) | collective-permute-done | bytes 196640 | tf_op jit(solution)/shard_map/ppermute | solution.py:58
  93.2 3.7 %collective-permute-start.9 = (bf16[512,1024]{1,0:T(8,128)(2,1)S(1)}, bf16[512,1024]{1,0:T(8,128)(2,1)S(1)}, u32[]{:S(2)}, u32[]{:S(2)}) collective-permute-start(bf16[512,1024]{1,0:T(8,128)(2,1)S(1)} %place.1.own_ref), channel_id=1, source_target_pairs={{0,4},{4,0},{8,12},{12,8},{16,20},{20,16},{24,28},{28,24},{32,36},... | collective-permute-start | bytes 3145736 | tf_op jit(solution)/shard_map/ppermute | solution.py:62
  96.9 2.2 %collective-permute-done.9.other_ref = bf16[512,1024]{1,0:T(8,128)(2,1)S(1)} collective-permute-done((bf16[512,1024]{1,0:T(8,128)(2,1)S(1)}, bf16[512,1024]{1,0:T(8,128)(2,1)S(1)}, u32[]{:S(2)}, u32[]{:S(2)}) %collective-permute-start.9) | collective-permute-done | bytes 1048608 | tf_op jit(solution)/shard_map/ppermute | solution.py:62
  104.7 3.2 %project.1 = bf16[32,24,512]{2,1,0:T(8,128)(2,1)S(1)} custom-call(s32[2]{0:T(128)S(1)} %pad_add_fusion.place_ref, bf16[512,1024]{1,0:T(8,128)(2,1)S(1)} %place.1.own_ref, bf16[512,1024]{1,0:T(8,128)(2,1)S(1)} %collective-permute-done.9.other_ref, bf16[96,1024]{1,0:T(8,128)(2,1)S(1)} %reshape.104.refs_0_, ...), custom_call_target="tpu_custom_call" | custom-call | flops 805306368 | bytes 4194304 | tf_op jit(solution)/shard_map/project/pallas_call | solution.py:172
  108.8 5.0 %all-to-all-start.2 = ((bf16[4,192,512]{2,1,0:T(8,128)(2,1)}), bf16[4,192,512]{2,1,0:T(8,128)(2,1)}, u32[]{:S(2)}, u32[]{:S(2)}) async-start(bf16[4,192,512]{2,1,0:T(8,128)(2,1)} %bitcast.11), calls=%async_computation.2 | async-start | bytes 1572864 | tf_op jit(solution)/shard_map/all_to_all | solution.py:41
  114.3 1.9 collective-permute-start.11
  117.8 7.6 %all-to-all-done.2 = bf16[4,192,512]{2,1,0:T(8,128)(2,1)} async-done(((bf16[4,192,512]{2,1,0:T(8,128)(2,1)}), bf16[4,192,512]{2,1,0:T(8,128)(2,1)}, u32[]{:S(2)}, u32[]{:S(2)}) %all-to-all-start.2) | async-done | bytes 786464 | tf_op jit(solution)/shard_map/all_to_all | solution.py:41
  126.8 14.5 %all_to_all.30 = bf16[4,192,512]{2,1,0:T(8,128)(2,1)S(1)} all-to-all(bf16[4,192,512]{2,1,0:T(8,128)(2,1)S(1)} %broadcast_in_dim.11), channel_id=1, replica_groups=mesh['seq'=128,'tp'=4] {'tp'}, dimensions={0} | all-to-all | bytes 1572864 | tf_op jit(solution)/shard_map/all_to_all | solution.py:41
  141.3 3.2 %term.1 = bf16[8,96,1024]{2,1,0:T(8,128)(2,1)} custom-call(s32[2]{0:T(128)S(1)} %pad_add_fusion.place_ref, bf16[32,24,512]{2,1,0:T(8,128)(2,1)S(1)} %bitcast.12, bf16[512,1024]{1,0:T(8,128)(2,1)S(1)} %place.1.own_ref, bf16[512,1024]{1,0:T(8,128)(2,1)S(1)} %collective-permute-done.9.other_ref), custom_call_target="tpu_custom_call" | custom-call | flops 805306368 | bytes 4194304 | tf_op jit(solution)/shard_map/term/pallas_call | solution.py:197
  144.5 6.8 %all-to-all-start.4 = ((bf16[8,96,1024]{2,1,0:T(8,128)(2,1)}), bf16[8,96,1024]{2,1,0:T(8,128)(2,1)S(1)}, u32[]{:S(2)}, u32[]{:S(2)}) async-start(bf16[8,96,1024]{2,1,0:T(8,128)(2,1)} %term.1), calls=%async_computation.4 | async-start | bytes 3145728 | tf_op jit(solution)/shard_map/all_to_all | solution.py:41
  151.3 2.8 %collective-permute-start.10 = (bf16[192,256]{1,0:T(8,128)(2,1)S(1)}, bf16[192,256]{1,0:T(8,128)(2,1)S(1)}, u32[]{:S(2)}, u32[]{:S(2)}) collective-permute-start(bf16[192,256]{1,0:T(8,128)(2,1)S(1)} %broadcast_select_fusion.2), channel_id=1, source_target_pairs={{0,4},{4,0},{8,12},{12,8},{16,20},{20,16},{24,28},{28,24},{32,36},... | collective-permute-start | bytes 294920 | tf_op jit(solution)/shard_map/ppermute | solution.py:62
  154.1 21.7 %all-to-all-done.4 = bf16[8,96,1024]{2,1,0:T(8,128)(2,1)S(1)} async-done(((bf16[8,96,1024]{2,1,0:T(8,128)(2,1)}), bf16[8,96,1024]{2,1,0:T(8,128)(2,1)S(1)}, u32[]{:S(2)}, u32[]{:S(2)}) %all-to-all-start.4) | async-done | bytes 1572896 | tf_op jit(solution)/shard_map/all_to_all | solution.py:41
  176.9 7.4 %all-to-all-start.5 = ((bf16[8,12,1024]{2,1,0:T(8,128)(2,1)}), bf16[8,12,1024]{2,1,0:T(8,128)(2,1)S(1)}, u32[]{:S(2)}, u32[]{:S(2)}) async-start(bf16[8,12,1024]{2,1,0:T(8,128)(2,1)} %reshape.108), calls=%async_computation.5 | async-start | bytes 524288 | tf_op jit(solution)/shard_map/all_to_all | solution.py:41
  185.6 9.2 %all-to-all-done.5 = bf16[8,12,1024]{2,1,0:T(8,128)(2,1)S(1)} async-done(((bf16[8,12,1024]{2,1,0:T(8,128)(2,1)}), bf16[8,12,1024]{2,1,0:T(8,128)(2,1)S(1)}, u32[]{:S(2)}, u32[]{:S(2)}) %all-to-all-start.5) | async-done | bytes 196640 | tf_op jit(solution)/shard_map/all_to_all | solution.py:41
  (65 shorter events, 21.6 us)
Async XLA Ops:
  0.6 113.2 %copy-start = (bf16[256,1536]{1,0:T(8,128)(2,1)S(1)}, bf16[256,1536]{1,0:T(8,128)(2,1)}, u32[]{:S(2)}) copy-start(bf16[256,1536]{1,0:T(8,128)(2,1)} %param.14) | copy-start | bytes 2359300
  0.6 16.5 %copy-start.14 = (bf16[256,1024]{1,0:T(8,128)(2,1)S(1)}, bf16[256,1024]{1,0:T(8,128)(2,1)}, u32[]{:S(2)}) copy-start(bf16[256,1024]{1,0:T(8,128)(2,1)} %q_ref.1) | copy-start | bytes 1572868
  2.5 14.6 %collective-permute-start.1 = (bf16[528,128]{1,0:T(8,128)(2,1)S(1)}, bf16[528,128]{1,0:T(8,128)(2,1)S(1)}, u32[]{:S(2)}, u32[]{:S(2)}) collective-permute-start(bf16[528,128]{1,0:T(8,128)(2,1)S(1)} %maximum_maximum_fusion.b0_ref), channel_id=1, source_target_pairs={{0,4},{4,8},{8,12},{12,16},{16,20},{20,24},{24,28},{28,32},{32,36}... | collective-permute-start | bytes 405512 | tf_op jit(solution)/shard_map/ppermute | solution.py:49
  4.3 12.8 %collective-permute-start = (bf16[528,128]{1,0:T(8,128)(2,1)S(1)}, bf16[528,128]{1,0:T(8,128)(2,1)S(1)}, u32[]{:S(2)}, u32[]{:S(2)}) collective-permute-start(bf16[528,128]{1,0:T(8,128)(2,1)S(1)} %maximum_maximum_fusion.b0_ref), channel_id=1, source_target_pairs={{0,8},{4,12},{8,16},{12,20},{16,24},{20,28},{24,32},{28,36},{32,40... | collective-permute-start | bytes 405512 | tf_op jit(solution)/shard_map/ppermute | solution.py:49
  9.4 16.7 %all-to-all-start = ((bf16[8,12,1024]{2,1,0:T(8,128)(2,1)}), bf16[8,12,1024]{2,1,0:T(8,128)(2,1)S(1)}, u32[]{:S(2)}, u32[]{:S(2)}) async-start(bf16[8,12,1024]{2,1,0:T(8,128)(2,1)} %broadcast_in_dim.9), calls=%async_computation | async-start | bytes 524288 | tf_op jit(solution)/shard_map/all_to_all | solution.py:41
  27.8 64.5 %all-to-all-start.1 = ((bf16[64,8,1152]{2,1,0:T(8,128)(2,1)}), bf16[64,8,1152]{2,1,0:T(8,128)(2,1)S(1)}, u32[]{:S(2)}, u32[]{:S(2)}) async-start(bf16[64,8,1152]{2,1,0:T(8,128)(2,1)} %fusion), calls=%async_computation.1 | async-start | bytes 2359296 | tf_op jit(solution)/shard_map/all_to_all | solution.py:41
  40.0 18.6 %collective-permute-start.2 = (bf16[96,1024]{1,0:T(8,128)(2,1)S(1)}, bf16[96,1024]{1,0:T(8,128)(2,1)S(1)}, u32[]{:S(2)}, u32[]{:S(2)}) collective-permute-start(bf16[96,1024]{1,0:T(8,128)(2,1)S(1)} %reshape.104.refs_0_), channel_id=1, source_target_pairs={{0,64},{4,12},{8,72},{12,20},{16,80},{20,28},{24,88},{28,36},{32,9... | collective-permute-start | bytes 589832 | tf_op jit(solution)/shard_map/ppermute | solution.py:58
  43.5 23.9 %collective-permute-start.6 = (bf16[96,1024]{1,0:T(8,128)(2,1)S(1)}, bf16[96,1024]{1,0:T(8,128)(2,1)S(1)}, u32[]{:S(2)}, u32[]{:S(2)}) collective-permute-start(bf16[96,1024]{1,0:T(8,128)(2,1)S(1)} %reshape.104.refs_0_), channel_id=1, source_target_pairs={{0,448},{4,60},{8,456},{12,4},{16,464},{20,12},{24,472},{28,20},{3... | collective-permute-start | bytes 589832 | tf_op jit(solution)/shard_map/ppermute | solution.py:58
  58.7 15.5 %collective-permute-start.3 = (bf16[96,1024]{1,0:T(8,128)(2,1)S(1)}, bf16[96,1024]{1,0:T(8,128)(2,1)S(1)}, u32[]{:S(2)}, u32[]{:S(2)}) collective-permute-start(bf16[96,1024]{1,0:T(8,128)(2,1)S(1)} %collective-permute-done.2.refs_1_), channel_id=1, source_target_pairs={{0,64},{4,12},{8,72},{12,20},{16,80},{20,28},{24,88},{28,36},{32,9... | collective-permute-start | bytes 589832 | tf_op jit(solution)/shard_map/ppermute | solution.py:58
  67.4 9.3 %collective-permute-start.7 = (bf16[96,1024]{1,0:T(8,128)(2,1)S(1)}, bf16[96,1024]{1,0:T(8,128)(2,1)S(1)}, u32[]{:S(2)}, u32[]{:S(2)}) collective-permute-start(bf16[96,1024]{1,0:T(8,128)(2,1)S(1)} %collective-permute-done.6.refs_7_), channel_id=1, source_target_pairs={{0,448},{4,60},{8,456},{12,4},{16,464},{20,12},{24,472},{28,20},{3... | collective-permute-start | bytes 589832 | tf_op jit(solution)/shard_map/ppermute | solution.py:58
  70.4 0.7 copy-start.2
  74.1 8.8 %collective-permute-start.4 = (bf16[96,1024]{1,0:T(8,128)(2,1)S(1)}, bf16[96,1024]{1,0:T(8,128)(2,1)S(1)}, u32[]{:S(2)}, u32[]{:S(2)}) collective-permute-start(bf16[96,1024]{1,0:T(8,128)(2,1)S(1)} %collective-permute-done.3.refs_2_), channel_id=1, source_target_pairs={{0,64},{4,12},{8,72},{12,20},{16,80},{20,28},{24,88},{28,36},{32,9... | collective-permute-start | bytes 589832 | tf_op jit(solution)/shard_map/ppermute | solution.py:58
  76.1 0.7 copy-start.4
  76.7 8.8 %collective-permute-start.8 = (bf16[96,1024]{1,0:T(8,128)(2,1)S(1)}, bf16[96,1024]{1,0:T(8,128)(2,1)S(1)}, u32[]{:S(2)}, u32[]{:S(2)}) collective-permute-start(bf16[96,1024]{1,0:T(8,128)(2,1)S(1)} %collective-permute-done.7.refs_6_), channel_id=1, source_target_pairs={{0,448},{4,60},{8,456},{12,4},{16,464},{20,12},{24,472},{28,20},{3... | collective-permute-start | bytes 589832 | tf_op jit(solution)/shard_map/ppermute | solution.py:58
  82.9 8.8 %collective-permute-start.5 = (bf16[96,1024]{1,0:T(8,128)(2,1)S(1)}, bf16[96,1024]{1,0:T(8,128)(2,1)S(1)}, u32[]{:S(2)}, u32[]{:S(2)}) collective-permute-start(bf16[96,1024]{1,0:T(8,128)(2,1)S(1)} %collective-permute-done.4.refs_3_), channel_id=1, source_target_pairs={{0,64},{4,12},{8,72},{12,20},{16,80},{20,28},{24,88},{28,36},{32,9... | collective-permute-start | bytes 589832 | tf_op jit(solution)/shard_map/ppermute | solution.py:58
  84.8 0.7 copy-start.8
  85.5 0.7 copy-start.10
  91.7 0.7 copy-start.12
  93.2 5.9 %collective-permute-start.9 = (bf16[512,1024]{1,0:T(8,128)(2,1)S(1)}, bf16[512,1024]{1,0:T(8,128)(2,1)S(1)}, u32[]{:S(2)}, u32[]{:S(2)}) collective-permute-start(bf16[512,1024]{1,0:T(8,128)(2,1)S(1)} %place.1.own_ref), channel_id=1, source_target_pairs={{0,4},{4,0},{8,12},{12,8},{16,20},{20,16},{24,28},{28,24},{32,36},... | collective-permute-start | bytes 3145736 | tf_op jit(solution)/shard_map/ppermute | solution.py:62
  99.1 0.9 copy-start.3
  100.0 0.9 copy-start.5
  101.0 0.9 copy-start.7
  101.9 0.9 copy-start.9
  102.8 0.9 copy-start.11
  103.7 0.9 copy-start.13
  107.9 0.9 copy-start.1
  108.8 5.0 %copy-start.15 = (s32[256]{0:T(256)S(1)}, s32[256]{0:T(256)}, u32[]{:S(2)}) copy-start(s32[256]{0:T(256)} %param.15) | copy-start | bytes 3076
  108.8 16.6 %all-to-all-start.2 = ((bf16[4,192,512]{2,1,0:T(8,128)(2,1)}), bf16[4,192,512]{2,1,0:T(8,128)(2,1)}, u32[]{:S(2)}, u32[]{:S(2)}) async-start(bf16[4,192,512]{2,1,0:T(8,128)(2,1)} %bitcast.11), calls=%async_computation.2 | async-start | bytes 1572864 | tf_op jit(solution)/shard_map/all_to_all | solution.py:41
  114.3 3.2 %collective-permute-start.11 = (bf16[192,256]{1,0:T(8,128)(2,1)S(1)}, bf16[192,256]{1,0:T(8,128)(2,1)S(1)}, u32[]{:S(2)}, u32[]{:S(2)}) collective-permute-start(bf16[192,256]{1,0:T(8,128)(2,1)S(1)} %convolution_convert_fusion.2), channel_id=1, source_target_pairs={{0,4},{4,0},{8,12},{12,8},{16,20},{20,16},{24,28},{28,24},{32,36},... | collective-permute-start | bytes 294920 | tf_op jit(solution)/shard_map/ppermute | solution.py:62
  144.5 31.3 %all-to-all-start.4 = ((bf16[8,96,1024]{2,1,0:T(8,128)(2,1)}), bf16[8,96,1024]{2,1,0:T(8,128)(2,1)S(1)}, u32[]{:S(2)}, u32[]{:S(2)}) async-start(bf16[8,96,1024]{2,1,0:T(8,128)(2,1)} %term.1), calls=%async_computation.4 | async-start | bytes 3145728 | tf_op jit(solution)/shard_map/all_to_all | solution.py:41
  151.3 33.3 %collective-permute-start.10 = (bf16[192,256]{1,0:T(8,128)(2,1)S(1)}, bf16[192,256]{1,0:T(8,128)(2,1)S(1)}, u32[]{:S(2)}, u32[]{:S(2)}) collective-permute-start(bf16[192,256]{1,0:T(8,128)(2,1)S(1)} %broadcast_select_fusion.2), channel_id=1, source_target_pairs={{0,4},{4,0},{8,12},{12,8},{16,20},{20,16},{24,28},{28,24},{32,36},... | collective-permute-start | bytes 294920 | tf_op jit(solution)/shard_map/ppermute | solution.py:62
  176.9 17.9 %all-to-all-start.5 = ((bf16[8,12,1024]{2,1,0:T(8,128)(2,1)}), bf16[8,12,1024]{2,1,0:T(8,128)(2,1)S(1)}, u32[]{:S(2)}, u32[]{:S(2)}) async-start(bf16[8,12,1024]{2,1,0:T(8,128)(2,1)} %reshape.108), calls=%async_computation.5 | async-start | bytes 524288 | tf_op jit(solution)/shard_map/all_to_all | solution.py:41
  (1 other events, 0.7 us)

commit v5 on v4

--- a/solution.py
+++ b/solution.py
@@ -1,3 +1,4 @@
+import functools
 import math
 
 import jax
@@ -47,15 +48,6 @@
     devices = range(lax.axis_size(axis))
     route = [(i - distance, i) for i in devices if i - distance in devices]
     return lax.ppermute(block, axis, route)
-
-
-def along_ring(block, distance):
-    route = []
-    for z in range(SIDE):
-        for y in range(SIDE):
-            route.append((seq_index(z, y, 0), seq_index((z + distance) % SIDE, y, 0)))
-            route.append((seq_index(z, y, 1), seq_index(z, (y + distance) % SIDE, 1)))
-    return lax.ppermute(block, "seq", route)
 
 
 def other_core(block):
@@ -156,55 +148,80 @@
     )(arrived)
 
 
-def project_kernel(place_ref, own_ref, other_ref, *refs):
-    blocks, out_ref = refs[:SIDE], refs[SIDE]
-    core, here = place_ref[0], place_ref[1]
-    both = own_ref[...] + other_ref[...]
-    for distance, block in enumerate(blocks):
-        ring = lax.rem(here - distance + SIDE, SIDE)
-        y = dot(block[...], both, ((1,), (1,))).astype(bf16)
+def project_kernel(add, place_ref, own_ref, other_ref, proj_ref, out_ref):
+    core, share = place_ref[0], place_ref[1]
+    if add:
+        both = own_ref[...] + other_ref[...]
+    else:
+        both = jnp.concatenate([own_ref[...], other_ref[...]], axis=0)
+    for ring in range(SIDE):
+        y = dot(proj_ref[ring * 96 : ring * 96 + 96], both, ((1,), (1,))).astype(bf16)
         for quarter in range(4):
-            out_ref[chunk_of(core, ring, quarter)] = y[quarter * 24 : quarter * 24 + 24]
-
-
-def project(place, own, other, blocks):
-    rows, feats = own.shape
+            chunk = chunk_of(core, ring, quarter)
+            away = lax.rem(chunk // 8 - share + 4, 4)
+            out_ref[away, lax.rem(chunk, 8)] = y[quarter * 24 : quarter * 24 + 24]
+
+
+def project(place, own, other, half_proj, add):
+    feats = own.shape[1]
+    rows = own.shape[0] if add else 2 * own.shape[0]
     return pl.pallas_call(
-        project_kernel,
-        out_shape=jax.ShapeDtypeStruct((32, 24, rows), bf16),
-        in_specs=[SMEM] + [VMEM] * (2 + SIDE),
+        functools.partial(project_kernel, add),
+        out_shape=jax.ShapeDtypeStruct((4, 8, 24, rows), bf16),
+        in_specs=[SMEM] + [VMEM] * 3,
         out_specs=VMEM,
         compiler_params=pltpu.CompilerParams(vmem_limit_bytes=16 << 20),
         cost_estimate=pl.CostEstimate(
             flops=2 * 768 * rows * feats, bytes_accessed=4 << 20, transcendentals=0
         ),
-        name="project",
-    )(place, own, other, *blocks)
-
-
-def term_kernel(place_ref, delta_ref, own_ref, other_ref, out_ref):
-    core = place_ref[0]
-    both = own_ref[...] + other_ref[...]
+    )(place, own, other, half_proj)
+
+
+def term_kernel(place_ref, *refs):
+    parts, (target_ref, own_ref, other_ref, own_m_ref, other_m_ref, out_ref, held) = refs[:4], refs[4:]
+    core, share = place_ref[0], place_ref[1]
+    for i, part in enumerate(parts):
+        held[i] = part[...]
+    attended = jnp.concatenate([own_ref[...], other_ref[...]], axis=0)
+    moved = own_m_ref[...] + other_m_ref[...]
     for ring in range(SIDE):
-        left = jnp.concatenate(
-            [delta_ref[chunk_of(core, ring, quarter)] for quarter in range(4)], axis=0
-        )
-        out_ref[ring] = dot(left, both, ((1,), (0,))).astype(bf16)
-
-
-def term_of(place, deltas, own, other):
-    rows, feats = own.shape
+        left, right = [], []
+        for quarter in range(4):
+            chunk = chunk_of(core, ring, quarter)
+            away = lax.rem(share - chunk // 8 + 4, 4)
+            left.append(held[away, lax.rem(chunk, 8)])
+            right.append(target_ref[chunk])
+        y_part = dot(jnp.concatenate(left, axis=0), attended, ((1,), (0,)))
+        t_part = dot(jnp.concatenate(right, axis=0), moved, ((1,), (0,)))
+        out_ref[ring] = (y_part - t_part).astype(bf16)
+
+
+def term_of(place, parts, targets, own, other, own_m, other_m):
+    rows, feats = own_m.shape
     return pl.pallas_call(
         term_kernel,
         out_shape=jax.ShapeDtypeStruct((SIDE, 96, feats), bf16),
-        in_specs=[SMEM] + [VMEM] * 3,
+        in_specs=[SMEM] + [VMEM] * 9,
         out_specs=VMEM,
+        scratch_shapes=[pltpu.VMEM((4, 8, 24, rows), bf16)],
         compiler_params=pltpu.CompilerParams(vmem_limit_bytes=24 << 20),
         cost_estimate=pl.CostEstimate(
-            flops=2 * 768 * rows * feats, bytes_accessed=4 << 20, transcendentals=0
+            flops=4 * 768 * rows * feats, bytes_accessed=8 << 20, transcendentals=0
         ),
         name="term",
-    )(place, deltas, own, other)
+    )(place, *parts, targets, own, other, own_m, other_m)
+
+
+def share_route(distance):
+    return [(i, (i + distance) % 4) for i in range(4)]
+
+
+def summed_share(y_split):
+    total = y_split[0].astype(f32)
+    got = [lax.ppermute(y_split[k], "tp", share_route(k)) for k in range(1, 4)]
+    for part in got:
+        total = total + part.astype(f32)
+    return total.astype(bf16)
 
 
 def spread_of(core):
@@ -220,60 +237,58 @@
     devices = lax.axis_size("seq")
     shares = lax.axis_size("tp")
     share = SW // shares
-    index = lax.axis_index("seq")
-    core = index % 2
-    here = jnp.where(core == 0, index // (2 * SIDE), (index // 2) % SIDE)
-    place = jnp.stack([core, here]).astype(i32)
+    core = lax.axis_index("seq") % 2
     tp_index = lax.axis_index("tp")
+    place = jnp.stack([core, tp_index]).astype(i32)
     feats = proj.shape[0]
+    row_ids = jnp.arange(rows, dtype=i32)
     near = exchange(to_all(proj, SIDE), NEAR).reshape(SIDE * feats, -1)
+    queries, near, place = lax.optimization_barrier((queries, near, place))
+    half_proj = exchange(to_all(near, SIDE), FAR).reshape(SIDE * SIDE * feats, -1)
     attended = attend(queries, keys, values, segment)
+    partner = other_core(attended)
     target_dev = repack // rows
     local_slot = repack - target_dev * rows
-    row_ids = jnp.arange(rows, dtype=i32)
     bucket_row = target_dev * GROUP_ROWS + row_ids % GROUP_ROWS
     pick = hot(jnp.arange(devices * GROUP_ROWS, dtype=i32)[:, None], bucket_row[None, :])
     slot_lanes = jnp.broadcast_to(local_slot.astype(bf16)[:, None], (rows, 128))
-    attended, near, place = lax.optimization_barrier((attended, near, place))
     wide = jnp.concatenate([attended, slot_lanes], 1)
     buckets = dot(pick, wide, ((1,), (0,))).astype(bf16)
     buckets = buckets.reshape(devices // 2, 2 * GROUP_ROWS, -1)
-    arrived = exchange(buckets, SAME_CORE)
-    blocks = [near] * SIDE
-    for step in range(1, SIDE // 2 + 1):
-        blocks[step] = along_ring(blocks[step - 1], 1)
-        if step < SIDE // 2:
-            blocks[SIDE - step] = along_ring(blocks[(SIDE - step + 1) % SIDE], -1)
-    arrived, blocks = lax.optimization_barrier((arrived, blocks))
-    own = placed_rows(arrived)
-    other = other_core(own)
-    y_split = project(place, own, other, blocks)
-    y_split, target_row = lax.optimization_barrier((y_split, target_row))
     mine, theirs = spread_of(core), spread_of(1 - core)
-    student_part = lax.dynamic_slice_in_dim(student_states, tp_index * share, share, 1)
-    chosen = dot(hot(target_row[:, None], row_ids[None, :]), student_part, ((1,), (0,)))
+    chosen = dot(hot(target_row[:, None], row_ids[None, :]), student_states, ((1,), (0,)))
     chosen = chosen.astype(bf16)
-    target_own = dot(mine, chosen, ((0,), (1,))).astype(bf16)
-    target_other = other_core(dot(theirs, chosen, ((0,), (1,))).astype(bf16))
-    target = jnp.concatenate(
+    chosen = [chosen[:, i * share : (i + 1) * share] for i in range(shares)]
+    target_own = jnp.concatenate([dot(mine, c, ((0,), (1,))) for c in chosen], 0).astype(bf16)
+    target_other = jnp.concatenate([dot(theirs, c, ((0,), (1,))) for c in chosen], 0)
+    target_other = other_core(target_other.astype(bf16))
+    targets = jnp.concatenate(
         [
             jnp.where(core == 0, target_own, target_other),
             jnp.where(core == 0, target_other, target_own),
         ],
         1,
     )
-    y_split = y_split.reshape(shares, -1, 2 * rows)
-    y_terms = exchange(y_split, axis="tp")
-    y_rounded = jnp.sum(y_terms.astype(f32), axis=0).astype(bf16)
-    delta = (y_rounded.astype(f32) - target.astype(f32)).astype(bf16)
-    deltas = exchange(to_all(delta, shares), axis="tp")
-    term = term_of(place, deltas.reshape(32, 24, 2 * rows), own, other)
+    buckets, half_proj, targets = lax.optimization_barrier((buckets, half_proj, targets))
+    arrived = exchange(buckets, SAME_CORE)
+    y_split = project(place, attended, partner, half_proj, False)
+    y_teacher = summed_share(y_split)
+    parts = [y_teacher]
+    for distance in range(1, shares):
+        parts.append(lax.ppermute(y_teacher, "tp", share_route(distance)))
+    arrived, parts[1] = lax.optimization_barrier((arrived, parts[1]))
+    own = placed_rows(arrived)
+    other = other_core(own)
+    term = term_of(place, parts, targets.reshape(32, 24, 2 * rows), attended, partner, own, other)
+    term, own = lax.optimization_barrier((term, own))
     far = exchange(term, FAR)
     far = jnp.sum(far.astype(f32), axis=0).astype(bf16)
     last = exchange(far.reshape(SIDE, feats, -1), NEAR)
     norm_factor = 1.0 / math.sqrt(rows * devices)
     grad = jnp.sum(last.astype(f32), axis=0) * norm_factor
-    first, second = y_rounded[:, :rows], y_rounded[:, rows:]
+    y_split = project(place, own, other, half_proj, True)
+    y_rows = summed_share(y_split).reshape(-1, 2 * rows)
+    first, second = y_rows[:, :rows], y_rows[:, rows:]
     rest = other_core(jnp.where(core == 0, second, first))
     out_rows = dot(jnp.where(core == 0, first, second), mine, ((0,), (1,)))
     out_rows = (out_rows + dot(rest, theirs, ((0,), (1,)))).astype(bf16)

time: 197 us -> 181 us (0.919)
  the two profiles are of different devices: /device:TPU:2 before, /device:TPU:6 now
where the time goes in v5:
time: 181 us; the launch traced here: 180 us
  starting transfers between devices  76.7 us (42%)
  waiting for transfers between devices  54.7 us (30%)
  Pallas kernels  16.4 us (9%)
  local copies, waits for them, and re-layouts  13 us (7%)
  other arithmetic  9.65 us (5%)
  matrix products  8.5 us (5%)
    all_to_all x5, starting transfers between devices, exchange(): lax.all_to_all(block, axis, split_axis=0, concat_axis=0, tiled=True, axis...  35.5 us
    all_to_all x5, waiting for transfers between devices, exchange(): lax.all_to_all(block, axis, split_axis=0, concat_axis=0, tiled=True, axis...  26.4 us
    ppermute x6, starting transfers between devices, summed_share(): got = [lax.ppermute(y_split[k], 'tp', share_route(k)) for k in range(1, 4)]  17.9 us
    ppermute x6, waiting for transfers between devices, summed_share(): got = [lax.ppermute(y_split[k], 'tp', share_route(k)) for k in range(1, 4)]  14.1 us
    ppermute x3, waiting for transfers between devices, on_device(): parts.append(lax.ppermute(y_teacher, 'tp', share_route(distance)))  12.2 us
    ppermute x3, starting transfers between devices, on_device(): parts.append(lax.ppermute(y_teacher, 'tp', share_route(distance)))  10.3 us
    unnamed x36, local copies, waits for them, and re-layouts  9.05 us
    dot_general x12, matrix products, dot(): return lax.dot_general(a, b, (dims, ((), ())), preferred_element_type=f32)  8.5 us
  transfers between devices with their start and end apart: 20, of which 10 were waited for; matrix products, arithmetic and copies ran while one was open for 11% of the time, Pallas kernels for 6%

profile of v5, /device:TPU:6, one launch (start us, length us, event | category | flops | bytes accessed | tf_op | source)
XLA Modules:
  0.0 179.9 jit_solution(15863341477411522293)
XLA Ops:
  4.2 3.7 %collective-permute-start = (bf16[528,128]{1,0:T(8,128)(2,1)S(1)}, bf16[528,128]{1,0:T(8,128)(2,1)S(1)}, u32[]{:S(2)}, u32[]{:S(2)}) collective-permute-start(bf16[528,128]{1,0:T(8,128)(2,1)S(1)} %maximum_maximum_fusion.b0_ref), channel_id=1, source_target_pairs={{0,8},{4,12},{8,16},{12,20},{16,24},{20,28},{24,32},{28,36},{32,40... | collective-permute-start | bytes 405512 | tf_op jit(solution)/shard_map/ppermute | solution.py:50
  9.4 6.2 %all-to-all-start = ((bf16[8,12,1024]{2,1,0:T(8,128)(2,1)}), bf16[8,12,1024]{2,1,0:T(8,128)(2,1)S(1)}, u32[]{:S(2)}, u32[]{:S(2)}) async-start(bf16[8,12,1024]{2,1,0:T(8,128)(2,1)} %broadcast_in_dim.8), calls=%async_computation | async-start | bytes 524288 | tf_op jit(solution)/shard_map/all_to_all | solution.py:42
  17.7 8.4 %all-to-all-done = bf16[8,12,1024]{2,1,0:T(8,128)(2,1)S(1)} async-done(((bf16[8,12,1024]{2,1,0:T(8,128)(2,1)}), bf16[8,12,1024]{2,1,0:T(8,128)(2,1)S(1)}, u32[]{:S(2)}, u32[]{:S(2)}) %all-to-all-start) | async-done | bytes 196640 | tf_op jit(solution)/shard_map/all_to_all | solution.py:42
  27.5 10.3 %all-to-all-start.1 = ((bf16[8,96,1024]{2,1,0:T(8,128)(2,1)}), bf16[8,96,1024]{2,1,0:T(8,128)(2,1)S(1)}, u32[]{:S(2)}, u32[]{:S(2)}) async-start(bf16[8,96,1024]{2,1,0:T(8,128)(2,1)} %broadcast_in_dim.11), calls=%async_computation.1 | async-start | bytes 3145728 | tf_op jit(solution)/shard_map/all_to_all | solution.py:42
  47.7 4.4 %attend.1.own_ref.refs_5_ = bf16[256,1024]{1,0:T(8,128)(2,1)S(1)} custom-call(bf16[256,1024]{1,0:T(8,128)(2,1)S(1)} %copy-done.13, bf16[528,128]{1,0:T(8,128)(2,1)S(1)} %collective-permute-done.b2_ref, bf16[528,128]{1,0:T(8,128)(2,1)S(1)} %collective-permute-done.1.b1_ref, bf16[528,128]{1,0:T(8,128)(2,1)S(1)} %maximum_maximum_fusion.b0_ref), custom_call_target="tpu_custom_call" | custom-call | flops 805306368 | bytes 2097152 | tf_op jit(solution)/shard_map/attend/pallas_call | solution.py:94
  55.9 6.4 %all-to-all-done.1 = bf16[8,96,1024]{2,1,0:T(8,128)(2,1)S(1)} async-done(((bf16[8,96,1024]{2,1,0:T(8,128)(2,1)}), bf16[8,96,1024]{2,1,0:T(8,128)(2,1)S(1)}, u32[]{:S(2)}, u32[]{:S(2)}) %all-to-all-start.1) | async-done | bytes 1572896 | tf_op jit(solution)/shard_map/all_to_all | solution.py:42
  62.4 5.5 %all-to-all-start.2 = ((bf16[64,8,1152]{2,1,0:T(8,128)(2,1)}), bf16[64,8,1152]{2,1,0:T(8,128)(2,1)}, u32[]{:S(2)}, u32[]{:S(2)}) async-start(bf16[64,8,1152]{2,1,0:T(8,128)(2,1)} %fusion), calls=%async_computation.2 | async-start | bytes 2359296 | tf_op jit(solution)/shard_map/all_to_all | solution.py:42
  67.9 1.9 %collective-permute-start.2 = (bf16[256,1024]{1,0:T(8,128)(2,1)S(1)}, bf16[256,1024]{1,0:T(8,128)(2,1)S(1)}, u32[]{:S(2)}, u32[]{:S(2)}) collective-permute-start(bf16[256,1024]{1,0:T(8,128)(2,1)S(1)} %attend.1.own_ref.refs_5_), channel_id=1, source_target_pairs={{0,4},{4,0},{8,12},{12,8},{16,20},{20,16},{24,28},{28,24},{32,36},... | collective-permute-start | bytes 1572872 | tf_op jit(solution)/shard_map/ppermute | solution.py:54
  71.7 3.2 %shard_map.95 = bf16[4,8,24,512]{3,2,1,0:T(8,128)(2,1)S(1)} custom-call(s32[2]{0:T(128)S(1)} %pad_add_fusion.place_ref, bf16[256,1024]{1,0:T(8,128)(2,1)S(1)} %attend.1.own_ref.refs_5_, bf16[256,1024]{1,0:T(8,128)(2,1)S(1)} %collective-permute-done.2.other_ref.refs_6_, bf16[768,1024]{1,0:T(8,128)(2,1)S(1)} %bitcast.33), custom_call_target="tpu_custom_call" | custom-call | flops 805306368 | bytes 4194304 | tf_op jit(solution)/shard_map/pallas_call | solution.py:168
  75.0 2.4 %collective-permute-start.4 = (bf16[8,24,512]{2,1,0:T(8,128)(2,1)S(1)}, bf16[8,24,512]{2,1,0:T(8,128)(2,1)S(1)}, u32[]{:S(2)}, u32[]{:S(2)}) collective-permute-start(bf16[8,24,512]{2,1,0:T(8,128)(2,1)S(1)} %get-tuple-element.27), channel_id=1, source_target_pairs={{0,1},{1,2},{2,3},{3,0},{4,5},{5,6},{6,7},{7,4},{8,9},{9,10},{10,1... | collective-permute-start | bytes 589832 | tf_op jit(solution)/shard_map/ppermute | solution.py:221
  77.3 3.5 %collective-permute-start.6 = (bf16[8,24,512]{2,1,0:T(8,128)(2,1)S(1)}, bf16[8,24,512]{2,1,0:T(8,128)(2,1)S(1)}, u32[]{:S(2)}, u32[]{:S(2)}) collective-permute-start(bf16[8,24,512]{2,1,0:T(8,128)(2,1)S(1)} %get-tuple-element.28), channel_id=1, source_target_pairs={{0,3},{1,0},{2,1},{3,2},{4,7},{5,4},{6,5},{7,6},{8,11},{9,8},{10,9... | collective-permute-start | bytes 589832 | tf_op jit(solution)/shard_map/ppermute | solution.py:221
  80.8 3.3 %collective-permute-start.5 = (bf16[8,24,512]{2,1,0:T(8,128)(2,1)S(1)}, bf16[8,24,512]{2,1,0:T(8,128)(2,1)S(1)}, u32[]{:S(2)}, u32[]{:S(2)}) collective-permute-start(bf16[8,24,512]{2,1,0:T(8,128)(2,1)S(1)} %get-tuple-element.29), channel_id=1, source_target_pairs={{0,2},{1,3},{2,0},{3,1},{4,6},{5,7},{6,4},{7,5},{8,10},{9,11},{10,... | collective-permute-start | bytes 589832 | tf_op jit(solution)/shard_map/ppermute | solution.py:221
  84.1 7.2 %collective-permute-done.6 = bf16[8,24,512]{2,1,0:T(8,128)(2,1)S(1)} collective-permute-done((bf16[8,24,512]{2,1,0:T(8,128)(2,1)S(1)}, bf16[8,24,512]{2,1,0:T(8,128)(2,1)S(1)}, u32[]{:S(2)}, u32[]{:S(2)}) %collective-permute-start.6) | collective-permute-done | bytes 196640 | tf_op jit(solution)/shard_map/ppermute | solution.py:221
  92.1 2.8 %collective-permute-start.7 = (bf16[8,24,512]{2,1,0:T(8,128)(2,1)S(1)}, bf16[8,24,512]{2,1,0:T(8,128)(2,1)S(1)}, u32[]{:S(2)}, u32[]{:S(2)}) collective-permute-start(bf16[8,24,512]{2,1,0:T(8,128)(2,1)S(1)} %fusion.10.refs_0_), channel_id=1, source_target_pairs={{0,1},{1,2},{2,3},{3,0},{4,5},{5,6},{6,7},{7,4},{8,9},{9,10},{10,1... | collective-permute-start | bytes 589832 | tf_op jit(solution)/shard_map/ppermute | solution.py:278
  95.0 4.9 %collective-permute-done.7.refs_1_ = bf16[8,24,512]{2,1,0:T(8,128)(2,1)S(1)} collective-permute-done((bf16[8,24,512]{2,1,0:T(8,128)(2,1)S(1)}, bf16[8,24,512]{2,1,0:T(8,128)(2,1)S(1)}, u32[]{:S(2)}, u32[]{:S(2)}) %collective-permute-start.7) | collective-permute-done | bytes 196640 | tf_op jit(solution)/shard_map/ppermute | solution.py:278
  100.5 2.1 %place.1.refs_7_.own_ref = bf16[512,1024]{1,0:T(8,128)(2,1)S(1)} custom-call(bf16[64,8,1152]{2,1,0:T(8,128)(2,1)} %all-to-all-done.2.in_ref), custom_call_target="tpu_custom_call" | custom-call | flops 536870912 | bytes 3145728 | tf_op jit(solution)/shard_map/place/pallas_call | solution.py:138
  102.7 1.9 %collective-permute-start.10 = (bf16[512,1024]{1,0:T(8,128)(2,1)S(1)}, bf16[512,1024]{1,0:T(8,128)(2,1)S(1)}, u32[]{:S(2)}, u32[]{:S(2)}) collective-permute-start(bf16[512,1024]{1,0:T(8,128)(2,1)S(1)} %place.1.refs_7_.own_ref), channel_id=1, source_target_pairs={{0,4},{4,0},{8,12},{12,8},{16,20},{20,16},{24,28},{28,24},{32,36},... | collective-permute-start | bytes 3145736 | tf_op jit(solution)/shard_map/ppermute | solution.py:54
  104.6 2.0 %collective-permute-start.9 = (bf16[8,24,512]{2,1,0:T(8,128)(2,1)S(1)}, bf16[8,24,512]{2,1,0:T(8,128)(2,1)S(1)}, u32[]{:S(2)}, u32[]{:S(2)}) collective-permute-start(bf16[8,24,512]{2,1,0:T(8,128)(2,1)S(1)} %copy-done.10), channel_id=1, source_target_pairs={{0,3},{1,0},{2,1},{3,2},{4,7},{5,4},{6,5},{7,6},{8,11},{9,8},{10,9... | collective-permute-start | bytes 589832 | tf_op jit(solution)/shard_map/ppermute | solution.py:278
  106.7 5.4 %collective-permute-start.8 = (bf16[8,24,512]{2,1,0:T(8,128)(2,1)S(1)}, bf16[8,24,512]{2,1,0:T(8,128)(2,1)S(1)}, u32[]{:S(2)}, u32[]{:S(2)}) collective-permute-start(bf16[8,24,512]{2,1,0:T(8,128)(2,1)S(1)} %copy-done.10), channel_id=1, source_target_pairs={{0,2},{1,3},{2,0},{3,1},{4,6},{5,7},{6,4},{7,5},{8,10},{9,11},{10,... | collective-permute-start | bytes 589832 | tf_op jit(solution)/shard_map/ppermute | solution.py:278
  112.1 3.2 %collective-permute-done.9.refs_3_ = bf16[8,24,512]{2,1,0:T(8,128)(2,1)S(1)} collective-permute-done((bf16[8,24,512]{2,1,0:T(8,128)(2,1)S(1)}, bf16[8,24,512]{2,1,0:T(8,128)(2,1)S(1)}, u32[]{:S(2)}, u32[]{:S(2)}) %collective-permute-start.9) | collective-permute-done | bytes 196640 | tf_op jit(solution)/shard_map/ppermute | solution.py:278
  115.3 4.2 %collective-permute-done.8.refs_2_ = bf16[8,24,512]{2,1,0:T(8,128)(2,1)S(1)} collective-permute-done((bf16[8,24,512]{2,1,0:T(8,128)(2,1)S(1)}, bf16[8,24,512]{2,1,0:T(8,128)(2,1)S(1)}, u32[]{:S(2)}, u32[]{:S(2)}) %collective-permute-start.8) | collective-permute-done | bytes 196640 | tf_op jit(solution)/shard_map/ppermute | solution.py:278
  122.7 3.4 %term.1 = bf16[8,96,1024]{2,1,0:T(8,128)(2,1)S(1)} custom-call(s32[2]{0:T(128)S(1)} %pad_add_fusion.place_ref, bf16[8,24,512]{2,1,0:T(8,128)(2,1)S(1)} %copy-done.10, bf16[8,24,512]{2,1,0:T(8,128)(2,1)S(1)} %copy-done.12, bf16[8,24,512]{2,1,0:T(8,128)(2,1)S(1)} %collective-permute-done.8.refs_2_, bf16[8,24,512]{2,1,0:T(8,128)(2,1)S(1)} %collective-permute-done.9.refs_3_, ...), custom_call_target="tpu_custom_call" | custom-call | flops 1610612736 | bytes 8388608 | tf_op jit(solution)/shard_map/term/pallas_call | solution.py:201
  128.2 6.8 %all-to-all-start.3 = ((bf16[8,96,1024]{2,1,0:T(8,128)(2,1)}), bf16[8,96,1024]{2,1,0:T(8,128)(2,1)}, u32[]{:S(2)}, u32[]{:S(2)}) async-start(bf16[8,96,1024]{2,1,0:T(8,128)(2,1)} %copy-done.1), calls=%async_computation.3 | async-start | bytes 3145728 | tf_op jit(solution)/shard_map/all_to_all | solution.py:42
  136.3 3.2 %shard_map.96 = bf16[4,8,24,512]{3,2,1,0:T(8,128)(2,1)S(1)} custom-call(s32[2]{0:T(128)S(1)} %pad_add_fusion.place_ref, bf16[512,1024]{1,0:T(8,128)(2,1)S(1)} %place.1.refs_7_.own_ref, bf16[512,1024]{1,0:T(8,128)(2,1)S(1)} %copy-done.5, bf16[768,1024]{1,0:T(8,128)(2,1)S(1)} %bitcast.34), custom_call_target="tpu_custom_call" | custom-call | flops 805306368 | bytes 4194304 | tf_op jit(solution)/shard_map/pallas_call | solution.py:168
  139.5 2.6 %collective-permute-start.11 = (bf16[8,24,512]{2,1,0:T(8,128)(2,1)S(1)}, bf16[8,24,512]{2,1,0:T(8,128)(2,1)S(1)}, u32[]{:S(2)}, u32[]{:S(2)}) collective-permute-start(bf16[8,24,512]{2,1,0:T(8,128)(2,1)S(1)} %get-tuple-element.24), channel_id=1, source_target_pairs={{0,1},{1,2},{2,3},{3,0},{4,5},{5,6},{6,7},{7,4},{8,9},{9,10},{10,1... | collective-permute-start | bytes 589832 | tf_op jit(solution)/shard_map/ppermute | solution.py:221
  142.2 3.2 %collective-permute-start.13 = (bf16[8,24,512]{2,1,0:T(8,128)(2,1)S(1)}, bf16[8,24,512]{2,1,0:T(8,128)(2,1)S(1)}, u32[]{:S(2)}, u32[]{:S(2)}) collective-permute-start(bf16[8,24,512]{2,1,0:T(8,128)(2,1)S(1)} %get-tuple-element.25), channel_id=1, source_target_pairs={{0,3},{1,0},{2,1},{3,2},{4,7},{5,4},{6,5},{7,6},{8,11},{9,8},{10,9... | collective-permute-start | bytes 589832 | tf_op jit(solution)/shard_map/ppermute | solution.py:221
  145.4 2.9 %collective-permute-start.12 = (bf16[8,24,512]{2,1,0:T(8,128)(2,1)S(1)}, bf16[8,24,512]{2,1,0:T(8,128)(2,1)S(1)}, u32[]{:S(2)}, u32[]{:S(2)}) collective-permute-start(bf16[8,24,512]{2,1,0:T(8,128)(2,1)S(1)} %get-tuple-element.26), channel_id=1, source_target_pairs={{0,2},{1,3},{2,0},{3,1},{4,6},{5,7},{6,4},{7,5},{8,10},{9,11},{10,... | collective-permute-start | bytes 589832 | tf_op jit(solution)/shard_map/ppermute | solution.py:221
  148.3 6.9 %collective-permute-done.13 = bf16[8,24,512]{2,1,0:T(8,128)(2,1)S(1)} collective-permute-done((bf16[8,24,512]{2,1,0:T(8,128)(2,1)S(1)}, bf16[8,24,512]{2,1,0:T(8,128)(2,1)S(1)}, u32[]{:S(2)}, u32[]{:S(2)}) %collective-permute-start.13) | collective-permute-done | bytes 196640 | tf_op jit(solution)/shard_map/ppermute | solution.py:221
  155.3 1.9 %collective-permute-start.14 = (bf16[192,256]{1,0:T(8,128)(2,1)S(1)}, bf16[192,256]{1,0:T(8,128)(2,1)S(1)}, u32[]{:S(2)}, u32[]{:S(2)}) collective-permute-start(bf16[192,256]{1,0:T(8,128)(2,1)S(1)} %broadcast_select_fusion.2), channel_id=1, source_target_pairs={{0,4},{4,0},{8,12},{12,8},{16,20},{20,16},{24,28},{28,24},{32,36},... | collective-permute-start | bytes 294920 | tf_op jit(solution)/shard_map/ppermute | solution.py:54
  157.3 2.4 %all-to-all-done.3 = bf16[8,96,1024]{2,1,0:T(8,128)(2,1)} async-done(((bf16[8,96,1024]{2,1,0:T(8,128)(2,1)}), bf16[8,96,1024]{2,1,0:T(8,128)(2,1)}, u32[]{:S(2)}, u32[]{:S(2)}) %all-to-all-start.3) | async-done | bytes 1572896 | tf_op jit(solution)/shard_map/all_to_all | solution.py:42
  162.1 6.7 %all-to-all-start.4 = ((bf16[8,12,1024]{2,1,0:T(8,128)(2,1)}), bf16[8,12,1024]{2,1,0:T(8,128)(2,1)S(1)}, u32[]{:S(2)}, u32[]{:S(2)}) async-start(bf16[8,12,1024]{2,1,0:T(8,128)(2,1)} %reshape.97), calls=%async_computation.4 | async-start | bytes 524288 | tf_op jit(solution)/shard_map/all_to_all | solution.py:42
  170.0 9.2 %all-to-all-done.4 = bf16[8,12,1024]{2,1,0:T(8,128)(2,1)S(1)} async-done(((bf16[8,12,1024]{2,1,0:T(8,128)(2,1)}), bf16[8,12,1024]{2,1,0:T(8,128)(2,1)S(1)}, u32[]{:S(2)}, u32[]{:S(2)}) %all-to-all-start.4) | async-done | bytes 196640 | tf_op jit(solution)/shard_map/all_to_all | solution.py:42
  (86 shorter events, 36.7 us)
Async XLA Ops:
  0.6 15.0 %copy-start = (bf16[256,1536]{1,0:T(8,128)(2,1)S(1)}, bf16[256,1536]{1,0:T(8,128)(2,1)}, u32[]{:S(2)}) copy-start(bf16[256,1536]{1,0:T(8,128)(2,1)} %param.14) | copy-start | bytes 2359300
  2.5 44.1 %collective-permute-start.1 = (bf16[528,128]{1,0:T(8,128)(2,1)S(1)}, bf16[528,128]{1,0:T(8,128)(2,1)S(1)}, u32[]{:S(2)}, u32[]{:S(2)}) collective-permute-start(bf16[528,128]{1,0:T(8,128)(2,1)S(1)} %maximum_maximum_fusion.b0_ref), channel_id=1, source_target_pairs={{0,4},{4,8},{8,12},{12,16},{16,20},{20,24},{24,28},{28,32},{32,36}... | collective-permute-start | bytes 405512 | tf_op jit(solution)/shard_map/ppermute | solution.py:50
  4.2 42.4 %collective-permute-start = (bf16[528,128]{1,0:T(8,128)(2,1)S(1)}, bf16[528,128]{1,0:T(8,128)(2,1)S(1)}, u32[]{:S(2)}, u32[]{:S(2)}) collective-permute-start(bf16[528,128]{1,0:T(8,128)(2,1)S(1)} %maximum_maximum_fusion.b0_ref), channel_id=1, source_target_pairs={{0,8},{4,12},{8,16},{12,20},{16,24},{20,28},{24,32},{28,36},{32,40... | collective-permute-start | bytes 405512 | tf_op jit(solution)/shard_map/ppermute | solution.py:50
  9.4 16.7 %all-to-all-start = ((bf16[8,12,1024]{2,1,0:T(8,128)(2,1)}), bf16[8,12,1024]{2,1,0:T(8,128)(2,1)S(1)}, u32[]{:S(2)}, u32[]{:S(2)}) async-start(bf16[8,12,1024]{2,1,0:T(8,128)(2,1)} %broadcast_in_dim.8), calls=%async_computation | async-start | bytes 524288 | tf_op jit(solution)/shard_map/all_to_all | solution.py:42
  27.5 34.8 %all-to-all-start.1 = ((bf16[8,96,1024]{2,1,0:T(8,128)(2,1)}), bf16[8,96,1024]{2,1,0:T(8,128)(2,1)S(1)}, u32[]{:S(2)}, u32[]{:S(2)}) async-start(bf16[8,96,1024]{2,1,0:T(8,128)(2,1)} %broadcast_in_dim.11), calls=%async_computation.1 | async-start | bytes 3145728 | tf_op jit(solution)/shard_map/all_to_all | solution.py:42
  42.3 11.5 %collective-permute-start.3 = (bf16[768,256]{1,0:T(8,128)(2,1)}, bf16[768,256]{1,0:T(8,128)(2,1)}, u32[]{:S(2)}, u32[]{:S(2)}) collective-permute-start(bf16[768,256]{1,0:T(8,128)(2,1)} %pad_maximum_fusion.2), channel_id=1, source_target_pairs={{0,4},{4,0},{8,12},{12,8},{16,20},{20,16},{24,28},{28,24},{32,36},... | collective-permute-start | bytes 1179656 | tf_op jit(solution)/shard_map/ppermute | solution.py:54
  44.2 2.4 %copy-start.16 = (s32[192]{0:T(256)}, s32[192]{0:T(256)S(1)}, u32[]{:S(2)}) copy-start(s32[192]{0:T(256)S(1)} %add_add_fusion.1) | copy-start | bytes 2308
  46.7 1.0 copy-start.13
  52.2 19.5 %copy-start.2 = (bf16[256,1024]{1,0:T(8,128)(2,1)}, bf16[256,1024]{1,0:T(8,128)(2,1)S(1)}, u32[]{:S(2)}) copy-start(bf16[256,1024]{1,0:T(8,128)(2,1)S(1)} %attend.1.own_ref.refs_5_) | copy-start | bytes 1572868
  62.4 38.2 %all-to-all-start.2 = ((bf16[64,8,1152]{2,1,0:T(8,128)(2,1)}), bf16[64,8,1152]{2,1,0:T(8,128)(2,1)}, u32[]{:S(2)}, u32[]{:S(2)}) async-start(bf16[64,8,1152]{2,1,0:T(8,128)(2,1)} %fusion), calls=%async_computation.2 | async-start | bytes 2359296 | tf_op jit(solution)/shard_map/all_to_all | solution.py:42
  67.9 3.8 %collective-permute-start.2 = (bf16[256,1024]{1,0:T(8,128)(2,1)S(1)}, bf16[256,1024]{1,0:T(8,128)(2,1)S(1)}, u32[]{:S(2)}, u32[]{:S(2)}) collective-permute-start(bf16[256,1024]{1,0:T(8,128)(2,1)S(1)} %attend.1.own_ref.refs_5_), channel_id=1, source_target_pairs={{0,4},{4,0},{8,12},{12,8},{16,20},{20,16},{24,28},{28,24},{32,36},... | collective-permute-start | bytes 1572872 | tf_op jit(solution)/shard_map/ppermute | solution.py:54
  71.7 3.2 %copy-start.7 = (bf16[256,1024]{1,0:T(8,128)(2,1)}, bf16[256,1024]{1,0:T(8,128)(2,1)S(1)}, u32[]{:S(2)}) copy-start(bf16[256,1024]{1,0:T(8,128)(2,1)S(1)} %collective-permute-done.2.other_ref.refs_6_) | copy-start | bytes 1572868
  75.0 9.2 %collective-permute-start.4 = (bf16[8,24,512]{2,1,0:T(8,128)(2,1)S(1)}, bf16[8,24,512]{2,1,0:T(8,128)(2,1)S(1)}, u32[]{:S(2)}, u32[]{:S(2)}) collective-permute-start(bf16[8,24,512]{2,1,0:T(8,128)(2,1)S(1)} %get-tuple-element.27), channel_id=1, source_target_pairs={{0,1},{1,2},{2,3},{3,0},{4,5},{5,6},{6,7},{7,4},{8,9},{9,10},{10,1... | collective-permute-start | bytes 589832 | tf_op jit(solution)/shard_map/ppermute | solution.py:221
  77.3 14.0 %collective-permute-start.6 = (bf16[8,24,512]{2,1,0:T(8,128)(2,1)S(1)}, bf16[8,24,512]{2,1,0:T(8,128)(2,1)S(1)}, u32[]{:S(2)}, u32[]{:S(2)}) collective-permute-start(bf16[8,24,512]{2,1,0:T(8,128)(2,1)S(1)} %get-tuple-element.28), channel_id=1, source_target_pairs={{0,3},{1,0},{2,1},{3,2},{4,7},{5,4},{6,5},{7,6},{8,11},{9,8},{10,9... | collective-permute-start | bytes 589832 | tf_op jit(solution)/shard_map/ppermute | solution.py:221
  80.8 10.5 %collective-permute-start.5 = (bf16[8,24,512]{2,1,0:T(8,128)(2,1)S(1)}, bf16[8,24,512]{2,1,0:T(8,128)(2,1)S(1)}, u32[]{:S(2)}, u32[]{:S(2)}) collective-permute-start(bf16[8,24,512]{2,1,0:T(8,128)(2,1)S(1)} %get-tuple-element.29), channel_id=1, source_target_pairs={{0,2},{1,3},{2,0},{3,1},{4,6},{5,7},{6,4},{7,5},{8,10},{9,11},{10,... | collective-permute-start | bytes 589832 | tf_op jit(solution)/shard_map/ppermute | solution.py:221
  92.1 7.7 %collective-permute-start.7 = (bf16[8,24,512]{2,1,0:T(8,128)(2,1)S(1)}, bf16[8,24,512]{2,1,0:T(8,128)(2,1)S(1)}, u32[]{:S(2)}, u32[]{:S(2)}) collective-permute-start(bf16[8,24,512]{2,1,0:T(8,128)(2,1)S(1)} %fusion.10.refs_0_), channel_id=1, source_target_pairs={{0,1},{1,2},{2,3},{3,0},{4,5},{5,6},{6,7},{7,4},{8,9},{9,10},{10,1... | collective-permute-start | bytes 589832 | tf_op jit(solution)/shard_map/ppermute | solution.py:278
  100.5 4.1 %copy-start.10 = (bf16[8,24,512]{2,1,0:T(8,128)(2,1)S(1)}, bf16[8,24,512]{2,1,0:T(8,128)(2,1)}, u32[]{:S(2)}) copy-start(bf16[8,24,512]{2,1,0:T(8,128)(2,1)} %copy-done.9) | copy-start | bytes 589828
  100.5 18.9 %copy-start.12 = (bf16[8,24,512]{2,1,0:T(8,128)(2,1)S(1)}, bf16[8,24,512]{2,1,0:T(8,128)(2,1)}, u32[]{:S(2)}) copy-start(bf16[8,24,512]{2,1,0:T(8,128)(2,1)} %copy-done.11) | copy-start | bytes 589828
  102.7 16.8 %collective-permute-start.10 = (bf16[512,1024]{1,0:T(8,128)(2,1)S(1)}, bf16[512,1024]{1,0:T(8,128)(2,1)S(1)}, u32[]{:S(2)}, u32[]{:S(2)}) collective-permute-start(bf16[512,1024]{1,0:T(8,128)(2,1)S(1)} %place.1.refs_7_.own_ref), channel_id=1, source_target_pairs={{0,4},{4,0},{8,12},{12,8},{16,20},{20,16},{24,28},{28,24},{32,36},... | collective-permute-start | bytes 3145736 | tf_op jit(solution)/shard_map/ppermute | solution.py:54
  104.6 10.7 %collective-permute-start.9 = (bf16[8,24,512]{2,1,0:T(8,128)(2,1)S(1)}, bf16[8,24,512]{2,1,0:T(8,128)(2,1)S(1)}, u32[]{:S(2)}, u32[]{:S(2)}) collective-permute-start(bf16[8,24,512]{2,1,0:T(8,128)(2,1)S(1)} %copy-done.10), channel_id=1, source_target_pairs={{0,3},{1,0},{2,1},{3,2},{4,7},{5,4},{6,5},{7,6},{8,11},{9,8},{10,9... | collective-permute-start | bytes 589832 | tf_op jit(solution)/shard_map/ppermute | solution.py:278
  106.7 12.8 %collective-permute-start.8 = (bf16[8,24,512]{2,1,0:T(8,128)(2,1)S(1)}, bf16[8,24,512]{2,1,0:T(8,128)(2,1)S(1)}, u32[]{:S(2)}, u32[]{:S(2)}) collective-permute-start(bf16[8,24,512]{2,1,0:T(8,128)(2,1)S(1)} %copy-done.10), channel_id=1, source_target_pairs={{0,2},{1,3},{2,0},{3,1},{4,6},{5,7},{6,4},{7,5},{8,10},{9,11},{10,... | collective-permute-start | bytes 589832 | tf_op jit(solution)/shard_map/ppermute | solution.py:278
  120.5 1.1 copy-start.6
  126.0 1.2 copy-start.1
  128.2 31.4 %all-to-all-start.3 = ((bf16[8,96,1024]{2,1,0:T(8,128)(2,1)}), bf16[8,96,1024]{2,1,0:T(8,128)(2,1)}, u32[]{:S(2)}, u32[]{:S(2)}) async-start(bf16[8,96,1024]{2,1,0:T(8,128)(2,1)} %copy-done.1), calls=%async_computation.3 | async-start | bytes 3145728 | tf_op jit(solution)/shard_map/all_to_all | solution.py:42
  135.0 1.2 copy-start.5
  139.5 8.7 %collective-permute-start.11 = (bf16[8,24,512]{2,1,0:T(8,128)(2,1)S(1)}, bf16[8,24,512]{2,1,0:T(8,128)(2,1)S(1)}, u32[]{:S(2)}, u32[]{:S(2)}) collective-permute-start(bf16[8,24,512]{2,1,0:T(8,128)(2,1)S(1)} %get-tuple-element.24), channel_id=1, source_target_pairs={{0,1},{1,2},{2,3},{3,0},{4,5},{5,6},{6,7},{7,4},{8,9},{9,10},{10,1... | collective-permute-start | bytes 589832 | tf_op jit(solution)/shard_map/ppermute | solution.py:221
  142.2 13.0 %collective-permute-start.13 = (bf16[8,24,512]{2,1,0:T(8,128)(2,1)S(1)}, bf16[8,24,512]{2,1,0:T(8,128)(2,1)S(1)}, u32[]{:S(2)}, u32[]{:S(2)}) collective-permute-start(bf16[8,24,512]{2,1,0:T(8,128)(2,1)S(1)} %get-tuple-element.25), channel_id=1, source_target_pairs={{0,3},{1,0},{2,1},{3,2},{4,7},{5,4},{6,5},{7,6},{8,11},{9,8},{10,9... | collective-permute-start | bytes 589832 | tf_op jit(solution)/shard_map/ppermute | solution.py:221
  145.4 9.8 %collective-permute-start.12 = (bf16[8,24,512]{2,1,0:T(8,128)(2,1)S(1)}, bf16[8,24,512]{2,1,0:T(8,128)(2,1)S(1)}, u32[]{:S(2)}, u32[]{:S(2)}) collective-permute-start(bf16[8,24,512]{2,1,0:T(8,128)(2,1)S(1)} %get-tuple-element.26), channel_id=1, source_target_pairs={{0,2},{1,3},{2,0},{3,1},{4,6},{5,7},{6,4},{7,5},{8,10},{9,11},{10,... | collective-permute-start | bytes 589832 | tf_op jit(solution)/shard_map/ppermute | solution.py:221
  155.3 13.5 %copy-start.17 = (s32[192]{0:T(256)S(1)}, s32[192]{0:T(256)}, u32[]{:S(2)}) copy-start(s32[192]{0:T(256)} %copy-done.16) | copy-start | bytes 2308
  155.3 13.8 %copy-start.15 = (s32[192]{0:T(256)S(1)}, s32[192]{0:T(256)}, u32[]{:S(2)}) copy-start(s32[192]{0:T(256)} %copy-done.14) | copy-start | bytes 2308
  155.3 13.7 %collective-permute-start.14 = (bf16[192,256]{1,0:T(8,128)(2,1)S(1)}, bf16[192,256]{1,0:T(8,128)(2,1)S(1)}, u32[]{:S(2)}, u32[]{:S(2)}) collective-permute-start(bf16[192,256]{1,0:T(8,128)(2,1)S(1)} %broadcast_select_fusion.2), channel_id=1, source_target_pairs={{0,4},{4,0},{8,12},{12,8},{16,20},{20,16},{24,28},{28,24},{32,36},... | collective-permute-start | bytes 294920 | tf_op jit(solution)/shard_map/ppermute | solution.py:54
  162.1 17.1 %all-to-all-start.4 = ((bf16[8,12,1024]{2,1,0:T(8,128)(2,1)}), bf16[8,12,1024]{2,1,0:T(8,128)(2,1)S(1)}, u32[]{:S(2)}, u32[]{:S(2)}) async-start(bf16[8,12,1024]{2,1,0:T(8,128)(2,1)} %reshape.97), calls=%async_computation.4 | async-start | bytes 524288 | tf_op jit(solution)/shard_map/all_to_all | solution.py:42
  (6 other events, 5.4 us)

commit v6 on v5

--- a/solution.py
+++ b/solution.py
@@ -12,10 +12,12 @@
 HEADS = 32
 KV_HEADS = 4
 HEAD_DIM = 128
-SW = 1536
 REACH = 2
 GROUP_ROWS = 4
 SIDE = 8
+
+VMEM = pl.BlockSpec(memory_space=pltpu.VMEM)
+SMEM = pl.BlockSpec(memory_space=pltpu.SMEM)
 
 neg_large = -1e30
 bf16, f32, i32 = jnp.bfloat16, jnp.float32, jnp.int32
@@ -58,7 +60,9 @@
     return jnp.broadcast_to(block[None], (count,) + block.shape)
 
 
-def attend_kernel(q_ref, b2_ref, b1_ref, b0_ref, o_ref, bias_ref):
+def attend_kernel(q_any, b2_ref, b1_ref, b0_ref, o_ref, bias_ref, q_ref, sem):
+    load = pltpu.make_async_copy(q_any, q_ref, sem)
+    load.start()
     rows = q_ref.shape[0]
     blocks = (b2_ref, b1_ref, b0_ref)
     seg_lanes = [
@@ -75,6 +79,7 @@
     keys = jnp.concatenate([b[0:rows, :] for b in blocks], axis=0)
     values = jnp.concatenate([b[rows : 2 * rows, :] for b in blocks], axis=0)
     scale = 1.0 / math.sqrt(HEAD_DIM)
+    load.wait()
     for head in range(HEADS // KV_HEADS):
         lanes = slice(head * HEAD_DIM, (head + 1) * HEAD_DIM)
         scores = dot(q_ref[:, lanes], keys, ((1,), (1,))) * scale + bias_ref[...]
@@ -84,25 +89,31 @@
         o_ref[:, lanes] = dot(weights, values, ((1,), (0,))).astype(bf16)
 
 
-def attend(queries, keys, values, segment):
-    rows, lanes = keys.shape
+def packed_rows(keys, values, segment):
+    lanes = keys.shape[1]
     seg_rows = (segment + 1).astype(bf16).reshape(-1, lanes)
     seg_rows = jnp.concatenate([seg_rows, jnp.zeros((14, lanes), bf16)], 0)
-    packed = jnp.concatenate([keys, values, seg_rows], 0)
-    earlier = [passed_along(packed, "seq", step) for step in (1, 2)]
-    vmem = pl.BlockSpec(memory_space=pltpu.VMEM)
+    return jnp.concatenate([keys, values, seg_rows], 0)
+
+
+def attend(queries, two_before, one_before, packed):
+    rows = queries.shape[0]
     return pl.pallas_call(
         attend_kernel,
         out_shape=jax.ShapeDtypeStruct(queries.shape, bf16),
-        in_specs=[vmem] * 4,
-        out_specs=vmem,
-        scratch_shapes=[pltpu.VMEM((rows, (REACH + 1) * rows), f32)],
+        in_specs=[pl.BlockSpec(memory_space=pl.ANY)] + [VMEM] * 3,
+        out_specs=VMEM,
+        scratch_shapes=[
+            pltpu.VMEM((rows, (REACH + 1) * rows), f32),
+            pltpu.VMEM(queries.shape, bf16),
+            pltpu.SemaphoreType.DMA,
+        ],
         compiler_params=pltpu.CompilerParams(vmem_limit_bytes=24 << 20),
         cost_estimate=pl.CostEstimate(
             flops=4 * rows * 3 * rows * 1024, bytes_accessed=2 << 20, transcendentals=rows * 3 * rows * 8
         ),
         name="attend",
-    )(queries, earlier[1], earlier[0], packed)
+    )(queries, two_before, one_before, packed)
 
 
 def dot(a, b, dims):
@@ -111,10 +122,6 @@
 
 def hot(a, b):
     return (a == b).astype(bf16)
-
-
-VMEM = pl.BlockSpec(memory_space=pltpu.VMEM)
-SMEM = pl.BlockSpec(memory_space=pltpu.SMEM)
 
 
 def chunk_of(core, ring, quarter):
@@ -177,23 +184,53 @@
     )(place, own, other, half_proj)
 
 
+def targets_kernel(row_ref, states_ref, mine_ref, theirs_ref, own_ref, other_ref):
+    rows = states_ref.shape[0]
+    source = lax.broadcasted_iota(i32, (rows, rows), 0)
+    chosen = jnp.where(source == row_ref[...], 1.0, 0.0).astype(bf16)
+    for spread_ref, out_ref in ((mine_ref, own_ref), (theirs_ref, other_ref)):
+        for share in range(4):
+            states = states_ref[:, share * 384 : share * 384 + 384]
+            part = dot(spread_ref[...], states, ((0,), (1,))).astype(bf16)
+            part = dot(part, chosen, ((1,), (0,))).astype(bf16)
+            for quarter in range(8):
+                out_ref[share * 8 + quarter] = part[quarter * 24 : quarter * 24 + 24]
+
+
+def targets_of(target_row, student_states, mine, theirs):
+    rows = student_states.shape[0]
+    out = jax.ShapeDtypeStruct((32, 24, rows), bf16)
+    return pl.pallas_call(
+        targets_kernel,
+        out_shape=(out, out),
+        in_specs=[VMEM] * 4,
+        out_specs=(VMEM, VMEM),
+        compiler_params=pltpu.CompilerParams(vmem_limit_bytes=16 << 20),
+        cost_estimate=pl.CostEstimate(
+            flops=2 * 1536 * rows * (384 + 256), bytes_accessed=2 << 20, transcendentals=0
+        ),
+        name="targets",
+    )(target_row.reshape(1, rows), student_states, mine, theirs)
+
+
 def term_kernel(place_ref, *refs):
-    parts, (target_ref, own_ref, other_ref, own_m_ref, other_m_ref, out_ref, held) = refs[:4], refs[4:]
+    parts, refs = refs[:4], refs[4:]
+    own_t, other_t, own_ref, other_ref, own_m, other_m, out_ref, held, moved = refs
     core, share = place_ref[0], place_ref[1]
+    half = own_t.shape[2]
     for i, part in enumerate(parts):
         held[i] = part[...]
     attended = jnp.concatenate([own_ref[...], other_ref[...]], axis=0)
-    moved = own_m_ref[...] + other_m_ref[...]
+    moved[...] = own_m[...] + other_m[...]
+    right = [moved[pl.ds(c * half, half), :] for c in (core, 1 - core)]
     for ring in range(SIDE):
-        left, right = [], []
-        for quarter in range(4):
-            chunk = chunk_of(core, ring, quarter)
-            away = lax.rem(share - chunk // 8 + 4, 4)
-            left.append(held[away, lax.rem(chunk, 8)])
-            right.append(target_ref[chunk])
-        y_part = dot(jnp.concatenate(left, axis=0), attended, ((1,), (0,)))
-        t_part = dot(jnp.concatenate(right, axis=0), moved, ((1,), (0,)))
-        out_ref[ring] = (y_part - t_part).astype(bf16)
+        chunks = [chunk_of(core, ring, quarter) for quarter in range(4)]
+        left = [held[lax.rem(share - k // 8 + 4, 4), lax.rem(k, 8)] for k in chunks]
+        total = dot(jnp.concatenate(left, axis=0), attended, ((1,), (0,)))
+        for target_ref, rows in zip((own_t, other_t), right):
+            left = jnp.concatenate([target_ref[k] for k in chunks], axis=0)
+            total = total - dot(left, rows, ((1,), (0,)))
+        out_ref[ring] = total.astype(bf16)
 
 
 def term_of(place, parts, targets, own, other, own_m, other_m):
@@ -201,15 +238,15 @@
     return pl.pallas_call(
         term_kernel,
         out_shape=jax.ShapeDtypeStruct((SIDE, 96, feats), bf16),
-        in_specs=[SMEM] + [VMEM] * 9,
+        in_specs=[SMEM] + [VMEM] * 10,
         out_specs=VMEM,
-        scratch_shapes=[pltpu.VMEM((4, 8, 24, rows), bf16)],
+        scratch_shapes=[pltpu.VMEM((4, 8, 24, rows), bf16), pltpu.VMEM((rows, feats), bf16)],
         compiler_params=pltpu.CompilerParams(vmem_limit_bytes=24 << 20),
         cost_estimate=pl.CostEstimate(
             flops=4 * 768 * rows * feats, bytes_accessed=8 << 20, transcendentals=0
         ),
         name="term",
-    )(place, *parts, targets, own, other, own_m, other_m)
+    )(place, *parts, *targets, own, other, own_m, other_m)
 
 
 def share_route(distance):
@@ -236,16 +273,18 @@
     rows = queries.shape[0]
     devices = lax.axis_size("seq")
     shares = lax.axis_size("tp")
-    share = SW // shares
     core = lax.axis_index("seq") % 2
     tp_index = lax.axis_index("tp")
     place = jnp.stack([core, tp_index]).astype(i32)
     feats = proj.shape[0]
     row_ids = jnp.arange(rows, dtype=i32)
     near = exchange(to_all(proj, SIDE), NEAR).reshape(SIDE * feats, -1)
+    packed = packed_rows(keys, values, segment)
+    one_before = passed_along(packed, "seq", 1)
+    two_before = passed_along(packed, "seq", 2)
     queries, near, place = lax.optimization_barrier((queries, near, place))
     half_proj = exchange(to_all(near, SIDE), FAR).reshape(SIDE * SIDE * feats, -1)
-    attended = attend(queries, keys, values, segment)
+    attended = attend(queries, two_before, one_before, packed)
     partner = other_core(attended)
     target_dev = repack // rows
     local_slot = repack - target_dev * rows
@@ -255,23 +294,13 @@
     wide = jnp.concatenate([attended, slot_lanes], 1)
     buckets = dot(pick, wide, ((1,), (0,))).astype(bf16)
     buckets = buckets.reshape(devices // 2, 2 * GROUP_ROWS, -1)
-    mine, theirs = spread_of(core), spread_of(1 - core)
-    chosen = dot(hot(target_row[:, None], row_ids[None, :]), student_states, ((1,), (0,)))
-    chosen = chosen.astype(bf16)
-    chosen = [chosen[:, i * share : (i + 1) * share] for i in range(shares)]
-    target_own = jnp.concatenate([dot(mine, c, ((0,), (1,))) for c in chosen], 0).astype(bf16)
-    target_other = jnp.concatenate([dot(theirs, c, ((0,), (1,))) for c in chosen], 0)
-    target_other = other_core(target_other.astype(bf16))
-    targets = jnp.concatenate(
-        [
-            jnp.where(core == 0, target_own, target_other),
-            jnp.where(core == 0, target_other, target_own),
-        ],
-        1,
-    )
-    buckets, half_proj, targets = lax.optimization_barrier((buckets, half_proj, targets))
+    buckets, half_proj = lax.optimization_barrier((buckets, half_proj))
     arrived = exchange(buckets, SAME_CORE)
     y_split = project(place, attended, partner, half_proj, False)
+    y_split, target_row = lax.optimization_barrier((y_split, target_row))
+    mine, theirs = spread_of(core), spread_of(1 - core)
+    target_own, target_other = targets_of(target_row, student_states, mine, theirs)
+    target_other = other_core(target_other)
     y_teacher = summed_share(y_split)
     parts = [y_teacher]
     for distance in range(1, shares):
@@ -279,8 +308,8 @@
     arrived, parts[1] = lax.optimization_barrier((arrived, parts[1]))
     own = placed_rows(arrived)
     other = other_core(own)
-    term = term_of(place, parts, targets.reshape(32, 24, 2 * rows), attended, partner, own, other)
-    term, own = lax.optimization_barrier((term, own))
+    targets = (target_own, target_other)
+    term = term_of(place, parts, targets, attended, partner, own, other)
     far = exchange(term, FAR)
     far = jnp.sum(far.astype(f32), axis=0).astype(bf16)
     last = exchange(far.reshape(SIDE, feats, -1), NEAR)

time: 181 us -> 183 us (1.011)
  the two profiles are of different devices: /device:TPU:6 before, /device:TPU:2 now
where the time goes in v6:
time: 183 us; the launch traced here: 182 us
  starting transfers between devices  80.2 us (44%)
  waiting for transfers between devices  69 us (38%)
  Pallas kernels  20 us (11%)
  local copies, waits for them, and re-layouts  6.16 us (3%)
  other arithmetic  2.98 us (2%)
  matrix products  2.78 us (2%)
    all_to_all x5, starting transfers between devices, exchange(): lax.all_to_all(block, axis, split_axis=0, concat_axis=0, tiled=True, axis...  37.8 us
    all_to_all x5, waiting for transfers between devices, exchange(): lax.all_to_all(block, axis, split_axis=0, concat_axis=0, tiled=True, axis...  35.2 us
    ppermute x6, starting transfers between devices, summed_share(): got = [lax.ppermute(y_split[k], 'tp', share_route(k)) for k in range(1, 4)]  20.2 us
    ppermute x3, waiting for transfers between devices, on_device(): parts.append(lax.ppermute(y_teacher, 'tp', share_route(distance)))  13.8 us
    ppermute x6, waiting for transfers between devices, summed_share(): got = [lax.ppermute(y_split[k], 'tp', share_route(k)) for k in range(1, 4)]  12.8 us
    ppermute x3, starting transfers between devices, on_device(): parts.append(lax.ppermute(y_teacher, 'tp', share_route(distance)))  10.3 us
    ppermute x4, starting transfers between devices, other_core(): lax.ppermute(block, 'seq', [(i, i ^ 1) for i in range(lax.axis_size('seq'...  8.17 us
    pallas_call x2, Pallas kernels, project(): pl.pallas_call(functools.partial(project_kernel, add), out_shape=jax.Shap...  7.18 us
  transfers between devices with their start and end apart: 20, of which 13 were waited for; matrix products, arithmetic and copies ran while one was open for 3% of the time, Pallas kernels for 8%

profile of v6, /device:TPU:2, one launch (start us, length us, event | category | flops | bytes accessed | tf_op | source)
XLA Modules:
  0.0 182.2 jit_solution(13410402752404829719)
XLA Ops:
  2.1 7.1 %all-to-all-start = ((bf16[8,12,1024]{2,1,0:T(8,128)(2,1)}), bf16[8,12,1024]{2,1,0:T(8,128)(2,1)S(1)}, u32[]{:S(2)}, u32[]{:S(2)}) async-start(bf16[8,12,1024]{2,1,0:T(8,128)(2,1)} %broadcast_in_dim.8), calls=%async_computation | async-start | bytes 524288 | tf_op jit(solution)/shard_map/all_to_all | solution.py:44
  9.3 10.4 %all-to-all-done = bf16[8,12,1024]{2,1,0:T(8,128)(2,1)S(1)} async-done(((bf16[8,12,1024]{2,1,0:T(8,128)(2,1)}), bf16[8,12,1024]{2,1,0:T(8,128)(2,1)S(1)}, u32[]{:S(2)}, u32[]{:S(2)}) %all-to-all-start) | async-done | bytes 196640 | tf_op jit(solution)/shard_map/all_to_all | solution.py:44
  21.1 10.5 %all-to-all-start.1 = ((bf16[8,96,1024]{2,1,0:T(8,128)(2,1)}), bf16[8,96,1024]{2,1,0:T(8,128)(2,1)S(1)}, u32[]{:S(2)}, u32[]{:S(2)}) async-start(bf16[8,96,1024]{2,1,0:T(8,128)(2,1)} %broadcast_in_dim.11), calls=%async_computation.1 | async-start | bytes 3145728 | tf_op jit(solution)/shard_map/all_to_all | solution.py:44
  31.8 2.5 %collective-permute-start = (bf16[528,128]{1,0:T(8,128)(2,1)S(1)}, bf16[528,128]{1,0:T(8,128)(2,1)S(1)}, u32[]{:S(2)}, u32[]{:S(2)}) collective-permute-start(bf16[528,128]{1,0:T(8,128)(2,1)S(1)} %maximum_maximum_fusion.b0_ref), channel_id=1, source_target_pairs={{0,8},{4,12},{8,16},{12,20},{16,24},{20,28},{24,32},{28,36},{32,40... | collective-permute-start | bytes 405512 | tf_op jit(solution)/shard_map/ppermute | solution.py:52
  35.6 5.3 %collective-permute-done.b2_ref = bf16[528,128]{1,0:T(8,128)(2,1)S(1)} collective-permute-done((bf16[528,128]{1,0:T(8,128)(2,1)S(1)}, bf16[528,128]{1,0:T(8,128)(2,1)S(1)}, u32[]{:S(2)}, u32[]{:S(2)}) %collective-permute-start) | collective-permute-done | bytes 135200 | tf_op jit(solution)/shard_map/ppermute | solution.py:52
  41.0 4.6 %attend.1.own_ref.refs_6_ = bf16[256,1024]{1,0:T(8,128)(2,1)S(1)} custom-call(bf16[256,1024]{1,0:T(8,128)(2,1)S(1)} %copy-done.4, bf16[528,128]{1,0:T(8,128)(2,1)S(1)} %collective-permute-done.b2_ref, bf16[528,128]{1,0:T(8,128)(2,1)S(1)} %collective-permute-done.1.b1_ref, bf16[528,128]{1,0:T(8,128)(2,1)S(1)} %maximum_maximum_fusion.b0_ref), custom_call_target="tpu_custom_call" | custom-call | flops 805306368 | bytes 2097152 | tf_op jit(solution)/shard_map/attend/pallas_call | solution.py:101
  47.2 13.3 %all-to-all-done.1 = bf16[8,96,1024]{2,1,0:T(8,128)(2,1)S(1)} async-done(((bf16[8,96,1024]{2,1,0:T(8,128)(2,1)}), bf16[8,96,1024]{2,1,0:T(8,128)(2,1)S(1)}, u32[]{:S(2)}, u32[]{:S(2)}) %all-to-all-start.1) | async-done | bytes 1572896 | tf_op jit(solution)/shard_map/all_to_all | solution.py:44
  60.5 6.9 %all-to-all-start.2 = ((bf16[64,8,1152]{2,1,0:T(8,128)(2,1)}), bf16[64,8,1152]{2,1,0:T(8,128)(2,1)}, u32[]{:S(2)}, u32[]{:S(2)}) async-start(bf16[64,8,1152]{2,1,0:T(8,128)(2,1)} %fusion), calls=%async_computation.2 | async-start | bytes 2359296 | tf_op jit(solution)/shard_map/all_to_all | solution.py:44
  71.2 3.2 %shard_map.95 = bf16[4,8,24,512]{3,2,1,0:T(8,128)(2,1)S(1)} custom-call(s32[2]{0:T(128)S(1)} %pad_add_fusion.place_ref, bf16[256,1024]{1,0:T(8,128)(2,1)S(1)} %attend.1.own_ref.refs_6_, bf16[256,1024]{1,0:T(8,128)(2,1)S(1)} %collective-permute-done.2.other_ref.refs_7_, bf16[768,1024]{1,0:T(8,128)(2,1)S(1)} %bitcast.30), custom_call_target="tpu_custom_call" | custom-call | flops 805306368 | bytes 4194304 | tf_op jit(solution)/shard_map/pallas_call | solution.py:175
  74.5 2.4 %collective-permute-start.5 = (bf16[8,24,512]{2,1,0:T(8,128)(2,1)S(1)}, bf16[8,24,512]{2,1,0:T(8,128)(2,1)S(1)}, u32[]{:S(2)}, u32[]{:S(2)}) collective-permute-start(bf16[8,24,512]{2,1,0:T(8,128)(2,1)S(1)} %get-tuple-element.30), channel_id=1, source_target_pairs={{0,3},{1,0},{2,1},{3,2},{4,7},{5,4},{6,5},{7,6},{8,11},{9,8},{10,9... | collective-permute-start | bytes 589832 | tf_op jit(solution)/shard_map/ppermute | solution.py:258
  76.9 4.3 %collective-permute-start.4 = (bf16[8,24,512]{2,1,0:T(8,128)(2,1)S(1)}, bf16[8,24,512]{2,1,0:T(8,128)(2,1)S(1)}, u32[]{:S(2)}, u32[]{:S(2)}) collective-permute-start(bf16[8,24,512]{2,1,0:T(8,128)(2,1)S(1)} %get-tuple-element.31), channel_id=1, source_target_pairs={{0,2},{1,3},{2,0},{3,1},{4,6},{5,7},{6,4},{7,5},{8,10},{9,11},{10,... | collective-permute-start | bytes 589832 | tf_op jit(solution)/shard_map/ppermute | solution.py:258
  81.3 3.7 %collective-permute-start.3 = (bf16[8,24,512]{2,1,0:T(8,128)(2,1)S(1)}, bf16[8,24,512]{2,1,0:T(8,128)(2,1)S(1)}, u32[]{:S(2)}, u32[]{:S(2)}) collective-permute-start(bf16[8,24,512]{2,1,0:T(8,128)(2,1)S(1)} %get-tuple-element.29), channel_id=1, source_target_pairs={{0,1},{1,2},{2,3},{3,0},{4,5},{5,6},{6,7},{7,4},{8,9},{9,10},{10,1... | collective-permute-start | bytes 589832 | tf_op jit(solution)/shard_map/ppermute | solution.py:258
  85.0 3.5 %collective-permute-done.4 = bf16[8,24,512]{2,1,0:T(8,128)(2,1)S(1)} collective-permute-done((bf16[8,24,512]{2,1,0:T(8,128)(2,1)S(1)}, bf16[8,24,512]{2,1,0:T(8,128)(2,1)S(1)}, u32[]{:S(2)}, u32[]{:S(2)}) %collective-permute-start.4) | collective-permute-done | bytes 196640 | tf_op jit(solution)/shard_map/ppermute | solution.py:258
  88.5 2.8 %collective-permute-done.3 = bf16[8,24,512]{2,1,0:T(8,128)(2,1)S(1)} collective-permute-done((bf16[8,24,512]{2,1,0:T(8,128)(2,1)S(1)}, bf16[8,24,512]{2,1,0:T(8,128)(2,1)S(1)}, u32[]{:S(2)}, u32[]{:S(2)}) %collective-permute-start.3) | collective-permute-done | bytes 196640 | tf_op jit(solution)/shard_map/ppermute | solution.py:258
  91.3 3.4 %collective-permute-start.6 = (bf16[8,24,512]{2,1,0:T(8,128)(2,1)S(1)}, bf16[8,24,512]{2,1,0:T(8,128)(2,1)S(1)}, u32[]{:S(2)}, u32[]{:S(2)}) collective-permute-start(bf16[8,24,512]{2,1,0:T(8,128)(2,1)S(1)} %fusion.10.refs_0_), channel_id=1, source_target_pairs={{0,1},{1,2},{2,3},{3,0},{4,5},{5,6},{6,7},{7,4},{8,9},{9,10},{10,1... | collective-permute-start | bytes 589832 | tf_op jit(solution)/shard_map/ppermute | solution.py:307
  94.7 6.3 %collective-permute-done.6.refs_1_ = bf16[8,24,512]{2,1,0:T(8,128)(2,1)S(1)} collective-permute-done((bf16[8,24,512]{2,1,0:T(8,128)(2,1)S(1)}, bf16[8,24,512]{2,1,0:T(8,128)(2,1)S(1)}, u32[]{:S(2)}, u32[]{:S(2)}) %collective-permute-start.6) | collective-permute-done | bytes 196640 | tf_op jit(solution)/shard_map/ppermute | solution.py:307
  101.0 2.1 %place.1.own_ref.refs_8_ = bf16[512,1024]{1,0:T(8,128)(2,1)S(1)} custom-call(bf16[64,8,1152]{2,1,0:T(8,128)(2,1)} %all-to-all-done.2.in_ref), custom_call_target="tpu_custom_call" | custom-call | flops 536870912 | bytes 3145728 | tf_op jit(solution)/shard_map/place/pallas_call | solution.py:145
  108.3 2.4 %collective-permute-start.14 = (bf16[32,24,256]{2,1,0:T(8,128)(2,1)S(1)}, bf16[32,24,256]{2,1,0:T(8,128)(2,1)S(1)}, u32[]{:S(2)}, u32[]{:S(2)}) collective-permute-start(bf16[32,24,256]{2,1,0:T(8,128)(2,1)S(1)} %get-tuple-element.23), channel_id=1, source_target_pairs={{0,4},{4,0},{8,12},{12,8},{16,20},{20,16},{24,28},{28,24},{32,36},... | collective-permute-start | bytes 1179656 | tf_op jit(solution)/shard_map/ppermute | solution.py:56
  110.7 3.2 %collective-permute-start.12 = (bf16[8,24,512]{2,1,0:T(8,128)(2,1)S(1)}, bf16[8,24,512]{2,1,0:T(8,128)(2,1)S(1)}, u32[]{:S(2)}, u32[]{:S(2)}) collective-permute-start(bf16[8,24,512]{2,1,0:T(8,128)(2,1)S(1)} %fusion.10.refs_0_), channel_id=1, source_target_pairs={{0,2},{1,3},{2,0},{3,1},{4,6},{5,7},{6,4},{7,5},{8,10},{9,11},{10,... | collective-permute-start | bytes 589832 | tf_op jit(solution)/shard_map/ppermute | solution.py:307
  114.0 3.7 %collective-permute-start.13 = (bf16[8,24,512]{2,1,0:T(8,128)(2,1)S(1)}, bf16[8,24,512]{2,1,0:T(8,128)(2,1)S(1)}, u32[]{:S(2)}, u32[]{:S(2)}) collective-permute-start(bf16[8,24,512]{2,1,0:T(8,128)(2,1)S(1)} %fusion.10.refs_0_), channel_id=1, source_target_pairs={{0,3},{1,0},{2,1},{3,2},{4,7},{5,4},{6,5},{7,6},{8,11},{9,8},{10,9... | collective-permute-start | bytes 589832 | tf_op jit(solution)/shard_map/ppermute | solution.py:307
  117.7 3.5 %collective-permute-done.12.refs_2_ = bf16[8,24,512]{2,1,0:T(8,128)(2,1)S(1)} collective-permute-done((bf16[8,24,512]{2,1,0:T(8,128)(2,1)S(1)}, bf16[8,24,512]{2,1,0:T(8,128)(2,1)S(1)}, u32[]{:S(2)}, u32[]{:S(2)}) %collective-permute-start.12) | collective-permute-done | bytes 196640 | tf_op jit(solution)/shard_map/ppermute | solution.py:307
  121.2 4.0 %collective-permute-done.13.refs_3_ = bf16[8,24,512]{2,1,0:T(8,128)(2,1)S(1)} collective-permute-done((bf16[8,24,512]{2,1,0:T(8,128)(2,1)S(1)}, bf16[8,24,512]{2,1,0:T(8,128)(2,1)S(1)}, u32[]{:S(2)}, u32[]{:S(2)}) %collective-permute-start.13) | collective-permute-done | bytes 196640 | tf_op jit(solution)/shard_map/ppermute | solution.py:307
  125.2 4.3 %term.1 = bf16[8,96,1024]{2,1,0:T(8,128)(2,1)S(1)} custom-call(s32[2]{0:T(128)S(1)} %pad_add_fusion.place_ref, bf16[8,24,512]{2,1,0:T(8,128)(2,1)S(1)} %fusion.10.refs_0_, bf16[8,24,512]{2,1,0:T(8,128)(2,1)S(1)} %collective-permute-done.6.refs_1_, bf16[8,24,512]{2,1,0:T(8,128)(2,1)S(1)} %collective-permute-done.12.refs_2_, ...), custom_call_target="tpu_custom_call" | custom-call | flops 1610612736 | bytes 8388608 | tf_op jit(solution)/shard_map/term/pallas_call | solution.py:238
  130.6 6.8 %all-to-all-start.3 = ((bf16[8,96,1024]{2,1,0:T(8,128)(2,1)}), bf16[8,96,1024]{2,1,0:T(8,128)(2,1)}, u32[]{:S(2)}, u32[]{:S(2)}) async-start(bf16[8,96,1024]{2,1,0:T(8,128)(2,1)} %copy-done), calls=%async_computation.3 | async-start | bytes 3145728 | tf_op jit(solution)/shard_map/all_to_all | solution.py:44
  137.4 4.0 %shard_map.96 = bf16[4,8,24,512]{3,2,1,0:T(8,128)(2,1)S(1)} custom-call(s32[2]{0:T(128)S(1)} %pad_add_fusion.place_ref, bf16[512,1024]{1,0:T(8,128)(2,1)S(1)} %place.1.own_ref.refs_8_, bf16[512,1024]{1,0:T(8,128)(2,1)} %collective-permute-done.7.other_ref.refs_9_, bf16[768,1024]{1,0:T(8,128)(2,1)S(1)} %bitcast.31), custom_call_target="tpu_custom_call" | custom-call | flops 805306368 | bytes 4194304 | tf_op jit(solution)/shard_map/pallas_call | solution.py:175
  143.4 3.9 %collective-permute-start.9 = (bf16[8,24,512]{2,1,0:T(8,128)(2,1)S(1)}, bf16[8,24,512]{2,1,0:T(8,128)(2,1)S(1)}, u32[]{:S(2)}, u32[]{:S(2)}) collective-permute-start(bf16[8,24,512]{2,1,0:T(8,128)(2,1)S(1)} %get-tuple-element.28), channel_id=1, source_target_pairs={{0,2},{1,3},{2,0},{3,1},{4,6},{5,7},{6,4},{7,5},{8,10},{9,11},{10,... | collective-permute-start | bytes 589832 | tf_op jit(solution)/shard_map/ppermute | solution.py:258
  147.3 3.8 %collective-permute-start.8 = (bf16[8,24,512]{2,1,0:T(8,128)(2,1)S(1)}, bf16[8,24,512]{2,1,0:T(8,128)(2,1)S(1)}, u32[]{:S(2)}, u32[]{:S(2)}) collective-permute-start(bf16[8,24,512]{2,1,0:T(8,128)(2,1)S(1)} %get-tuple-element.26), channel_id=1, source_target_pairs={{0,1},{1,2},{2,3},{3,0},{4,5},{5,6},{6,7},{7,4},{8,9},{9,10},{10,1... | collective-permute-start | bytes 589832 | tf_op jit(solution)/shard_map/ppermute | solution.py:258
  151.1 2.9 %collective-permute-done.10 = bf16[8,24,512]{2,1,0:T(8,128)(2,1)S(1)} collective-permute-done((bf16[8,24,512]{2,1,0:T(8,128)(2,1)S(1)}, bf16[8,24,512]{2,1,0:T(8,128)(2,1)S(1)}, u32[]{:S(2)}, u32[]{:S(2)}) %collective-permute-start.10) | collective-permute-done | bytes 196640 | tf_op jit(solution)/shard_map/ppermute | solution.py:258
  154.0 3.7 %collective-permute-done.8 = bf16[8,24,512]{2,1,0:T(8,128)(2,1)S(1)} collective-permute-done((bf16[8,24,512]{2,1,0:T(8,128)(2,1)S(1)}, bf16[8,24,512]{2,1,0:T(8,128)(2,1)S(1)}, u32[]{:S(2)}, u32[]{:S(2)}) %collective-permute-start.8) | collective-permute-done | bytes 196640 | tf_op jit(solution)/shard_map/ppermute | solution.py:258
  159.8 2.3 %all-to-all-done.3 = bf16[8,96,1024]{2,1,0:T(8,128)(2,1)} async-done(((bf16[8,96,1024]{2,1,0:T(8,128)(2,1)}), bf16[8,96,1024]{2,1,0:T(8,128)(2,1)}, u32[]{:S(2)}, u32[]{:S(2)}) %all-to-all-start.3) | async-done | bytes 1572896 | tf_op jit(solution)/shard_map/all_to_all | solution.py:44
  164.5 6.6 %all-to-all-start.4 = ((bf16[8,12,1024]{2,1,0:T(8,128)(2,1)}), bf16[8,12,1024]{2,1,0:T(8,128)(2,1)S(1)}, u32[]{:S(2)}, u32[]{:S(2)}) async-start(bf16[8,12,1024]{2,1,0:T(8,128)(2,1)} %reshape.96), calls=%async_computation.4 | async-start | bytes 524288 | tf_op jit(solution)/shard_map/all_to_all | solution.py:44
  172.3 9.2 %all-to-all-done.4 = bf16[8,12,1024]{2,1,0:T(8,128)(2,1)S(1)} async-done(((bf16[8,12,1024]{2,1,0:T(8,128)(2,1)}), bf16[8,12,1024]{2,1,0:T(8,128)(2,1)S(1)}, u32[]{:S(2)}, u32[]{:S(2)}) %all-to-all-start.4) | async-done | bytes 196640 | tf_op jit(solution)/shard_map/all_to_all | solution.py:44
  (61 shorter events, 24.8 us)
Async XLA Ops:
  2.1 17.6 %all-to-all-start = ((bf16[8,12,1024]{2,1,0:T(8,128)(2,1)}), bf16[8,12,1024]{2,1,0:T(8,128)(2,1)S(1)}, u32[]{:S(2)}, u32[]{:S(2)}) async-start(bf16[8,12,1024]{2,1,0:T(8,128)(2,1)} %broadcast_in_dim.8), calls=%async_computation | async-start | bytes 524288 | tf_op jit(solution)/shard_map/all_to_all | solution.py:44
  21.1 10.6 %copy-start.9 = (s32[256]{0:T(256)S(1)}, s32[256]{0:T(256)}, u32[]{:S(2)}) copy-start(s32[256]{0:T(256)} %param.11) | copy-start | bytes 3076
  21.1 10.6 %copy-start.6 = (bf16[256,128]{1,0:T(8,128)(2,1)S(1)}, bf16[256,128]{1,0:T(8,128)(2,1)}, u32[]{:S(2)}) copy-start(bf16[256,128]{1,0:T(8,128)(2,1)} %param.10) | copy-start | bytes 196612
  21.1 10.6 %copy-start.7 = (bf16[256,128]{1,0:T(8,128)(2,1)S(1)}, bf16[256,128]{1,0:T(8,128)(2,1)}, u32[]{:S(2)}) copy-start(bf16[256,128]{1,0:T(8,128)(2,1)} %param.9) | copy-start | bytes 196612
  21.1 14.5 %copy-start.8 = (s32[256]{0:T(256)S(1)}, s32[256]{0:T(256)}, u32[]{:S(2)}) copy-start(s32[256]{0:T(256)} %param.12) | copy-start | bytes 3076
  21.1 19.9 %copy-start.4 = (bf16[256,1024]{1,0:T(8,128)(2,1)S(1)}, bf16[256,1024]{1,0:T(8,128)(2,1)}, u32[]{:S(2)}) copy-start(bf16[256,1024]{1,0:T(8,128)(2,1)} %q_any) | copy-start | bytes 1572868
  21.1 39.4 %all-to-all-start.1 = ((bf16[8,96,1024]{2,1,0:T(8,128)(2,1)}), bf16[8,96,1024]{2,1,0:T(8,128)(2,1)S(1)}, u32[]{:S(2)}, u32[]{:S(2)}) async-start(bf16[8,96,1024]{2,1,0:T(8,128)(2,1)} %broadcast_in_dim.11), calls=%async_computation.1 | async-start | bytes 3145728 | tf_op jit(solution)/shard_map/all_to_all | solution.py:44
  31.8 9.2 %collective-permute-start = (bf16[528,128]{1,0:T(8,128)(2,1)S(1)}, bf16[528,128]{1,0:T(8,128)(2,1)S(1)}, u32[]{:S(2)}, u32[]{:S(2)}) collective-permute-start(bf16[528,128]{1,0:T(8,128)(2,1)S(1)} %maximum_maximum_fusion.b0_ref), channel_id=1, source_target_pairs={{0,8},{4,12},{8,16},{12,20},{16,24},{20,28},{24,32},{28,36},{32,40... | collective-permute-start | bytes 405512 | tf_op jit(solution)/shard_map/ppermute | solution.py:52
  34.3 6.7 %collective-permute-start.1 = (bf16[528,128]{1,0:T(8,128)(2,1)S(1)}, bf16[528,128]{1,0:T(8,128)(2,1)S(1)}, u32[]{:S(2)}, u32[]{:S(2)}) collective-permute-start(bf16[528,128]{1,0:T(8,128)(2,1)S(1)} %maximum_maximum_fusion.b0_ref), channel_id=1, source_target_pairs={{0,4},{4,8},{8,12},{12,16},{16,20},{20,24},{24,28},{28,32},{32,36}... | collective-permute-start | bytes 405512 | tf_op jit(solution)/shard_map/ppermute | solution.py:52
  60.5 40.5 %all-to-all-start.2 = ((bf16[64,8,1152]{2,1,0:T(8,128)(2,1)}), bf16[64,8,1152]{2,1,0:T(8,128)(2,1)}, u32[]{:S(2)}, u32[]{:S(2)}) async-start(bf16[64,8,1152]{2,1,0:T(8,128)(2,1)} %fusion), calls=%async_computation.2 | async-start | bytes 2359296 | tf_op jit(solution)/shard_map/all_to_all | solution.py:44
  67.4 3.8 %collective-permute-start.2 = (bf16[256,1024]{1,0:T(8,128)(2,1)S(1)}, bf16[256,1024]{1,0:T(8,128)(2,1)S(1)}, u32[]{:S(2)}, u32[]{:S(2)}) collective-permute-start(bf16[256,1024]{1,0:T(8,128)(2,1)S(1)} %attend.1.own_ref.refs_6_), channel_id=1, source_target_pairs={{0,4},{4,0},{8,12},{12,8},{16,20},{20,16},{24,28},{28,24},{32,36},... | collective-permute-start | bytes 1572872 | tf_op jit(solution)/shard_map/ppermute | solution.py:56
  71.2 3.2 %copy-start.1 = (bf16[256,1024]{1,0:T(8,128)(2,1)}, bf16[256,1024]{1,0:T(8,128)(2,1)S(1)}, u32[]{:S(2)}) copy-start(bf16[256,1024]{1,0:T(8,128)(2,1)S(1)} %collective-permute-done.2.other_ref.refs_7_) | copy-start | bytes 1572868
  74.5 10.5 %collective-permute-start.5 = (bf16[8,24,512]{2,1,0:T(8,128)(2,1)S(1)}, bf16[8,24,512]{2,1,0:T(8,128)(2,1)S(1)}, u32[]{:S(2)}, u32[]{:S(2)}) collective-permute-start(bf16[8,24,512]{2,1,0:T(8,128)(2,1)S(1)} %get-tuple-element.30), channel_id=1, source_target_pairs={{0,3},{1,0},{2,1},{3,2},{4,7},{5,4},{6,5},{7,6},{8,11},{9,8},{10,9... | collective-permute-start | bytes 589832 | tf_op jit(solution)/shard_map/ppermute | solution.py:258
  76.9 11.5 %collective-permute-start.4 = (bf16[8,24,512]{2,1,0:T(8,128)(2,1)S(1)}, bf16[8,24,512]{2,1,0:T(8,128)(2,1)S(1)}, u32[]{:S(2)}, u32[]{:S(2)}) collective-permute-start(bf16[8,24,512]{2,1,0:T(8,128)(2,1)S(1)} %get-tuple-element.31), channel_id=1, source_target_pairs={{0,2},{1,3},{2,0},{3,1},{4,6},{5,7},{6,4},{7,5},{8,10},{9,11},{10,... | collective-permute-start | bytes 589832 | tf_op jit(solution)/shard_map/ppermute | solution.py:258
  81.3 9.9 %collective-permute-start.3 = (bf16[8,24,512]{2,1,0:T(8,128)(2,1)S(1)}, bf16[8,24,512]{2,1,0:T(8,128)(2,1)S(1)}, u32[]{:S(2)}, u32[]{:S(2)}) collective-permute-start(bf16[8,24,512]{2,1,0:T(8,128)(2,1)S(1)} %get-tuple-element.29), channel_id=1, source_target_pairs={{0,1},{1,2},{2,3},{3,0},{4,5},{5,6},{6,7},{7,4},{8,9},{9,10},{10,1... | collective-permute-start | bytes 589832 | tf_op jit(solution)/shard_map/ppermute | solution.py:258
  91.3 9.7 %collective-permute-start.6 = (bf16[8,24,512]{2,1,0:T(8,128)(2,1)S(1)}, bf16[8,24,512]{2,1,0:T(8,128)(2,1)S(1)}, u32[]{:S(2)}, u32[]{:S(2)}) collective-permute-start(bf16[8,24,512]{2,1,0:T(8,128)(2,1)S(1)} %fusion.10.refs_0_), channel_id=1, source_target_pairs={{0,1},{1,2},{2,3},{3,0},{4,5},{5,6},{6,7},{7,4},{8,9},{9,10},{10,1... | collective-permute-start | bytes 589832 | tf_op jit(solution)/shard_map/ppermute | solution.py:307
  94.7 10.5 %copy-start.5 = (s32[256]{0:T(256)S(1)}, s32[256]{0:T(256)}, u32[]{:S(2)}) copy-start(s32[256]{0:T(256)} %param.15) | copy-start | bytes 3076
  103.1 22.1 %collective-permute-start.7 = (bf16[512,1024]{1,0:T(8,128)(2,1)S(1)}, bf16[512,1024]{1,0:T(8,128)(2,1)}, u32[]{:S(2)}, u32[]{:S(2)}) collective-permute-start(bf16[512,1024]{1,0:T(8,128)(2,1)S(1)} %place.1.own_ref.refs_8_), channel_id=1, source_target_pairs={{0,4},{4,0},{8,12},{12,8},{16,20},{20,16},{24,28},{28,24},{32,36},... | collective-permute-start | bytes 3145736 | tf_op jit(solution)/shard_map/ppermute | solution.py:56
  105.1 20.1 %copy-start.2 = (bf16[256,1024]{1,0:T(8,128)(2,1)S(1)}, bf16[256,1024]{1,0:T(8,128)(2,1)}, u32[]{:S(2)}) copy-start(bf16[256,1024]{1,0:T(8,128)(2,1)} %copy-done.1) | copy-start | bytes 1572868
  105.2 1.1 copy-start.3
  108.3 16.8 %collective-permute-start.14 = (bf16[32,24,256]{2,1,0:T(8,128)(2,1)S(1)}, bf16[32,24,256]{2,1,0:T(8,128)(2,1)S(1)}, u32[]{:S(2)}, u32[]{:S(2)}) collective-permute-start(bf16[32,24,256]{2,1,0:T(8,128)(2,1)S(1)} %get-tuple-element.23), channel_id=1, source_target_pairs={{0,4},{4,0},{8,12},{12,8},{16,20},{20,16},{24,28},{28,24},{32,36},... | collective-permute-start | bytes 1179656 | tf_op jit(solution)/shard_map/ppermute | solution.py:56
  110.7 10.5 %collective-permute-start.12 = (bf16[8,24,512]{2,1,0:T(8,128)(2,1)S(1)}, bf16[8,24,512]{2,1,0:T(8,128)(2,1)S(1)}, u32[]{:S(2)}, u32[]{:S(2)}) collective-permute-start(bf16[8,24,512]{2,1,0:T(8,128)(2,1)S(1)} %fusion.10.refs_0_), channel_id=1, source_target_pairs={{0,2},{1,3},{2,0},{3,1},{4,6},{5,7},{6,4},{7,5},{8,10},{9,11},{10,... | collective-permute-start | bytes 589832 | tf_op jit(solution)/shard_map/ppermute | solution.py:307
  114.0 11.2 %collective-permute-start.13 = (bf16[8,24,512]{2,1,0:T(8,128)(2,1)S(1)}, bf16[8,24,512]{2,1,0:T(8,128)(2,1)S(1)}, u32[]{:S(2)}, u32[]{:S(2)}) collective-permute-start(bf16[8,24,512]{2,1,0:T(8,128)(2,1)S(1)} %fusion.10.refs_0_), channel_id=1, source_target_pairs={{0,3},{1,0},{2,1},{3,2},{4,7},{5,4},{6,5},{7,6},{8,11},{9,8},{10,9... | collective-permute-start | bytes 589832 | tf_op jit(solution)/shard_map/ppermute | solution.py:307
  129.4 1.1 copy-start
  130.6 31.4 %all-to-all-start.3 = ((bf16[8,96,1024]{2,1,0:T(8,128)(2,1)}), bf16[8,96,1024]{2,1,0:T(8,128)(2,1)}, u32[]{:S(2)}, u32[]{:S(2)}) async-start(bf16[8,96,1024]{2,1,0:T(8,128)(2,1)} %copy-done), calls=%async_computation.3 | async-start | bytes 3145728 | tf_op jit(solution)/shard_map/all_to_all | solution.py:44
  141.4 12.6 %collective-permute-start.10 = (bf16[8,24,512]{2,1,0:T(8,128)(2,1)S(1)}, bf16[8,24,512]{2,1,0:T(8,128)(2,1)S(1)}, u32[]{:S(2)}, u32[]{:S(2)}) collective-permute-start(bf16[8,24,512]{2,1,0:T(8,128)(2,1)S(1)} %get-tuple-element.27), channel_id=1, source_target_pairs={{0,3},{1,0},{2,1},{3,2},{4,7},{5,4},{6,5},{7,6},{8,11},{9,8},{10,9... | collective-permute-start | bytes 589832 | tf_op jit(solution)/shard_map/ppermute | solution.py:258
  143.4 10.6 %collective-permute-start.9 = (bf16[8,24,512]{2,1,0:T(8,128)(2,1)S(1)}, bf16[8,24,512]{2,1,0:T(8,128)(2,1)S(1)}, u32[]{:S(2)}, u32[]{:S(2)}) collective-permute-start(bf16[8,24,512]{2,1,0:T(8,128)(2,1)S(1)} %get-tuple-element.28), channel_id=1, source_target_pairs={{0,2},{1,3},{2,0},{3,1},{4,6},{5,7},{6,4},{7,5},{8,10},{9,11},{10,... | collective-permute-start | bytes 589832 | tf_op jit(solution)/shard_map/ppermute | solution.py:258
  147.3 10.4 %collective-permute-start.8 = (bf16[8,24,512]{2,1,0:T(8,128)(2,1)S(1)}, bf16[8,24,512]{2,1,0:T(8,128)(2,1)S(1)}, u32[]{:S(2)}, u32[]{:S(2)}) collective-permute-start(bf16[8,24,512]{2,1,0:T(8,128)(2,1)S(1)} %get-tuple-element.26), channel_id=1, source_target_pairs={{0,1},{1,2},{2,3},{3,0},{4,5},{5,6},{6,7},{7,4},{8,9},{9,10},{10,1... | collective-permute-start | bytes 589832 | tf_op jit(solution)/shard_map/ppermute | solution.py:258
  157.8 13.5 %collective-permute-start.11 = (bf16[192,256]{1,0:T(8,128)(2,1)S(1)}, bf16[192,256]{1,0:T(8,128)(2,1)S(1)}, u32[]{:S(2)}, u32[]{:S(2)}) collective-permute-start(bf16[192,256]{1,0:T(8,128)(2,1)S(1)} %broadcast_select_fusion), channel_id=1, source_target_pairs={{0,4},{4,0},{8,12},{12,8},{16,20},{20,16},{24,28},{28,24},{32,36},... | collective-permute-start | bytes 294920 | tf_op jit(solution)/shard_map/ppermute | solution.py:56
  164.5 17.0 %all-to-all-start.4 = ((bf16[8,12,1024]{2,1,0:T(8,128)(2,1)}), bf16[8,12,1024]{2,1,0:T(8,128)(2,1)S(1)}, u32[]{:S(2)}, u32[]{:S(2)}) async-start(bf16[8,12,1024]{2,1,0:T(8,128)(2,1)} %reshape.96), calls=%async_computation.4 | async-start | bytes 524288 | tf_op jit(solution)/shard_map/all_to_all | solution.py:44

commit v7 on v6

--- a/solution.py
+++ b/solution.py
@@ -253,12 +253,15 @@
     return [(i, (i + distance) % 4) for i in range(4)]
 
 
-def summed_share(y_split):
+def summed_share(y_split, after=None):
     total = y_split[0].astype(f32)
     got = [lax.ppermute(y_split[k], "tp", share_route(k)) for k in range(1, 4)]
+    if after is not None:
+        got, after = lax.optimization_barrier((got, after))
     for part in got:
         total = total + part.astype(f32)
-    return total.astype(bf16)
+    total = total.astype(bf16)
+    return total if after is None else (total, after)
 
 
 def spread_of(core):
@@ -294,13 +297,14 @@
     wide = jnp.concatenate([attended, slot_lanes], 1)
     buckets = dot(pick, wide, ((1,), (0,))).astype(bf16)
     buckets = buckets.reshape(devices // 2, 2 * GROUP_ROWS, -1)
-    buckets, half_proj = lax.optimization_barrier((buckets, half_proj))
-    arrived = exchange(buckets, SAME_CORE)
-    y_split = project(place, attended, partner, half_proj, False)
-    y_split, target_row = lax.optimization_barrier((y_split, target_row))
     mine, theirs = spread_of(core), spread_of(1 - core)
     target_own, target_other = targets_of(target_row, student_states, mine, theirs)
     target_other = other_core(target_other)
+    buckets, half_proj, partner, target_own, target_other = lax.optimization_barrier(
+        (buckets, half_proj, partner, target_own, target_other)
+    )
+    arrived = exchange(buckets, SAME_CORE)
+    y_split = project(place, attended, partner, half_proj, False)
     y_teacher = summed_share(y_split)
     parts = [y_teacher]
     for distance in range(1, shares):
@@ -311,12 +315,13 @@
     targets = (target_own, target_other)
     term = term_of(place, parts, targets, attended, partner, own, other)
     far = exchange(term, FAR)
+    y_split = project(place, own, other, half_proj, True)
+    y_rows, far = summed_share(y_split, far)
+    y_rows = y_rows.reshape(-1, 2 * rows)
     far = jnp.sum(far.astype(f32), axis=0).astype(bf16)
     last = exchange(far.reshape(SIDE, feats, -1), NEAR)
     norm_factor = 1.0 / math.sqrt(rows * devices)
     grad = jnp.sum(last.astype(f32), axis=0) * norm_factor
-    y_split = project(place, own, other, half_proj, True)
-    y_rows = summed_share(y_split).reshape(-1, 2 * rows)
     first, second = y_rows[:, :rows], y_rows[:, rows:]
     rest = other_core(jnp.where(core == 0, second, first))
     out_rows = dot(jnp.where(core == 0, first, second), mine, ((0,), (1,)))

time: 183 us -> 188 us (1.027)
  waiting for transfers between devices: 69 us -> 51.3 us
  starting transfers between devices: 80.2 us -> 91.9 us
  local copies, waits for them, and re-layouts: 6.16 us -> 17.8 us
    unnamed x20 -> x42, local copies, waits for them, and re-layouts: 2.3 us -> 13.9 us
    all_to_all x5, waiting for transfers between devices: 35.2 us -> 24.9 us  [exchange(): lax.all_to_all(block, axis, split_axis=0, concat_axis=0, tiled=True, axis...]
    ppermute x4, starting transfers between devices: 8.17 us -> 18.1 us  [other_core(): lax.ppermute(block, 'seq', [(i, i ^ 1) for i in range(lax.axis_size('seq'...]
    ppermute x2, waiting for transfers between devices: 5.34 us -> 0.01 us  [passed_along(): return lax.ppermute(block, axis, route)]
  transfers between devices with their start and end apart: 20 -> 20, of which waited for: 13 -> 11; matrix products, arithmetic and copies ran while one was open for 3% -> 3% of each run, Pallas kernels for 8% -> 7%
where the time goes in v7:
time: 188 us; the launch traced here: 186 us
  starting transfers between devices  91.9 us (49%)
  waiting for transfers between devices  51.3 us (27%)
  Pallas kernels  18.6 us (10%)
  local copies, waits for them, and re-layouts  17.8 us (9%)
  other arithmetic  2.99 us (2%)
  matrix products  2.78 us (1%)
    all_to_all x5, starting transfers between devices, exchange(): lax.all_to_all(block, axis, split_axis=0, concat_axis=0, tiled=True, axis...  38.3 us
    all_to_all x5, waiting for transfers between devices, exchange(): lax.all_to_all(block, axis, split_axis=0, concat_axis=0, tiled=True, axis...  24.9 us
    ppermute x6, starting transfers between devices, summed_share(): got = [lax.ppermute(y_split[k], 'tp', share_route(k)) for k in range(1, 4)]  20.8 us
    ppermute x4, starting transfers between devices, other_core(): lax.ppermute(block, 'seq', [(i, i ^ 1) for i in range(lax.axis_size('seq'...  18.1 us
    unnamed x42, local copies, waits for them, and re-layouts  13.9 us
    ppermute x3, waiting for transfers between devices, on_device(): parts.append(lax.ppermute(y_teacher, 'tp', share_route(distance)))  13.7 us
    ppermute x6, waiting for transfers between devices, summed_share(): got = [lax.ppermute(y_split[k], 'tp', share_route(k)) for k in range(1, 4)]  12.6 us
    ppermute x3, starting transfers between devices, on_device(): parts.append(lax.ppermute(y_teacher, 'tp', share_route(distance)))  10.9 us
  transfers between devices with their start and end apart: 20, of which 11 were waited for; matrix products, arithmetic and copies ran while one was open for 3% of the time, Pallas kernels for 7%

profile of v7, /device:TPU:2, one launch (start us, length us, event | category | flops | bytes accessed | tf_op | source)
XLA Modules:
  0.0 186.4 jit_solution(5788807468246853106)
XLA Ops:
  2.1 7.1 %all-to-all-start = ((bf16[8,12,1024]{2,1,0:T(8,128)(2,1)}), bf16[8,12,1024]{2,1,0:T(8,128)(2,1)S(1)}, u32[]{:S(2)}, u32[]{:S(2)}) async-start(bf16[8,12,1024]{2,1,0:T(8,128)(2,1)} %broadcast_in_dim.8), calls=%async_computation | async-start | bytes 524288 | tf_op jit(solution)/shard_map/all_to_all | solution.py:44
  9.3 10.4 %all-to-all-done = bf16[8,12,1024]{2,1,0:T(8,128)(2,1)S(1)} async-done(((bf16[8,12,1024]{2,1,0:T(8,128)(2,1)}), bf16[8,12,1024]{2,1,0:T(8,128)(2,1)S(1)}, u32[]{:S(2)}, u32[]{:S(2)}) %all-to-all-start) | async-done | bytes 196640 | tf_op jit(solution)/shard_map/all_to_all | solution.py:44
  21.1 10.5 %all-to-all-start.1 = ((bf16[8,96,1024]{2,1,0:T(8,128)(2,1)}), bf16[8,96,1024]{2,1,0:T(8,128)(2,1)S(1)}, u32[]{:S(2)}, u32[]{:S(2)}) async-start(bf16[8,96,1024]{2,1,0:T(8,128)(2,1)} %broadcast_in_dim.11), calls=%async_computation.1 | async-start | bytes 3145728 | tf_op jit(solution)/shard_map/all_to_all | solution.py:44
  31.8 2.5 %collective-permute-start = (bf16[528,128]{1,0:T(8,128)(2,1)S(1)}, bf16[528,128]{1,0:T(8,128)(2,1)S(1)}, u32[]{:S(2)}, u32[]{:S(2)}) collective-permute-start(bf16[528,128]{1,0:T(8,128)(2,1)S(1)} %maximum_maximum_fusion.b0_ref), channel_id=1, source_target_pairs={{0,8},{4,12},{8,16},{12,20},{16,24},{20,28},{24,32},{28,36},{32,40... | collective-permute-start | bytes 405512 | tf_op jit(solution)/shard_map/ppermute | solution.py:52
  38.6 2.9 %collective-permute-start.3 = (bf16[32,24,256]{2,1,0:T(8,128)(2,1)S(1)}, bf16[32,24,256]{2,1,0:T(8,128)(2,1)S(1)}, u32[]{:S(2)}, u32[]{:S(2)}) collective-permute-start(bf16[32,24,256]{2,1,0:T(8,128)(2,1)S(1)} %get-tuple-element.22), channel_id=1, source_target_pairs={{0,4},{4,0},{8,12},{12,8},{16,20},{20,16},{24,28},{28,24},{32,36},... | collective-permute-start | bytes 1179656 | tf_op jit(solution)/shard_map/ppermute | solution.py:56
  45.7 4.6 %attend.1.own_ref.refs_6_ = bf16[256,1024]{1,0:T(8,128)(2,1)S(1)} custom-call(bf16[256,1024]{1,0:T(8,128)(2,1)S(1)} %copy-done.11, bf16[528,128]{1,0:T(8,128)(2,1)S(1)} %copy-done.13, bf16[528,128]{1,0:T(8,128)(2,1)S(1)} %copy-done.15, bf16[528,128]{1,0:T(8,128)(2,1)S(1)} %maximum_maximum_fusion.b0_ref), custom_call_target="tpu_custom_call" | custom-call | flops 805306368 | bytes 2097152 | tf_op jit(solution)/shard_map/attend/pallas_call | solution.py:101
  50.2 11.4 %collective-permute-start.2 = (bf16[256,1024]{1,0:T(8,128)(2,1)S(1)}, bf16[256,1024]{1,0:T(8,128)(2,1)S(1)}, u32[]{:S(2)}, u32[]{:S(2)}) collective-permute-start(bf16[256,1024]{1,0:T(8,128)(2,1)S(1)} %attend.1.own_ref.refs_6_), channel_id=1, source_target_pairs={{0,4},{4,0},{8,12},{12,8},{16,20},{20,16},{24,28},{28,24},{32,36},... | collective-permute-start | bytes 1572872 | tf_op jit(solution)/shard_map/ppermute | solution.py:56
  64.8 9.6 %all-to-all-start.2 = ((bf16[64,8,1152]{2,1,0:T(8,128)(2,1)}), bf16[64,8,1152]{2,1,0:T(8,128)(2,1)}, u32[]{:S(2)}, u32[]{:S(2)}) async-start(bf16[64,8,1152]{2,1,0:T(8,128)(2,1)} %fusion), calls=%async_computation.2 | async-start | bytes 2359296 | tf_op jit(solution)/shard_map/all_to_all | solution.py:44
  75.5 3.2 %shard_map.95 = bf16[4,8,24,512]{3,2,1,0:T(8,128)(2,1)S(1)} custom-call(s32[2]{0:T(128)S(1)} %pad_add_fusion.place_ref, bf16[256,1024]{1,0:T(8,128)(2,1)S(1)} %attend.1.own_ref.refs_6_, bf16[256,1024]{1,0:T(8,128)(2,1)S(1)} %copy-done.4, bf16[768,1024]{1,0:T(8,128)(2,1)S(1)} %bitcast.32), custom_call_target="tpu_custom_call" | custom-call | flops 805306368 | bytes 4194304 | tf_op jit(solution)/shard_map/pallas_call | solution.py:175
  78.7 2.4 %collective-permute-start.6 = (bf16[8,24,512]{2,1,0:T(8,128)(2,1)S(1)}, bf16[8,24,512]{2,1,0:T(8,128)(2,1)S(1)}, u32[]{:S(2)}, u32[]{:S(2)}) collective-permute-start(bf16[8,24,512]{2,1,0:T(8,128)(2,1)S(1)} %get-tuple-element.40), channel_id=1, source_target_pairs={{0,3},{1,0},{2,1},{3,2},{4,7},{5,4},{6,5},{7,6},{8,11},{9,8},{10,9... | collective-permute-start | bytes 589832 | tf_op jit(solution)/shard_map/ppermute | solution.py:258
  81.2 4.3 %collective-permute-start.5 = (bf16[8,24,512]{2,1,0:T(8,128)(2,1)S(1)}, bf16[8,24,512]{2,1,0:T(8,128)(2,1)S(1)}, u32[]{:S(2)}, u32[]{:S(2)}) collective-permute-start(bf16[8,24,512]{2,1,0:T(8,128)(2,1)S(1)} %get-tuple-element.41), channel_id=1, source_target_pairs={{0,2},{1,3},{2,0},{3,1},{4,6},{5,7},{6,4},{7,5},{8,10},{9,11},{10,... | collective-permute-start | bytes 589832 | tf_op jit(solution)/shard_map/ppermute | solution.py:258
  85.5 3.7 %collective-permute-start.4 = (bf16[8,24,512]{2,1,0:T(8,128)(2,1)S(1)}, bf16[8,24,512]{2,1,0:T(8,128)(2,1)S(1)}, u32[]{:S(2)}, u32[]{:S(2)}) collective-permute-start(bf16[8,24,512]{2,1,0:T(8,128)(2,1)S(1)} %get-tuple-element.39), channel_id=1, source_target_pairs={{0,1},{1,2},{2,3},{3,0},{4,5},{5,6},{6,7},{7,4},{8,9},{9,10},{10,1... | collective-permute-start | bytes 589832 | tf_op jit(solution)/shard_map/ppermute | solution.py:258
  89.3 3.5 %collective-permute-done.5 = bf16[8,24,512]{2,1,0:T(8,128)(2,1)S(1)} collective-permute-done((bf16[8,24,512]{2,1,0:T(8,128)(2,1)S(1)}, bf16[8,24,512]{2,1,0:T(8,128)(2,1)S(1)}, u32[]{:S(2)}, u32[]{:S(2)}) %collective-permute-start.5) | collective-permute-done | bytes 196640 | tf_op jit(solution)/shard_map/ppermute | solution.py:258
  92.8 2.8 %collective-permute-done.4 = bf16[8,24,512]{2,1,0:T(8,128)(2,1)S(1)} collective-permute-done((bf16[8,24,512]{2,1,0:T(8,128)(2,1)S(1)}, bf16[8,24,512]{2,1,0:T(8,128)(2,1)S(1)}, u32[]{:S(2)}, u32[]{:S(2)}) %collective-permute-start.4) | collective-permute-done | bytes 196640 | tf_op jit(solution)/shard_map/ppermute | solution.py:258
  95.7 3.4 %collective-permute-start.7 = (bf16[8,24,512]{2,1,0:T(8,128)(2,1)S(1)}, bf16[8,24,512]{2,1,0:T(8,128)(2,1)S(1)}, u32[]{:S(2)}, u32[]{:S(2)}) collective-permute-start(bf16[8,24,512]{2,1,0:T(8,128)(2,1)S(1)} %fusion.10.refs_0_), channel_id=1, source_target_pairs={{0,1},{1,2},{2,3},{3,0},{4,5},{5,6},{6,7},{7,4},{8,9},{9,10},{10,1... | collective-permute-start | bytes 589832 | tf_op jit(solution)/shard_map/ppermute | solution.py:311
  99.1 6.4 %collective-permute-done.7.refs_1_ = bf16[8,24,512]{2,1,0:T(8,128)(2,1)S(1)} collective-permute-done((bf16[8,24,512]{2,1,0:T(8,128)(2,1)S(1)}, bf16[8,24,512]{2,1,0:T(8,128)(2,1)S(1)}, u32[]{:S(2)}, u32[]{:S(2)}) %collective-permute-start.7) | collective-permute-done | bytes 196640 | tf_op jit(solution)/shard_map/ppermute | solution.py:311
  107.2 2.1 %place.1.own_ref.refs_8_ = bf16[512,1024]{1,0:T(8,128)(2,1)S(1)} custom-call(bf16[64,8,1152]{2,1,0:T(8,128)(2,1)} %all-to-all-done.2.in_ref), custom_call_target="tpu_custom_call" | custom-call | flops 536870912 | bytes 3145728 | tf_op jit(solution)/shard_map/place/pallas_call | solution.py:145
  111.2 4.0 %collective-permute-start.12 = (bf16[8,24,512]{2,1,0:T(8,128)(2,1)S(1)}, bf16[8,24,512]{2,1,0:T(8,128)(2,1)S(1)}, u32[]{:S(2)}, u32[]{:S(2)}) collective-permute-start(bf16[8,24,512]{2,1,0:T(8,128)(2,1)S(1)} %fusion.10.refs_0_), channel_id=1, source_target_pairs={{0,2},{1,3},{2,0},{3,1},{4,6},{5,7},{6,4},{7,5},{8,10},{9,11},{10,... | collective-permute-start | bytes 589832 | tf_op jit(solution)/shard_map/ppermute | solution.py:311
  115.3 3.5 %collective-permute-start.13 = (bf16[8,24,512]{2,1,0:T(8,128)(2,1)S(1)}, bf16[8,24,512]{2,1,0:T(8,128)(2,1)S(1)}, u32[]{:S(2)}, u32[]{:S(2)}) collective-permute-start(bf16[8,24,512]{2,1,0:T(8,128)(2,1)S(1)} %fusion.10.refs_0_), channel_id=1, source_target_pairs={{0,3},{1,0},{2,1},{3,2},{4,7},{5,4},{6,5},{7,6},{8,11},{9,8},{10,9... | collective-permute-start | bytes 589832 | tf_op jit(solution)/shard_map/ppermute | solution.py:311
  118.8 3.6 %collective-permute-done.12.refs_2_ = bf16[8,24,512]{2,1,0:T(8,128)(2,1)S(1)} collective-permute-done((bf16[8,24,512]{2,1,0:T(8,128)(2,1)S(1)}, bf16[8,24,512]{2,1,0:T(8,128)(2,1)S(1)}, u32[]{:S(2)}, u32[]{:S(2)}) %collective-permute-start.12) | collective-permute-done | bytes 196640 | tf_op jit(solution)/shard_map/ppermute | solution.py:311
  122.4 3.7 %collective-permute-done.13.refs_3_ = bf16[8,24,512]{2,1,0:T(8,128)(2,1)S(1)} collective-permute-done((bf16[8,24,512]{2,1,0:T(8,128)(2,1)S(1)}, bf16[8,24,512]{2,1,0:T(8,128)(2,1)S(1)}, u32[]{:S(2)}, u32[]{:S(2)}) %collective-permute-start.13) | collective-permute-done | bytes 196640 | tf_op jit(solution)/shard_map/ppermute | solution.py:311
  129.2 3.6 %term.1 = bf16[8,96,1024]{2,1,0:T(8,128)(2,1)S(1)} custom-call(s32[2]{0:T(128)S(1)} %pad_add_fusion.place_ref, bf16[8,24,512]{2,1,0:T(8,128)(2,1)S(1)} %fusion.10.refs_0_, bf16[8,24,512]{2,1,0:T(8,128)(2,1)S(1)} %collective-permute-done.7.refs_1_, bf16[8,24,512]{2,1,0:T(8,128)(2,1)S(1)} %collective-permute-done.12.refs_2_, ...), custom_call_target="tpu_custom_call" | custom-call | flops 1610612736 | bytes 8388608 | tf_op jit(solution)/shard_map/term/pallas_call | solution.py:238
  134.9 4.5 %all-to-all-start.3 = ((bf16[8,96,1024]{2,1,0:T(8,128)(2,1)}), bf16[8,96,1024]{2,1,0:T(8,128)(2,1)}, u32[]{:S(2)}, u32[]{:S(2)}) async-start(bf16[8,96,1024]{2,1,0:T(8,128)(2,1)} %copy-done), calls=%async_computation.3 | async-start | bytes 3145728 | tf_op jit(solution)/shard_map/all_to_all | solution.py:44
  140.6 3.2 %shard_map.96 = bf16[4,8,24,512]{3,2,1,0:T(8,128)(2,1)S(1)} custom-call(s32[2]{0:T(128)S(1)} %pad_add_fusion.place_ref, bf16[512,1024]{1,0:T(8,128)(2,1)S(1)} %place.1.own_ref.refs_8_, bf16[512,1024]{1,0:T(8,128)(2,1)S(1)} %copy-done.2, bf16[768,1024]{1,0:T(8,128)(2,1)S(1)} %bitcast.33), custom_call_target="tpu_custom_call" | custom-call | flops 805306368 | bytes 4194304 | tf_op jit(solution)/shard_map/pallas_call | solution.py:175
  143.8 2.5 %collective-permute-start.9 = (bf16[8,24,512]{2,1,0:T(8,128)(2,1)S(1)}, bf16[8,24,512]{2,1,0:T(8,128)(2,1)S(1)}, u32[]{:S(2)}, u32[]{:S(2)}) collective-permute-start(bf16[8,24,512]{2,1,0:T(8,128)(2,1)S(1)} %get-tuple-element.38), channel_id=1, source_target_pairs={{0,1},{1,2},{2,3},{3,0},{4,5},{5,6},{6,7},{7,4},{8,9},{9,10},{10,1... | collective-permute-start | bytes 589832 | tf_op jit(solution)/shard_map/ppermute | solution.py:258
  146.3 3.9 %collective-permute-start.10 = (bf16[8,24,512]{2,1,0:T(8,128)(2,1)S(1)}, bf16[8,24,512]{2,1,0:T(8,128)(2,1)S(1)}, u32[]{:S(2)}, u32[]{:S(2)}) collective-permute-start(bf16[8,24,512]{2,1,0:T(8,128)(2,1)S(1)} %get-tuple-element.37), channel_id=1, source_target_pairs={{0,2},{1,3},{2,0},{3,1},{4,6},{5,7},{6,4},{7,5},{8,10},{9,11},{10,... | collective-permute-start | bytes 589832 | tf_op jit(solution)/shard_map/ppermute | solution.py:258
  150.2 4.0 %collective-permute-start.11 = (bf16[8,24,512]{2,1,0:T(8,128)(2,1)S(1)}, bf16[8,24,512]{2,1,0:T(8,128)(2,1)S(1)}, u32[]{:S(2)}, u32[]{:S(2)}) collective-permute-start(bf16[8,24,512]{2,1,0:T(8,128)(2,1)S(1)} %get-tuple-element.36), channel_id=1, source_target_pairs={{0,3},{1,0},{2,1},{3,2},{4,7},{5,4},{6,5},{7,6},{8,11},{9,8},{10,9... | collective-permute-start | bytes 589832 | tf_op jit(solution)/shard_map/ppermute | solution.py:258
  154.2 3.3 %collective-permute-done.10 = bf16[8,24,512]{2,1,0:T(8,128)(2,1)S(1)} collective-permute-done((bf16[8,24,512]{2,1,0:T(8,128)(2,1)S(1)}, bf16[8,24,512]{2,1,0:T(8,128)(2,1)S(1)}, u32[]{:S(2)}, u32[]{:S(2)}) %collective-permute-start.10) | collective-permute-done | bytes 196640 | tf_op jit(solution)/shard_map/ppermute | solution.py:258
  157.5 3.0 %collective-permute-done.11 = bf16[8,24,512]{2,1,0:T(8,128)(2,1)S(1)} collective-permute-done((bf16[8,24,512]{2,1,0:T(8,128)(2,1)S(1)}, bf16[8,24,512]{2,1,0:T(8,128)(2,1)S(1)}, u32[]{:S(2)}, u32[]{:S(2)}) %collective-permute-start.11) | collective-permute-done | bytes 196640 | tf_op jit(solution)/shard_map/ppermute | solution.py:258
  160.5 3.5 %all-to-all-done.3 = bf16[8,96,1024]{2,1,0:T(8,128)(2,1)} async-done(((bf16[8,96,1024]{2,1,0:T(8,128)(2,1)}), bf16[8,96,1024]{2,1,0:T(8,128)(2,1)}, u32[]{:S(2)}, u32[]{:S(2)}) %all-to-all-start.3) | async-done | bytes 1572896 | tf_op jit(solution)/shard_map/all_to_all | solution.py:44
  168.5 6.7 %all-to-all-start.4 = ((bf16[8,12,1024]{2,1,0:T(8,128)(2,1)}), bf16[8,12,1024]{2,1,0:T(8,128)(2,1)S(1)}, u32[]{:S(2)}, u32[]{:S(2)}) async-start(bf16[8,12,1024]{2,1,0:T(8,128)(2,1)} %reshape.96), calls=%async_computation.4 | async-start | bytes 524288 | tf_op jit(solution)/shard_map/all_to_all | solution.py:44
  176.4 9.2 %all-to-all-done.4 = bf16[8,12,1024]{2,1,0:T(8,128)(2,1)S(1)} async-done(((bf16[8,12,1024]{2,1,0:T(8,128)(2,1)}), bf16[8,12,1024]{2,1,0:T(8,128)(2,1)S(1)}, u32[]{:S(2)}, u32[]{:S(2)}) %all-to-all-start.4) | async-done | bytes 196640 | tf_op jit(solution)/shard_map/all_to_all | solution.py:44
  (82 shorter events, 32.5 us)
Async XLA Ops:
  2.1 17.6 %all-to-all-start = ((bf16[8,12,1024]{2,1,0:T(8,128)(2,1)}), bf16[8,12,1024]{2,1,0:T(8,128)(2,1)S(1)}, u32[]{:S(2)}, u32[]{:S(2)}) async-start(bf16[8,12,1024]{2,1,0:T(8,128)(2,1)} %broadcast_in_dim.8), calls=%async_computation | async-start | bytes 524288 | tf_op jit(solution)/shard_map/all_to_all | solution.py:44
  21.1 10.6 %copy-start.20 = (s32[256]{0:T(256)S(1)}, s32[256]{0:T(256)}, u32[]{:S(2)}) copy-start(s32[256]{0:T(256)} %param.11) | copy-start | bytes 3076
  21.1 10.6 %copy-start.17 = (bf16[256,128]{1,0:T(8,128)(2,1)S(1)}, bf16[256,128]{1,0:T(8,128)(2,1)}, u32[]{:S(2)}) copy-start(bf16[256,128]{1,0:T(8,128)(2,1)} %param.10) | copy-start | bytes 196612
  21.1 10.6 %copy-start.18 = (bf16[256,128]{1,0:T(8,128)(2,1)S(1)}, bf16[256,128]{1,0:T(8,128)(2,1)}, u32[]{:S(2)}) copy-start(bf16[256,128]{1,0:T(8,128)(2,1)} %param.9) | copy-start | bytes 196612
  21.1 14.7 %copy-start.10 = (bf16[256,1536]{1,0:T(8,128)(2,1)S(1)}, bf16[256,1536]{1,0:T(8,128)(2,1)}, u32[]{:S(2)}) copy-start(bf16[256,1536]{1,0:T(8,128)(2,1)} %states_ref.1) | copy-start | bytes 2359300
  21.1 14.7 %copy-start.16 = (s32[256]{0:T(256)S(1)}, s32[256]{0:T(256)}, u32[]{:S(2)}) copy-start(s32[256]{0:T(256)} %param.15) | copy-start | bytes 3076
  21.1 42.9 %all-to-all-start.1 = ((bf16[8,96,1024]{2,1,0:T(8,128)(2,1)}), bf16[8,96,1024]{2,1,0:T(8,128)(2,1)S(1)}, u32[]{:S(2)}, u32[]{:S(2)}) async-start(bf16[8,96,1024]{2,1,0:T(8,128)(2,1)} %broadcast_in_dim.11), calls=%async_computation.1 | async-start | bytes 3145728 | tf_op jit(solution)/shard_map/all_to_all | solution.py:44
  31.8 9.6 %collective-permute-start = (bf16[528,128]{1,0:T(8,128)(2,1)S(1)}, bf16[528,128]{1,0:T(8,128)(2,1)S(1)}, u32[]{:S(2)}, u32[]{:S(2)}) collective-permute-start(bf16[528,128]{1,0:T(8,128)(2,1)S(1)} %maximum_maximum_fusion.b0_ref), channel_id=1, source_target_pairs={{0,8},{4,12},{8,16},{12,20},{16,24},{20,28},{24,32},{28,36},{32,40... | collective-permute-start | bytes 405512 | tf_op jit(solution)/shard_map/ppermute | solution.py:52
  34.3 7.8 %collective-permute-start.1 = (bf16[528,128]{1,0:T(8,128)(2,1)S(1)}, bf16[528,128]{1,0:T(8,128)(2,1)S(1)}, u32[]{:S(2)}, u32[]{:S(2)}) collective-permute-start(bf16[528,128]{1,0:T(8,128)(2,1)S(1)} %maximum_maximum_fusion.b0_ref), channel_id=1, source_target_pairs={{0,4},{4,8},{8,12},{12,16},{16,20},{20,24},{24,28},{28,32},{32,36}... | collective-permute-start | bytes 405512 | tf_op jit(solution)/shard_map/ppermute | solution.py:52
  38.5 23.0 %copy-start.19 = (s32[256]{0:T(256)S(1)}, s32[256]{0:T(256)}, u32[]{:S(2)}) copy-start(s32[256]{0:T(256)} %param.12) | copy-start | bytes 3076
  38.6 24.7 %collective-permute-start.3 = (bf16[32,24,256]{2,1,0:T(8,128)(2,1)S(1)}, bf16[32,24,256]{2,1,0:T(8,128)(2,1)S(1)}, u32[]{:S(2)}, u32[]{:S(2)}) collective-permute-start(bf16[32,24,256]{2,1,0:T(8,128)(2,1)S(1)} %get-tuple-element.22), channel_id=1, source_target_pairs={{0,4},{4,0},{8,12},{12,8},{16,20},{20,16},{24,28},{28,24},{32,36},... | collective-permute-start | bytes 1179656 | tf_op jit(solution)/shard_map/ppermute | solution.py:56
  42.8 1.0 copy-start.11
  50.2 13.8 %collective-permute-start.2 = (bf16[256,1024]{1,0:T(8,128)(2,1)S(1)}, bf16[256,1024]{1,0:T(8,128)(2,1)S(1)}, u32[]{:S(2)}, u32[]{:S(2)}) collective-permute-start(bf16[256,1024]{1,0:T(8,128)(2,1)S(1)} %attend.1.own_ref.refs_6_), channel_id=1, source_target_pairs={{0,4},{4,0},{8,12},{12,8},{16,20},{20,16},{24,28},{28,24},{32,36},... | collective-permute-start | bytes 1572872 | tf_op jit(solution)/shard_map/ppermute | solution.py:56
  64.8 42.4 %all-to-all-start.2 = ((bf16[64,8,1152]{2,1,0:T(8,128)(2,1)}), bf16[64,8,1152]{2,1,0:T(8,128)(2,1)}, u32[]{:S(2)}, u32[]{:S(2)}) async-start(bf16[64,8,1152]{2,1,0:T(8,128)(2,1)} %fusion), calls=%async_computation.2 | async-start | bytes 2359296 | tf_op jit(solution)/shard_map/all_to_all | solution.py:44
  74.4 1.0 copy-start.4
  78.7 10.5 %collective-permute-start.6 = (bf16[8,24,512]{2,1,0:T(8,128)(2,1)S(1)}, bf16[8,24,512]{2,1,0:T(8,128)(2,1)S(1)}, u32[]{:S(2)}, u32[]{:S(2)}) collective-permute-start(bf16[8,24,512]{2,1,0:T(8,128)(2,1)S(1)} %get-tuple-element.40), channel_id=1, source_target_pairs={{0,3},{1,0},{2,1},{3,2},{4,7},{5,4},{6,5},{7,6},{8,11},{9,8},{10,9... | collective-permute-start | bytes 589832 | tf_op jit(solution)/shard_map/ppermute | solution.py:258
  81.2 11.6 %collective-permute-start.5 = (bf16[8,24,512]{2,1,0:T(8,128)(2,1)S(1)}, bf16[8,24,512]{2,1,0:T(8,128)(2,1)S(1)}, u32[]{:S(2)}, u32[]{:S(2)}) collective-permute-start(bf16[8,24,512]{2,1,0:T(8,128)(2,1)S(1)} %get-tuple-element.41), channel_id=1, source_target_pairs={{0,2},{1,3},{2,0},{3,1},{4,6},{5,7},{6,4},{7,5},{8,10},{9,11},{10,... | collective-permute-start | bytes 589832 | tf_op jit(solution)/shard_map/ppermute | solution.py:258
  85.5 10.0 %collective-permute-start.4 = (bf16[8,24,512]{2,1,0:T(8,128)(2,1)S(1)}, bf16[8,24,512]{2,1,0:T(8,128)(2,1)S(1)}, u32[]{:S(2)}, u32[]{:S(2)}) collective-permute-start(bf16[8,24,512]{2,1,0:T(8,128)(2,1)S(1)} %get-tuple-element.39), channel_id=1, source_target_pairs={{0,1},{1,2},{2,3},{3,0},{4,5},{5,6},{6,7},{7,4},{8,9},{9,10},{10,1... | collective-permute-start | bytes 589832 | tf_op jit(solution)/shard_map/ppermute | solution.py:258
  95.7 9.8 %collective-permute-start.7 = (bf16[8,24,512]{2,1,0:T(8,128)(2,1)S(1)}, bf16[8,24,512]{2,1,0:T(8,128)(2,1)S(1)}, u32[]{:S(2)}, u32[]{:S(2)}) collective-permute-start(bf16[8,24,512]{2,1,0:T(8,128)(2,1)S(1)} %fusion.10.refs_0_), channel_id=1, source_target_pairs={{0,1},{1,2},{2,3},{3,0},{4,5},{5,6},{6,7},{7,4},{8,9},{9,10},{10,1... | collective-permute-start | bytes 589832 | tf_op jit(solution)/shard_map/ppermute | solution.py:311
  109.3 16.8 %collective-permute-start.8 = (bf16[512,1024]{1,0:T(8,128)(2,1)S(1)}, bf16[512,1024]{1,0:T(8,128)(2,1)S(1)}, u32[]{:S(2)}, u32[]{:S(2)}) collective-permute-start(bf16[512,1024]{1,0:T(8,128)(2,1)S(1)} %place.1.own_ref.refs_8_), channel_id=1, source_target_pairs={{0,4},{4,0},{8,12},{12,8},{16,20},{20,16},{24,28},{28,24},{32,36},... | collective-permute-start | bytes 3145736 | tf_op jit(solution)/shard_map/ppermute | solution.py:56
  111.2 11.2 %collective-permute-start.12 = (bf16[8,24,512]{2,1,0:T(8,128)(2,1)S(1)}, bf16[8,24,512]{2,1,0:T(8,128)(2,1)S(1)}, u32[]{:S(2)}, u32[]{:S(2)}) collective-permute-start(bf16[8,24,512]{2,1,0:T(8,128)(2,1)S(1)} %fusion.10.refs_0_), channel_id=1, source_target_pairs={{0,2},{1,3},{2,0},{3,1},{4,6},{5,7},{6,4},{7,5},{8,10},{9,11},{10,... | collective-permute-start | bytes 589832 | tf_op jit(solution)/shard_map/ppermute | solution.py:311
  115.3 10.9 %collective-permute-start.13 = (bf16[8,24,512]{2,1,0:T(8,128)(2,1)S(1)}, bf16[8,24,512]{2,1,0:T(8,128)(2,1)S(1)}, u32[]{:S(2)}, u32[]{:S(2)}) collective-permute-start(bf16[8,24,512]{2,1,0:T(8,128)(2,1)S(1)} %fusion.10.refs_0_), channel_id=1, source_target_pairs={{0,3},{1,0},{2,1},{3,2},{4,7},{5,4},{6,5},{7,6},{8,11},{9,8},{10,9... | collective-permute-start | bytes 589832 | tf_op jit(solution)/shard_map/ppermute | solution.py:311
  126.2 1.0 copy-start.5
  128.2 1.0 copy-start.9
  132.7 1.2 copy-start
  134.9 29.1 %all-to-all-start.3 = ((bf16[8,96,1024]{2,1,0:T(8,128)(2,1)}), bf16[8,96,1024]{2,1,0:T(8,128)(2,1)}, u32[]{:S(2)}, u32[]{:S(2)}) async-start(bf16[8,96,1024]{2,1,0:T(8,128)(2,1)} %copy-done), calls=%async_computation.3 | async-start | bytes 3145728 | tf_op jit(solution)/shard_map/all_to_all | solution.py:44
  139.4 1.2 copy-start.2
  143.8 10.4 %collective-permute-start.9 = (bf16[8,24,512]{2,1,0:T(8,128)(2,1)S(1)}, bf16[8,24,512]{2,1,0:T(8,128)(2,1)S(1)}, u32[]{:S(2)}, u32[]{:S(2)}) collective-permute-start(bf16[8,24,512]{2,1,0:T(8,128)(2,1)S(1)} %get-tuple-element.38), channel_id=1, source_target_pairs={{0,1},{1,2},{2,3},{3,0},{4,5},{5,6},{6,7},{7,4},{8,9},{9,10},{10,1... | collective-permute-start | bytes 589832 | tf_op jit(solution)/shard_map/ppermute | solution.py:258
  146.3 11.2 %collective-permute-start.10 = (bf16[8,24,512]{2,1,0:T(8,128)(2,1)S(1)}, bf16[8,24,512]{2,1,0:T(8,128)(2,1)S(1)}, u32[]{:S(2)}, u32[]{:S(2)}) collective-permute-start(bf16[8,24,512]{2,1,0:T(8,128)(2,1)S(1)} %get-tuple-element.37), channel_id=1, source_target_pairs={{0,2},{1,3},{2,0},{3,1},{4,6},{5,7},{6,4},{7,5},{8,10},{9,11},{10,... | collective-permute-start | bytes 589832 | tf_op jit(solution)/shard_map/ppermute | solution.py:258
  150.2 10.3 %collective-permute-start.11 = (bf16[8,24,512]{2,1,0:T(8,128)(2,1)S(1)}, bf16[8,24,512]{2,1,0:T(8,128)(2,1)S(1)}, u32[]{:S(2)}, u32[]{:S(2)}) collective-permute-start(bf16[8,24,512]{2,1,0:T(8,128)(2,1)S(1)} %get-tuple-element.36), channel_id=1, source_target_pairs={{0,3},{1,0},{2,1},{3,2},{4,7},{5,4},{6,5},{7,6},{8,11},{9,8},{10,9... | collective-permute-start | bytes 589832 | tf_op jit(solution)/shard_map/ppermute | solution.py:258
  164.1 11.4 %collective-permute-start.14 = (bf16[192,256]{1,0:T(8,128)(2,1)S(1)}, bf16[192,256]{1,0:T(8,128)(2,1)S(1)}, u32[]{:S(2)}, u32[]{:S(2)}) collective-permute-start(bf16[192,256]{1,0:T(8,128)(2,1)S(1)} %broadcast_select_fusion), channel_id=1, source_target_pairs={{0,4},{4,0},{8,12},{12,8},{16,20},{20,16},{24,28},{28,24},{32,36},... | collective-permute-start | bytes 294920 | tf_op jit(solution)/shard_map/ppermute | solution.py:56
  168.5 17.2 %all-to-all-start.4 = ((bf16[8,12,1024]{2,1,0:T(8,128)(2,1)}), bf16[8,12,1024]{2,1,0:T(8,128)(2,1)S(1)}, u32[]{:S(2)}, u32[]{:S(2)}) async-start(bf16[8,12,1024]{2,1,0:T(8,128)(2,1)} %reshape.96), calls=%async_computation.4 | async-start | bytes 524288 | tf_op jit(solution)/shard_map/all_to_all | solution.py:44
  (9 other events, 7.4 us)

commit v8 on v7

--- a/solution.py
+++ b/solution.py
@@ -177,7 +177,7 @@
         out_shape=jax.ShapeDtypeStruct((4, 8, 24, rows), bf16),
         in_specs=[SMEM] + [VMEM] * 3,
         out_specs=VMEM,
-        compiler_params=pltpu.CompilerParams(vmem_limit_bytes=16 << 20),
+        compiler_params=pltpu.CompilerParams(vmem_limit_bytes=(56 if add else 16) << 20),
         cost_estimate=pl.CostEstimate(
             flops=2 * 768 * rows * feats, bytes_accessed=4 << 20, transcendentals=0
         ),
@@ -241,7 +241,7 @@
         in_specs=[SMEM] + [VMEM] * 10,
         out_specs=VMEM,
         scratch_shapes=[pltpu.VMEM((4, 8, 24, rows), bf16), pltpu.VMEM((rows, feats), bf16)],
-        compiler_params=pltpu.CompilerParams(vmem_limit_bytes=24 << 20),
+        compiler_params=pltpu.CompilerParams(vmem_limit_bytes=56 << 20),
         cost_estimate=pl.CostEstimate(
             flops=4 * 768 * rows * feats, bytes_accessed=8 << 20, transcendentals=0
         ),
@@ -253,15 +253,12 @@
     return [(i, (i + distance) % 4) for i in range(4)]
 
 
-def summed_share(y_split, after=None):
+def summed_share(y_split):
+    got = [lax.ppermute(y_split[k], "tp", share_route(k)) for k in range(1, 4)]
     total = y_split[0].astype(f32)
-    got = [lax.ppermute(y_split[k], "tp", share_route(k)) for k in range(1, 4)]
-    if after is not None:
-        got, after = lax.optimization_barrier((got, after))
     for part in got:
         total = total + part.astype(f32)
-    total = total.astype(bf16)
-    return total if after is None else (total, after)
+    return total.astype(bf16)
 
 
 def spread_of(core):
@@ -309,14 +306,14 @@
     parts = [y_teacher]
     for distance in range(1, shares):
         parts.append(lax.ppermute(y_teacher, "tp", share_route(distance)))
-    arrived, parts[1] = lax.optimization_barrier((arrived, parts[1]))
+    arrived, parts[0] = lax.optimization_barrier((arrived, parts[0]))
     own = placed_rows(arrived)
     other = other_core(own)
     targets = (target_own, target_other)
     term = term_of(place, parts, targets, attended, partner, own, other)
     far = exchange(term, FAR)
     y_split = project(place, own, other, half_proj, True)
-    y_rows, far = summed_share(y_split, far)
+    y_rows = summed_share(y_split)
     y_rows = y_rows.reshape(-1, 2 * rows)
     far = jnp.sum(far.astype(f32), axis=0).astype(bf16)
     last = exchange(far.reshape(SIDE, feats, -1), NEAR)

time: 188 us -> 184 us (0.979)
  the two profiles are of different devices: /device:TPU:2 before, /device:TPU:1 now
where the time goes in v8:
time: 184 us; the launch traced here: 183 us
  starting transfers between devices  84.5 us (46%)
  waiting for transfers between devices  58.5 us (32%)
  Pallas kernels  22.7 us (12%)
  local copies, waits for them, and re-layouts  11.1 us (6%)
  matrix products  2.78 us (2%)
  other arithmetic  2.51 us (1%)
    all_to_all x5, starting transfers between devices, exchange(): lax.all_to_all(block, axis, split_axis=0, concat_axis=0, tiled=True, axis...  36.9 us
    all_to_all x5, waiting for transfers between devices, exchange(): lax.all_to_all(block, axis, split_axis=0, concat_axis=0, tiled=True, axis...  25.1 us
    ppermute x6, starting transfers between devices, summed_share(): got = [lax.ppermute(y_split[k], 'tp', share_route(k)) for k in range(1, 4)]  19.5 us
    ppermute x6, waiting for transfers between devices, summed_share(): got = [lax.ppermute(y_split[k], 'tp', share_route(k)) for k in range(1, 4)]  17.9 us
    ppermute x4, starting transfers between devices, other_core(): lax.ppermute(block, 'seq', [(i, i ^ 1) for i in range(lax.axis_size('seq'...  10.9 us
    ppermute x3, starting transfers between devices, on_device(): parts.append(lax.ppermute(y_teacher, 'tp', share_route(distance)))  10.7 us
    ppermute x2, waiting for transfers between devices, passed_along(): return lax.ppermute(block, axis, route)  10.1 us
    pallas_call x2, Pallas kernels, project(): pl.pallas_call(functools.partial(project_kernel, add), out_shape=jax.Shap...  8.83 us
  transfers between devices with their start and end apart: 20, of which 12 were waited for; matrix products, arithmetic and copies ran while one was open for 4% of the time, Pallas kernels for 8%

profile of v8, /device:TPU:1, one launch (start us, length us, event | category | flops | bytes accessed | tf_op | source)
XLA Modules:
  0.0 183.2 jit_solution(3794438211893460674)
XLA Ops:
  2.1 10.9 %all-to-all-start = ((bf16[8,12,1024]{2,1,0:T(8,128)(2,1)}), bf16[8,12,1024]{2,1,0:T(8,128)(2,1)S(1)}, u32[]{:S(2)}, u32[]{:S(2)}) async-start(bf16[8,12,1024]{2,1,0:T(8,128)(2,1)} %broadcast_in_dim.8), calls=%async_computation | async-start | bytes 524288 | tf_op jit(solution)/shard_map/all_to_all | solution.py:44
  13.0 9.3 %all-to-all-done = bf16[8,12,1024]{2,1,0:T(8,128)(2,1)S(1)} async-done(((bf16[8,12,1024]{2,1,0:T(8,128)(2,1)}), bf16[8,12,1024]{2,1,0:T(8,128)(2,1)S(1)}, u32[]{:S(2)}, u32[]{:S(2)}) %all-to-all-start) | async-done | bytes 196640 | tf_op jit(solution)/shard_map/all_to_all | solution.py:44
  23.8 6.9 %all-to-all-start.1 = ((bf16[8,96,1024]{2,1,0:T(8,128)(2,1)}), bf16[8,96,1024]{2,1,0:T(8,128)(2,1)S(1)}, u32[]{:S(2)}, u32[]{:S(2)}) async-start(bf16[8,96,1024]{2,1,0:T(8,128)(2,1)} %broadcast_in_dim.11), calls=%async_computation.1 | async-start | bytes 3145728 | tf_op jit(solution)/shard_map/all_to_all | solution.py:44
  31.0 3.4 %collective-permute-start = (bf16[528,128]{1,0:T(8,128)(2,1)S(1)}, bf16[528,128]{1,0:T(8,128)(2,1)S(1)}, u32[]{:S(2)}, u32[]{:S(2)}) collective-permute-start(bf16[528,128]{1,0:T(8,128)(2,1)S(1)} %maximum_maximum_fusion.b0_ref), channel_id=1, source_target_pairs={{0,8},{4,12},{8,16},{12,20},{16,24},{20,28},{24,32},{28,36},{32,40... | collective-permute-start | bytes 405512 | tf_op jit(solution)/shard_map/ppermute | solution.py:52
  34.3 3.2 %collective-permute-start.1 = (bf16[528,128]{1,0:T(8,128)(2,1)S(1)}, bf16[528,128]{1,0:T(8,128)(2,1)S(1)}, u32[]{:S(2)}, u32[]{:S(2)}) collective-permute-start(bf16[528,128]{1,0:T(8,128)(2,1)S(1)} %maximum_maximum_fusion.b0_ref), channel_id=1, source_target_pairs={{0,4},{4,8},{8,12},{12,16},{16,20},{20,24},{24,28},{28,32},{32,36}... | collective-permute-start | bytes 405512 | tf_op jit(solution)/shard_map/ppermute | solution.py:52
  40.4 2.0 %collective-permute-start.3 = (bf16[32,24,256]{2,1,0:T(8,128)(2,1)S(1)}, bf16[32,24,256]{2,1,0:T(8,128)(2,1)S(1)}, u32[]{:S(2)}, u32[]{:S(2)}) collective-permute-start(bf16[32,24,256]{2,1,0:T(8,128)(2,1)S(1)} %get-tuple-element.18), channel_id=1, source_target_pairs={{0,4},{4,0},{8,12},{12,8},{16,20},{20,16},{24,28},{28,24},{32,36},... | collective-permute-start | bytes 1179656 | tf_op jit(solution)/shard_map/ppermute | solution.py:56
  42.5 6.7 %collective-permute-done.b2_ref = bf16[528,128]{1,0:T(8,128)(2,1)S(1)} collective-permute-done((bf16[528,128]{1,0:T(8,128)(2,1)S(1)}, bf16[528,128]{1,0:T(8,128)(2,1)S(1)}, u32[]{:S(2)}, u32[]{:S(2)}) %collective-permute-start) | collective-permute-done | bytes 135200 | tf_op jit(solution)/shard_map/ppermute | solution.py:52
  49.2 3.4 %collective-permute-done.1.b1_ref = bf16[528,128]{1,0:T(8,128)(2,1)S(1)} collective-permute-done((bf16[528,128]{1,0:T(8,128)(2,1)S(1)}, bf16[528,128]{1,0:T(8,128)(2,1)S(1)}, u32[]{:S(2)}, u32[]{:S(2)}) %collective-permute-start.1) | collective-permute-done | bytes 135200 | tf_op jit(solution)/shard_map/ppermute | solution.py:52
  53.6 4.6 %attend.1.own_ref.refs_6_ = bf16[256,1024]{1,0:T(8,128)(2,1)S(1)} custom-call(bf16[256,1024]{1,0:T(8,128)(2,1)S(1)} %copy-done.8, bf16[528,128]{1,0:T(8,128)(2,1)S(1)} %collective-permute-done.b2_ref, bf16[528,128]{1,0:T(8,128)(2,1)S(1)} %collective-permute-done.1.b1_ref, bf16[528,128]{1,0:T(8,128)(2,1)S(1)} %maximum_maximum_fusion.b0_ref), custom_call_target="tpu_custom_call" | custom-call | flops 805306368 | bytes 2097152 | tf_op jit(solution)/shard_map/attend/pallas_call | solution.py:101
  63.4 9.6 %all-to-all-start.2 = ((bf16[64,8,1152]{2,1,0:T(8,128)(2,1)}), bf16[64,8,1152]{2,1,0:T(8,128)(2,1)S(1)}, u32[]{:S(2)}, u32[]{:S(2)}) async-start(bf16[64,8,1152]{2,1,0:T(8,128)(2,1)} %fusion), calls=%async_computation.2 | async-start | bytes 2359296 | tf_op jit(solution)/shard_map/all_to_all | solution.py:44
  74.0 3.2 %shard_map.95 = bf16[4,8,24,512]{3,2,1,0:T(8,128)(2,1)S(1)} custom-call(s32[2]{0:T(128)S(1)} %pad_add_fusion.place_ref, bf16[256,1024]{1,0:T(8,128)(2,1)S(1)} %attend.1.own_ref.refs_6_, bf16[256,1024]{1,0:T(8,128)(2,1)S(1)} %copy-done.4, bf16[768,1024]{1,0:T(8,128)(2,1)S(1)} %bitcast.32), custom_call_target="tpu_custom_call" | custom-call | flops 805306368 | bytes 4194304 | tf_op jit(solution)/shard_map/pallas_call | solution.py:175
  77.3 4.4 %collective-permute-start.6 = (bf16[8,24,512]{2,1,0:T(8,128)(2,1)S(1)}, bf16[8,24,512]{2,1,0:T(8,128)(2,1)S(1)}, u32[]{:S(2)}, u32[]{:S(2)}) collective-permute-start(bf16[8,24,512]{2,1,0:T(8,128)(2,1)S(1)} %get-tuple-element.32), channel_id=1, source_target_pairs={{0,3},{1,0},{2,1},{3,2},{4,7},{5,4},{6,5},{7,6},{8,11},{9,8},{10,9... | collective-permute-start | bytes 589832 | tf_op jit(solution)/shard_map/ppermute | solution.py:257
  81.7 2.4 %collective-permute-start.5 = (bf16[8,24,512]{2,1,0:T(8,128)(2,1)S(1)}, bf16[8,24,512]{2,1,0:T(8,128)(2,1)S(1)}, u32[]{:S(2)}, u32[]{:S(2)}) collective-permute-start(bf16[8,24,512]{2,1,0:T(8,128)(2,1)S(1)} %get-tuple-element.33), channel_id=1, source_target_pairs={{0,2},{1,3},{2,0},{3,1},{4,6},{5,7},{6,4},{7,5},{8,10},{9,11},{10,... | collective-permute-start | bytes 589832 | tf_op jit(solution)/shard_map/ppermute | solution.py:257
  84.1 2.5 %collective-permute-start.4 = (bf16[8,24,512]{2,1,0:T(8,128)(2,1)S(1)}, bf16[8,24,512]{2,1,0:T(8,128)(2,1)S(1)}, u32[]{:S(2)}, u32[]{:S(2)}) collective-permute-start(bf16[8,24,512]{2,1,0:T(8,128)(2,1)S(1)} %get-tuple-element.31), channel_id=1, source_target_pairs={{0,1},{1,2},{2,3},{3,0},{4,5},{5,6},{6,7},{7,4},{8,9},{9,10},{10,1... | collective-permute-start | bytes 589832 | tf_op jit(solution)/shard_map/ppermute | solution.py:257
  86.7 3.1 %collective-permute-done.6 = bf16[8,24,512]{2,1,0:T(8,128)(2,1)S(1)} collective-permute-done((bf16[8,24,512]{2,1,0:T(8,128)(2,1)S(1)}, bf16[8,24,512]{2,1,0:T(8,128)(2,1)S(1)}, u32[]{:S(2)}, u32[]{:S(2)}) %collective-permute-start.6) | collective-permute-done | bytes 196640 | tf_op jit(solution)/shard_map/ppermute | solution.py:257
  91.0 5.1 %collective-permute-done.4 = bf16[8,24,512]{2,1,0:T(8,128)(2,1)S(1)} collective-permute-done((bf16[8,24,512]{2,1,0:T(8,128)(2,1)S(1)}, bf16[8,24,512]{2,1,0:T(8,128)(2,1)S(1)}, u32[]{:S(2)}, u32[]{:S(2)}) %collective-permute-start.4) | collective-permute-done | bytes 196640 | tf_op jit(solution)/shard_map/ppermute | solution.py:257
  96.2 7.7 %all-to-all-done.2.in_ref = bf16[64,8,1152]{2,1,0:T(8,128)(2,1)S(1)} async-done(((bf16[64,8,1152]{2,1,0:T(8,128)(2,1)}), bf16[64,8,1152]{2,1,0:T(8,128)(2,1)S(1)}, u32[]{:S(2)}, u32[]{:S(2)}) %all-to-all-start.2) | async-done | bytes 1179680 | tf_op jit(solution)/shard_map/all_to_all | solution.py:44
  104.7 4.2 %collective-permute-start.7 = (bf16[512,1024]{1,0:T(8,128)(2,1)S(1)}, bf16[512,1024]{1,0:T(8,128)(2,1)S(1)}, u32[]{:S(2)}, u32[]{:S(2)}) collective-permute-start(bf16[512,1024]{1,0:T(8,128)(2,1)S(1)} %place.1.own_ref.refs_8_), channel_id=1, source_target_pairs={{0,4},{4,0},{8,12},{12,8},{16,20},{20,16},{24,28},{28,24},{32,36},... | collective-permute-start | bytes 3145736 | tf_op jit(solution)/shard_map/ppermute | solution.py:56
  108.9 3.1 %collective-permute-start.12 = (bf16[8,24,512]{2,1,0:T(8,128)(2,1)S(1)}, bf16[8,24,512]{2,1,0:T(8,128)(2,1)S(1)}, u32[]{:S(2)}, u32[]{:S(2)}) collective-permute-start(bf16[8,24,512]{2,1,0:T(8,128)(2,1)S(1)} %fusion.10.refs_0_), channel_id=1, source_target_pairs={{0,1},{1,2},{2,3},{3,0},{4,5},{5,6},{6,7},{7,4},{8,9},{9,10},{10,1... | collective-permute-start | bytes 589832 | tf_op jit(solution)/shard_map/ppermute | solution.py:308
  112.0 4.4 %collective-permute-start.13 = (bf16[8,24,512]{2,1,0:T(8,128)(2,1)S(1)}, bf16[8,24,512]{2,1,0:T(8,128)(2,1)S(1)}, u32[]{:S(2)}, u32[]{:S(2)}) collective-permute-start(bf16[8,24,512]{2,1,0:T(8,128)(2,1)S(1)} %fusion.10.refs_0_), channel_id=1, source_target_pairs={{0,2},{1,3},{2,0},{3,1},{4,6},{5,7},{6,4},{7,5},{8,10},{9,11},{10,... | collective-permute-start | bytes 589832 | tf_op jit(solution)/shard_map/ppermute | solution.py:308
  116.4 3.2 %collective-permute-start.14 = (bf16[8,24,512]{2,1,0:T(8,128)(2,1)S(1)}, bf16[8,24,512]{2,1,0:T(8,128)(2,1)S(1)}, u32[]{:S(2)}, u32[]{:S(2)}) collective-permute-start(bf16[8,24,512]{2,1,0:T(8,128)(2,1)S(1)} %fusion.10.refs_0_), channel_id=1, source_target_pairs={{0,3},{1,0},{2,1},{3,2},{4,7},{5,4},{6,5},{7,6},{8,11},{9,8},{10,9... | collective-permute-start | bytes 589832 | tf_op jit(solution)/shard_map/ppermute | solution.py:308
  119.7 4.0 %collective-permute-done.13.refs_2_ = bf16[8,24,512]{2,1,0:T(8,128)(2,1)S(1)} collective-permute-done((bf16[8,24,512]{2,1,0:T(8,128)(2,1)S(1)}, bf16[8,24,512]{2,1,0:T(8,128)(2,1)S(1)}, u32[]{:S(2)}, u32[]{:S(2)}) %collective-permute-start.13) | collective-permute-done | bytes 196640 | tf_op jit(solution)/shard_map/ppermute | solution.py:308
  126.7 6.6 %term.1 = bf16[8,96,1024]{2,1,0:T(8,128)(2,1)} custom-call(s32[2]{0:T(128)} %copy-done.6, bf16[8,24,512]{2,1,0:T(8,128)(2,1)} %copy-done.11, bf16[8,24,512]{2,1,0:T(8,128)(2,1)} %copy-done.13, bf16[8,24,512]{2,1,0:T(8,128)(2,1)} %copy-done.14, bf16[8,24,512]{2,1,0:T(8,128)(2,1)} %copy-done.15, bf16[32,24,256]{2,1,0:T(8,128)(2,1)} %copy-done.5, ...), custom_call_target="tpu_custom_call" | custom-call | flops 1610612736 | bytes 8388608 | tf_op jit(solution)/shard_map/term/pallas_call | solution.py:238
  133.3 4.7 %all-to-all-start.3 = ((bf16[8,96,1024]{2,1,0:T(8,128)(2,1)}), bf16[8,96,1024]{2,1,0:T(8,128)(2,1)S(1)}, u32[]{:S(2)}, u32[]{:S(2)}) async-start(bf16[8,96,1024]{2,1,0:T(8,128)(2,1)} %term.1), calls=%async_computation.3 | async-start | bytes 3145728 | tf_op jit(solution)/shard_map/all_to_all | solution.py:44
  138.0 5.6 %shard_map.96 = bf16[4,8,24,512]{3,2,1,0:T(8,128)(2,1)} custom-call(s32[2]{0:T(128)} %copy-done.6, bf16[512,1024]{1,0:T(8,128)(2,1)} %copy-done.1, bf16[512,1024]{1,0:T(8,128)(2,1)} %copy-done.10, bf16[768,1024]{1,0:T(8,128)(2,1)} %bitcast.33), custom_call_target="tpu_custom_call" | custom-call | flops 805306368 | bytes 4194304 | tf_op jit(solution)/shard_map/pallas_call | solution.py:175
  144.7 4.3 %collective-permute-start.10 = (bf16[8,24,512]{2,1,0:T(8,128)(2,1)S(1)}, bf16[8,24,512]{2,1,0:T(8,128)(2,1)S(1)}, u32[]{:S(2)}, u32[]{:S(2)}) collective-permute-start(bf16[8,24,512]{2,1,0:T(8,128)(2,1)S(1)} %get-tuple-element.29), channel_id=1, source_target_pairs={{0,3},{1,0},{2,1},{3,2},{4,7},{5,4},{6,5},{7,6},{8,11},{9,8},{10,9... | collective-permute-start | bytes 589832 | tf_op jit(solution)/shard_map/ppermute | solution.py:257
  149.1 3.9 %collective-permute-start.9 = (bf16[8,24,512]{2,1,0:T(8,128)(2,1)S(1)}, bf16[8,24,512]{2,1,0:T(8,128)(2,1)S(1)}, u32[]{:S(2)}, u32[]{:S(2)}) collective-permute-start(bf16[8,24,512]{2,1,0:T(8,128)(2,1)S(1)} %get-tuple-element.30), channel_id=1, source_target_pairs={{0,2},{1,3},{2,0},{3,1},{4,6},{5,7},{6,4},{7,5},{8,10},{9,11},{10,... | collective-permute-start | bytes 589832 | tf_op jit(solution)/shard_map/ppermute | solution.py:257
  154.9 3.4 %collective-permute-done.9 = bf16[8,24,512]{2,1,0:T(8,128)(2,1)S(1)} collective-permute-done((bf16[8,24,512]{2,1,0:T(8,128)(2,1)S(1)}, bf16[8,24,512]{2,1,0:T(8,128)(2,1)S(1)}, u32[]{:S(2)}, u32[]{:S(2)}) %collective-permute-start.9) | collective-permute-done | bytes 196640 | tf_op jit(solution)/shard_map/ppermute | solution.py:257
  158.3 5.1 %collective-permute-done.8 = bf16[8,24,512]{2,1,0:T(8,128)(2,1)S(1)} collective-permute-done((bf16[8,24,512]{2,1,0:T(8,128)(2,1)S(1)}, bf16[8,24,512]{2,1,0:T(8,128)(2,1)S(1)}, u32[]{:S(2)}, u32[]{:S(2)}) %collective-permute-start.8) | collective-permute-done | bytes 196640 | tf_op jit(solution)/shard_map/ppermute | solution.py:257
  164.5 2.8 %collective-permute-start.11 = (bf16[192,256]{1,0:T(8,128)(2,1)S(1)}, bf16[192,256]{1,0:T(8,128)(2,1)S(1)}, u32[]{:S(2)}, u32[]{:S(2)}) collective-permute-start(bf16[192,256]{1,0:T(8,128)(2,1)S(1)} %broadcast_select_fusion), channel_id=1, source_target_pairs={{0,4},{4,0},{8,12},{12,8},{16,20},{20,16},{24,28},{28,24},{32,36},... | collective-permute-start | bytes 294920 | tf_op jit(solution)/shard_map/ppermute | solution.py:56
  168.3 4.9 %all-to-all-start.4 = ((bf16[8,12,1024]{2,1,0:T(8,128)(2,1)}), bf16[8,12,1024]{2,1,0:T(8,128)(2,1)S(1)}, u32[]{:S(2)}, u32[]{:S(2)}) async-start(bf16[8,12,1024]{2,1,0:T(8,128)(2,1)} %reshape.96), calls=%async_computation.4 | async-start | bytes 524288 | tf_op jit(solution)/shard_map/all_to_all | solution.py:44
  174.4 8.1 %all-to-all-done.4 = bf16[8,12,1024]{2,1,0:T(8,128)(2,1)S(1)} async-done(((bf16[8,12,1024]{2,1,0:T(8,128)(2,1)}), bf16[8,12,1024]{2,1,0:T(8,128)(2,1)S(1)}, u32[]{:S(2)}, u32[]{:S(2)}) %all-to-all-start.4) | async-done | bytes 196640 | tf_op jit(solution)/shard_map/all_to_all | solution.py:44
  (80 shorter events, 25.6 us)
Async XLA Ops:
  2.1 20.2 %all-to-all-start = ((bf16[8,12,1024]{2,1,0:T(8,128)(2,1)}), bf16[8,12,1024]{2,1,0:T(8,128)(2,1)S(1)}, u32[]{:S(2)}, u32[]{:S(2)}) async-start(bf16[8,12,1024]{2,1,0:T(8,128)(2,1)} %broadcast_in_dim.8), calls=%async_computation | async-start | bytes 524288 | tf_op jit(solution)/shard_map/all_to_all | solution.py:44
  13.0 59.9 %copy-start.6 = (s32[2]{0:T(128)}, s32[2]{0:T(128)S(1)}, u32[]{:S(2)}) copy-start(s32[2]{0:T(128)S(1)} %pad_add_fusion.place_ref) | copy-start | bytes 28
  23.8 7.0 %copy-start.19 = (s32[256]{0:T(256)S(1)}, s32[256]{0:T(256)}, u32[]{:S(2)}) copy-start(s32[256]{0:T(256)} %param.11) | copy-start | bytes 3076
  23.8 7.0 %copy-start.16 = (bf16[256,128]{1,0:T(8,128)(2,1)S(1)}, bf16[256,128]{1,0:T(8,128)(2,1)}, u32[]{:S(2)}) copy-start(bf16[256,128]{1,0:T(8,128)(2,1)} %param.10) | copy-start | bytes 196612
  23.8 7.0 %copy-start.17 = (bf16[256,128]{1,0:T(8,128)(2,1)S(1)}, bf16[256,128]{1,0:T(8,128)(2,1)}, u32[]{:S(2)}) copy-start(bf16[256,128]{1,0:T(8,128)(2,1)} %param.9) | copy-start | bytes 196612
  23.8 13.9 %copy-start.7 = (bf16[256,1536]{1,0:T(8,128)(2,1)S(1)}, bf16[256,1536]{1,0:T(8,128)(2,1)}, u32[]{:S(2)}) copy-start(bf16[256,1536]{1,0:T(8,128)(2,1)} %states_ref.1) | copy-start | bytes 2359300
  23.8 13.9 %copy-start.9 = (s32[256]{0:T(256)S(1)}, s32[256]{0:T(256)}, u32[]{:S(2)}) copy-start(s32[256]{0:T(256)} %param.15) | copy-start | bytes 3076
  23.8 39.6 %all-to-all-start.1 = ((bf16[8,96,1024]{2,1,0:T(8,128)(2,1)}), bf16[8,96,1024]{2,1,0:T(8,128)(2,1)S(1)}, u32[]{:S(2)}, u32[]{:S(2)}) async-start(bf16[8,96,1024]{2,1,0:T(8,128)(2,1)} %broadcast_in_dim.11), calls=%async_computation.1 | async-start | bytes 3145728 | tf_op jit(solution)/shard_map/all_to_all | solution.py:44
  31.0 18.3 %collective-permute-start = (bf16[528,128]{1,0:T(8,128)(2,1)S(1)}, bf16[528,128]{1,0:T(8,128)(2,1)S(1)}, u32[]{:S(2)}, u32[]{:S(2)}) collective-permute-start(bf16[528,128]{1,0:T(8,128)(2,1)S(1)} %maximum_maximum_fusion.b0_ref), channel_id=1, source_target_pairs={{0,8},{4,12},{8,16},{12,20},{16,24},{20,28},{24,32},{28,36},{32,40... | collective-permute-start | bytes 405512 | tf_op jit(solution)/shard_map/ppermute | solution.py:52
  34.3 18.3 %collective-permute-start.1 = (bf16[528,128]{1,0:T(8,128)(2,1)S(1)}, bf16[528,128]{1,0:T(8,128)(2,1)S(1)}, u32[]{:S(2)}, u32[]{:S(2)}) collective-permute-start(bf16[528,128]{1,0:T(8,128)(2,1)S(1)} %maximum_maximum_fusion.b0_ref), channel_id=1, source_target_pairs={{0,4},{4,8},{8,12},{12,16},{16,20},{20,24},{24,28},{28,32},{32,36}... | collective-permute-start | bytes 405512 | tf_op jit(solution)/shard_map/ppermute | solution.py:52
  40.4 19.7 %copy-start.18 = (s32[256]{0:T(256)S(1)}, s32[256]{0:T(256)}, u32[]{:S(2)}) copy-start(s32[256]{0:T(256)} %param.12) | copy-start | bytes 3076
  40.4 21.4 %collective-permute-start.3 = (bf16[32,24,256]{2,1,0:T(8,128)(2,1)S(1)}, bf16[32,24,256]{2,1,0:T(8,128)(2,1)S(1)}, u32[]{:S(2)}, u32[]{:S(2)}) collective-permute-start(bf16[32,24,256]{2,1,0:T(8,128)(2,1)S(1)} %get-tuple-element.18), channel_id=1, source_target_pairs={{0,4},{4,0},{8,12},{12,8},{16,20},{20,16},{24,28},{28,24},{32,36},... | collective-permute-start | bytes 1179656 | tf_op jit(solution)/shard_map/ppermute | solution.py:56
  58.2 14.8 %copy-start.2 = (bf16[256,1024]{1,0:T(8,128)(2,1)}, bf16[256,1024]{1,0:T(8,128)(2,1)S(1)}, u32[]{:S(2)}) copy-start(bf16[256,1024]{1,0:T(8,128)(2,1)S(1)} %attend.1.own_ref.refs_6_) | copy-start | bytes 1572868
  58.2 4.4 %collective-permute-start.2 = (bf16[256,1024]{1,0:T(8,128)(2,1)S(1)}, bf16[256,1024]{1,0:T(8,128)(2,1)S(1)}, u32[]{:S(2)}, u32[]{:S(2)}) collective-permute-start(bf16[256,1024]{1,0:T(8,128)(2,1)S(1)} %attend.1.own_ref.refs_6_), channel_id=1, source_target_pairs={{0,4},{4,0},{8,12},{12,8},{16,20},{20,16},{24,28},{28,24},{32,36},... | collective-permute-start | bytes 1572872 | tf_op jit(solution)/shard_map/ppermute | solution.py:56
  63.4 9.6 %copy-start = (bf16[8,96,1024]{2,1,0:T(8,128)(2,1)}, bf16[8,96,1024]{2,1,0:T(8,128)(2,1)S(1)}, u32[]{:S(2)}) copy-start(bf16[8,96,1024]{2,1,0:T(8,128)(2,1)S(1)} %all-to-all-done.1) | copy-start | bytes 4718596
  63.4 40.5 %all-to-all-start.2 = ((bf16[64,8,1152]{2,1,0:T(8,128)(2,1)}), bf16[64,8,1152]{2,1,0:T(8,128)(2,1)S(1)}, u32[]{:S(2)}, u32[]{:S(2)}) async-start(bf16[64,8,1152]{2,1,0:T(8,128)(2,1)} %fusion), calls=%async_computation.2 | async-start | bytes 2359296 | tf_op jit(solution)/shard_map/all_to_all | solution.py:44
  77.3 12.4 %collective-permute-start.6 = (bf16[8,24,512]{2,1,0:T(8,128)(2,1)S(1)}, bf16[8,24,512]{2,1,0:T(8,128)(2,1)S(1)}, u32[]{:S(2)}, u32[]{:S(2)}) collective-permute-start(bf16[8,24,512]{2,1,0:T(8,128)(2,1)S(1)} %get-tuple-element.32), channel_id=1, source_target_pairs={{0,3},{1,0},{2,1},{3,2},{4,7},{5,4},{6,5},{7,6},{8,11},{9,8},{10,9... | collective-permute-start | bytes 589832 | tf_op jit(solution)/shard_map/ppermute | solution.py:257
  81.7 9.3 %collective-permute-start.5 = (bf16[8,24,512]{2,1,0:T(8,128)(2,1)S(1)}, bf16[8,24,512]{2,1,0:T(8,128)(2,1)S(1)}, u32[]{:S(2)}, u32[]{:S(2)}) collective-permute-start(bf16[8,24,512]{2,1,0:T(8,128)(2,1)S(1)} %get-tuple-element.33), channel_id=1, source_target_pairs={{0,2},{1,3},{2,0},{3,1},{4,6},{5,7},{6,4},{7,5},{8,10},{9,11},{10,... | collective-permute-start | bytes 589832 | tf_op jit(solution)/shard_map/ppermute | solution.py:257
  84.1 12.0 %collective-permute-start.4 = (bf16[8,24,512]{2,1,0:T(8,128)(2,1)S(1)}, bf16[8,24,512]{2,1,0:T(8,128)(2,1)S(1)}, u32[]{:S(2)}, u32[]{:S(2)}) collective-permute-start(bf16[8,24,512]{2,1,0:T(8,128)(2,1)S(1)} %get-tuple-element.31), channel_id=1, source_target_pairs={{0,1},{1,2},{2,3},{3,0},{4,5},{5,6},{6,7},{7,4},{8,9},{9,10},{10,1... | collective-permute-start | bytes 589832 | tf_op jit(solution)/shard_map/ppermute | solution.py:257
  96.2 28.8 %copy-start.11 = (bf16[8,24,512]{2,1,0:T(8,128)(2,1)}, bf16[8,24,512]{2,1,0:T(8,128)(2,1)S(1)}, u32[]{:S(2)}) copy-start(bf16[8,24,512]{2,1,0:T(8,128)(2,1)S(1)} %fusion.10.refs_0_) | copy-start | bytes 589828
  104.7 20.3 %copy-start.1 = (bf16[512,1024]{1,0:T(8,128)(2,1)}, bf16[512,1024]{1,0:T(8,128)(2,1)S(1)}, u32[]{:S(2)}) copy-start(bf16[512,1024]{1,0:T(8,128)(2,1)S(1)} %place.1.own_ref.refs_8_) | copy-start | bytes 3145732
  104.7 20.3 %collective-permute-start.7 = (bf16[512,1024]{1,0:T(8,128)(2,1)S(1)}, bf16[512,1024]{1,0:T(8,128)(2,1)S(1)}, u32[]{:S(2)}, u32[]{:S(2)}) collective-permute-start(bf16[512,1024]{1,0:T(8,128)(2,1)S(1)} %place.1.own_ref.refs_8_), channel_id=1, source_target_pairs={{0,4},{4,0},{8,12},{12,8},{16,20},{20,16},{24,28},{28,24},{32,36},... | collective-permute-start | bytes 3145736 | tf_op jit(solution)/shard_map/ppermute | solution.py:56
  108.9 10.7 %collective-permute-start.12 = (bf16[8,24,512]{2,1,0:T(8,128)(2,1)S(1)}, bf16[8,24,512]{2,1,0:T(8,128)(2,1)S(1)}, u32[]{:S(2)}, u32[]{:S(2)}) collective-permute-start(bf16[8,24,512]{2,1,0:T(8,128)(2,1)S(1)} %fusion.10.refs_0_), channel_id=1, source_target_pairs={{0,1},{1,2},{2,3},{3,0},{4,5},{5,6},{6,7},{7,4},{8,9},{9,10},{10,1... | collective-permute-start | bytes 589832 | tf_op jit(solution)/shard_map/ppermute | solution.py:308
  112.0 11.6 %collective-permute-start.13 = (bf16[8,24,512]{2,1,0:T(8,128)(2,1)S(1)}, bf16[8,24,512]{2,1,0:T(8,128)(2,1)S(1)}, u32[]{:S(2)}, u32[]{:S(2)}) collective-permute-start(bf16[8,24,512]{2,1,0:T(8,128)(2,1)S(1)} %fusion.10.refs_0_), channel_id=1, source_target_pairs={{0,2},{1,3},{2,0},{3,1},{4,6},{5,7},{6,4},{7,5},{8,10},{9,11},{10,... | collective-permute-start | bytes 589832 | tf_op jit(solution)/shard_map/ppermute | solution.py:308
  116.4 8.6 %collective-permute-start.14 = (bf16[8,24,512]{2,1,0:T(8,128)(2,1)S(1)}, bf16[8,24,512]{2,1,0:T(8,128)(2,1)S(1)}, u32[]{:S(2)}, u32[]{:S(2)}) collective-permute-start(bf16[8,24,512]{2,1,0:T(8,128)(2,1)S(1)} %fusion.10.refs_0_), channel_id=1, source_target_pairs={{0,3},{1,0},{2,1},{3,2},{4,7},{5,4},{6,5},{7,6},{8,11},{9,8},{10,9... | collective-permute-start | bytes 589832 | tf_op jit(solution)/shard_map/ppermute | solution.py:308
  119.7 5.4 %copy-start.13 = (bf16[8,24,512]{2,1,0:T(8,128)(2,1)}, bf16[8,24,512]{2,1,0:T(8,128)(2,1)S(1)}, u32[]{:S(2)}) copy-start(bf16[8,24,512]{2,1,0:T(8,128)(2,1)S(1)} %collective-permute-done.12.refs_1_) | copy-start | bytes 589828
  133.3 33.9 %all-to-all-start.3 = ((bf16[8,96,1024]{2,1,0:T(8,128)(2,1)}), bf16[8,96,1024]{2,1,0:T(8,128)(2,1)S(1)}, u32[]{:S(2)}, u32[]{:S(2)}) async-start(bf16[8,96,1024]{2,1,0:T(8,128)(2,1)} %term.1), calls=%async_computation.3 | async-start | bytes 3145728 | tf_op jit(solution)/shard_map/all_to_all | solution.py:44
  144.7 10.2 %collective-permute-start.10 = (bf16[8,24,512]{2,1,0:T(8,128)(2,1)S(1)}, bf16[8,24,512]{2,1,0:T(8,128)(2,1)S(1)}, u32[]{:S(2)}, u32[]{:S(2)}) collective-permute-start(bf16[8,24,512]{2,1,0:T(8,128)(2,1)S(1)} %get-tuple-element.29), channel_id=1, source_target_pairs={{0,3},{1,0},{2,1},{3,2},{4,7},{5,4},{6,5},{7,6},{8,11},{9,8},{10,9... | collective-permute-start | bytes 589832 | tf_op jit(solution)/shard_map/ppermute | solution.py:257
  149.1 9.2 %collective-permute-start.9 = (bf16[8,24,512]{2,1,0:T(8,128)(2,1)S(1)}, bf16[8,24,512]{2,1,0:T(8,128)(2,1)S(1)}, u32[]{:S(2)}, u32[]{:S(2)}) collective-permute-start(bf16[8,24,512]{2,1,0:T(8,128)(2,1)S(1)} %get-tuple-element.30), channel_id=1, source_target_pairs={{0,2},{1,3},{2,0},{3,1},{4,6},{5,7},{6,4},{7,5},{8,10},{9,11},{10,... | collective-permute-start | bytes 589832 | tf_op jit(solution)/shard_map/ppermute | solution.py:257
  153.0 10.4 %collective-permute-start.8 = (bf16[8,24,512]{2,1,0:T(8,128)(2,1)S(1)}, bf16[8,24,512]{2,1,0:T(8,128)(2,1)S(1)}, u32[]{:S(2)}, u32[]{:S(2)}) collective-permute-start(bf16[8,24,512]{2,1,0:T(8,128)(2,1)S(1)} %get-tuple-element.28), channel_id=1, source_target_pairs={{0,1},{1,2},{2,3},{3,0},{4,5},{5,6},{6,7},{7,4},{8,9},{9,10},{10,1... | collective-permute-start | bytes 589832 | tf_op jit(solution)/shard_map/ppermute | solution.py:257
  164.5 9.0 %collective-permute-start.11 = (bf16[192,256]{1,0:T(8,128)(2,1)S(1)}, bf16[192,256]{1,0:T(8,128)(2,1)S(1)}, u32[]{:S(2)}, u32[]{:S(2)}) collective-permute-start(bf16[192,256]{1,0:T(8,128)(2,1)S(1)} %broadcast_select_fusion), channel_id=1, source_target_pairs={{0,4},{4,0},{8,12},{12,8},{16,20},{20,16},{24,28},{28,24},{32,36},... | collective-permute-start | bytes 294920 | tf_op jit(solution)/shard_map/ppermute | solution.py:56
  168.3 14.2 %all-to-all-start.4 = ((bf16[8,12,1024]{2,1,0:T(8,128)(2,1)}), bf16[8,12,1024]{2,1,0:T(8,128)(2,1)S(1)}, u32[]{:S(2)}, u32[]{:S(2)}) async-start(bf16[8,12,1024]{2,1,0:T(8,128)(2,1)} %reshape.96), calls=%async_computation.4 | async-start | bytes 524288 | tf_op jit(solution)/shard_map/all_to_all | solution.py:44
  (8 other events, 7.5 us)
